TPU v7x, 32 devices: a whole 2x2x4 slice. The times are simulated.
32 devices in a mesh: seg: 8 (over y, x, core), dev: 4 (over z).
Axes of the slice: x: 2, y: 2, z: 4, core: 2. Of those that a mesh axis runs over, the one named last changes fastest.
Arguments:
- queries: bfloat16 [4096, 1536], P(('seg', 'dev')), may hold values from -12 to 12
- keys: bfloat16 [4096, 1536], P(('seg', 'dev')), may hold values from -12 to 12
- values: bfloat16 [4096, 1536], P(('seg', 'dev')), may hold values from -4 to 4
Outputs:
- grad_queries: bfloat16 [4096, 1536], P(('seg', 'dev'))
- grad_keys: bfloat16 [4096, 1536], P(('seg', 'dev'))
- grad_values: bfloat16 [4096, 1536], P(('seg', 'dev'))
All inputs are finite; a program needn't handle non-finite values.
Results may differ from a plain program's by a relative error of at most 0.015.
Values may be sent and summed in bfloat16 or wider, within the bound.
No kernel may reach another device: no remote copies, remote signals or barrier semaphores. Data moves between devices by JAX's collectives and lax.ppermute only.
A program may use at most 128 MiB of HBM per device.

v0:
```python
import functools
import math

import jax
import jax.numpy as jnp
from jax import lax
from jax.experimental import pallas as pl
from jax.experimental.pallas import tpu as pltpu
from jax.sharding import PartitionSpec as P


HEADS = 16
WINDOW = 256
CHUNKS = 2
NEGATIVE = -1e30
LOG2E = math.log2(math.e)
BF16 = jnp.bfloat16
F32 = jnp.float32


SMEM_SPEC = pl.BlockSpec(memory_space=pltpu.SMEM)
VMEM_SPEC = pl.BlockSpec(memory_space=pltpu.VMEM)
HBM_SPEC = pl.BlockSpec(memory_space=pltpu.HBM)


def call(kernel, place, arrays, outs, scratch=(), flops=0, spec=VMEM_SPEC):
    moved = sum(a.size * a.dtype.itemsize for a in arrays)
    moved += sum(math.prod(o.shape) * o.dtype.itemsize for o in outs)
    return pl.pallas_call(
        kernel,
        out_shape=tuple(outs),
        in_specs=[SMEM_SPEC] + [spec] * len(arrays),
        out_specs=tuple([VMEM_SPEC] * len(outs)),
        scratch_shapes=list(scratch),
        cost_estimate=pl.CostEstimate(flops=flops, bytes_accessed=moved, transcendentals=0),
        compiler_params=pltpu.CompilerParams(vmem_limit_bytes=48 * 1024 * 1024),
    )(place, *arrays)


def shape(dims, dtype=BF16):
    return jax.ShapeDtypeStruct(dims, dtype)


class Plan:
    def __init__(self, rows, width, devs):
        self.rows, self.width, self.devs = rows, width, devs
        self.dim = width // HEADS
        self.local_heads = HEADS // devs
        self.local_width = width // devs
        self.chunks = CHUNKS if self.local_heads % CHUNKS == 0 else 1
        self.heads = self.local_heads // self.chunks
        self.chunk_width = self.heads * self.dim
        self.fold = 128 // math.gcd(self.chunk_width, 128)
        self.fold_rows = rows // self.fold
        self.piece = (self.fold_rows, self.fold * self.chunk_width)
        self.reach = WINDOW // rows
        self.seg_rows = rows * devs
        self.scale = self.dim ** (-0.5)


def folded(x, plan):
    parts = [x[i * plan.fold_rows : (i + 1) * plan.fold_rows] for i in range(plan.fold)]
    return parts[0] if plan.fold == 1 else jnp.concatenate(parts, axis=1)


def pack_kernel(plan, chunk, place, *refs):
    me = place[1]
    in_refs, out_refs = refs[:3], refs[3 : 3 + plan.devs]
    held, sems = refs[3 + plan.devs :]
    copies = [pltpu.make_async_copy(r, held.at[i], sems.at[i]) for i, r in enumerate(in_refs)]
    for copy in copies:
        copy.start()
    for at, copy in enumerate(copies):
        copy.wait()
        for step, out_ref in enumerate(out_refs):
            start = pl.multiple_of((me ^ step) * plan.local_width, 128)
            x = held[at, :, pl.ds(start, plan.local_width)]
            x = x[:, chunk * plan.chunk_width : (chunk + 1) * plan.chunk_width]
            out_ref[at] = folded(x, plan)


def pack(plan, chunk, place, arrays):
    if plan.local_width % 128 == 0:
        outs = [shape((3,) + plan.piece) for _ in range(plan.devs)]
        scratch = [
            pltpu.VMEM((3, plan.rows, plan.width), BF16),
            pltpu.SemaphoreType.DMA((3,)),
        ]
        kernel = functools.partial(pack_kernel, plan, chunk)
        return call(kernel, place, arrays, outs, scratch, spec=HBM_SPEC)
    pieces = []
    for step in range(plan.devs):
        start = (place[1] ^ step) * plan.local_width + chunk * plan.chunk_width
        taken = [lax.dynamic_slice_in_dim(a, start, plan.chunk_width, 1) for a in arrays]
        pieces.append(jnp.stack([folded(x, plan) for x in taken]))
    return pieces


def unpack_kernel(plan, place, *refs):
    me = place[1]
    piece_refs, out_refs = refs[:-3], refs[-3:]
    for step in range(plan.devs):
        start = pl.multiple_of((me ^ step) * plan.local_width, 128)
        for at, out_ref in enumerate(out_refs):
            rows = []
            for part in range(plan.fold):
                lanes = slice(part * plan.chunk_width, (part + 1) * plan.chunk_width)
                held = [
                    piece_refs[c * plan.devs + step][at, :, lanes] for c in range(plan.chunks)
                ]
                rows.append(held[0] if plan.chunks == 1 else jnp.concatenate(held, axis=1))
            out_ref[:, pl.ds(start, plan.local_width)] = (
                rows[0] if plan.fold == 1 else jnp.concatenate(rows, axis=0)
            )


def unpack(plan, place, pieces):
    if plan.local_width % 128 == 0:
        flat = [piece for chunk in pieces for piece in chunk]
        outs = [shape((plan.rows, plan.width)) for _ in range(3)]
        return call(functools.partial(unpack_kernel, plan), place, flat, outs)
    order = jnp.arange(plan.devs, dtype=jnp.int32) ^ place[1]
    chunks = []
    for chunk in pieces:
        x = jnp.take(jnp.stack(chunk), order, axis=0)
        x = x.reshape(plan.devs, 3, plan.fold_rows, plan.fold, plan.chunk_width)
        x = x.transpose(1, 3, 2, 0, 4)
        chunks.append(x.reshape(3, plan.rows, plan.devs, plan.chunk_width))
    out = jnp.concatenate(chunks, axis=3).reshape(3, plan.rows, plan.width)
    return out[0], out[1], out[2]


def exchange(plan, pieces):
    got = [pieces[0]] + [None] * (plan.devs - 1)
    for step in range(plan.devs - 1, 0, -1):
        pairs = [(i, i ^ step) for i in range(plan.devs)]
        got[step] = lax.ppermute(pieces[step], "dev", pairs)
    return got


def dot(a, b, over):
    return lax.dot_general(a, b, ((over[:1], over[1:]), ((), ())), preferred_element_type=F32)


def head_part(ref, index, head, part, plan):
    start = part * plan.chunk_width + head * plan.dim
    return ref[index + (slice(None), slice(start, start + plan.dim))]


def teacher_kernel(plan, place, *refs):
    me = place[1]
    piece_refs, (held_ref, target_ref) = refs[: plan.devs], refs[plan.devs :]
    for step, ref in enumerate(piece_refs):
        first = (me ^ step) * plan.rows
        for at in range(3):
            for head in range(plan.heads):
                for part in range(plan.fold):
                    start = pl.multiple_of(first + part * plan.fold_rows, plan.fold_rows)
                    held_ref[at, head, pl.ds(start, plan.fold_rows), :] = head_part(
                        ref, (at,), head, part, plan
                    )

    def body(i, _):
        head, block = i // plan.devs, i % plan.devs
        rows = pl.ds(pl.multiple_of(block * plan.rows, plan.rows), plan.rows)
        scores = dot(held_ref[0, head, rows, :], held_ref[1, head], (1, 1))
        top = scores.max(-1, keepdims=True)
        e = jnp.exp2((scores - top) * (plan.scale * LOG2E))
        total = e.sum(-1, keepdims=True)
        out = dot(e.astype(BF16), held_ref[2, head], (1, 0))
        target_ref[head, rows, :] = (out / total).astype(BF16)
        return 0

    lax.fori_loop(0, plan.heads * plan.devs, body, 0, unroll=4)


def teacher(plan, place, pieces):
    outs = [
        shape((3, plan.heads, plan.seg_rows, plan.dim)),
        shape((plan.heads, plan.seg_rows, plan.dim)),
    ]
    flops = 4 * plan.heads * plan.seg_rows * plan.seg_rows * plan.dim
    return call(functools.partial(teacher_kernel, plan), place, list(pieces), outs, flops=flops)


def student_block(plan, q, k, v, target, open_far):
    rows, reach = plan.rows, plan.reach
    scores = dot(q, k, (1, 1))
    query_at = lax.broadcasted_iota(jnp.int32, scores.shape, 0)
    key_at = lax.broadcasted_iota(jnp.int32, scores.shape, 1)
    allowed = (key_at >= query_at) & (key_at - reach * rows <= query_at)
    if open_far is not None:
        allowed &= key_at >= open_far
    scores = jnp.where(allowed, scores, NEGATIVE)
    top = scores.max(-1, keepdims=True)
    e = jnp.exp2((scores - top) * (plan.scale * LOG2E))
    probability = e * (1.0 / e.sum(-1, keepdims=True))
    weights = probability.astype(BF16)
    out = dot(weights, v, (1, 0))
    d_out = (128.0 * (out - target.astype(F32))).astype(BF16)
    d_prob = dot(d_out, v, (1, 1))
    inner = (probability * d_prob).sum(-1, keepdims=True)
    d_scores = (probability * (d_prob - inner) * plan.scale).astype(BF16)
    grad_q = dot(d_scores, k, (1, 0))
    grad_k = dot(d_scores, q, (0, 0))
    grad_v = dot(weights, d_out, (0, 0))
    return grad_q, grad_k, grad_v


def first_kernel(plan, place, held_ref, target_ref, halo_ref, gq_ref, gkv_ref, far_ref, ext, acc):
    seg = place[0]
    near = plan.reach * plan.rows
    for at in range(2):
        for head in range(plan.heads):
            for block in range(plan.reach):
                for part in range(plan.fold):
                    start = block * plan.rows + part * plan.fold_rows
                    ext[at, head, start : start + plan.fold_rows, :] = head_part(
                        halo_ref, (block, at), head, part, plan
                    )
            ext[at, head, near:, :] = held_ref[1 + at, head, :near, :]
    acc[...] = jnp.zeros_like(acc)

    def body(i, _):
        head, block = i // plan.reach, i % plan.reach
        start = pl.multiple_of(block * plan.rows, plan.rows)
        rows, keys = pl.ds(start, plan.rows), pl.ds(start, near + plan.rows)
        open_far = jnp.where(seg == 0, near - start, 0)
        gq, gk, gv = student_block(
            plan,
            held_ref[0, head, rows, :],
            ext[0, head, keys, :],
            ext[1, head, keys, :],
            target_ref[head, rows, :],
            open_far,
        )
        gq_ref[head, rows, :] = gq.astype(BF16)
        acc[0, head, keys, :] += gk
        acc[1, head, keys, :] += gv
        return 0

    lax.fori_loop(0, plan.heads * plan.reach, body, 0, unroll=2)
    gkv_ref[...] = acc[:, :, near:, :]
    for at in range(2):
        for block in range(plan.reach):
            for part in range(plan.fold):
                start = block * plan.rows + part * plan.fold_rows
                for head in range(plan.heads):
                    lane = part * plan.chunk_width + head * plan.dim
                    far_ref[block, at, :, lane : lane + plan.dim] = acc[
                        at, head, start : start + plan.fold_rows, :
                    ].astype(BF16)


def first_blocks(plan, place, held, target, halo):
    near = plan.reach * plan.rows
    outs = [
        shape((plan.heads, near, plan.dim)),
        shape((2, plan.heads, near, plan.dim), F32),
        shape((plan.reach, 2) + plan.piece),
    ]
    scratch = [
        pltpu.VMEM((2, plan.heads, 2 * near, plan.dim), BF16),
        pltpu.VMEM((2, plan.heads, 2 * near, plan.dim), F32),
    ]
    flops = 12 * plan.heads * near * (near + plan.rows) * plan.dim
    return call(
        functools.partial(first_kernel, plan), place, [held, target, halo], outs, scratch, flops
    )


def rest_kernel(plan, place, held_ref, target_ref, start_ref, gq_ref, acc):
    near = plan.reach * plan.rows
    acc[:, :, :near, :] = start_ref[...]
    acc[:, :, near:, :] = jnp.zeros((2, plan.heads, plan.seg_rows - near, plan.dim), F32)
    count = plan.devs - plan.reach

    def body(i, _):
        head, block = i // count, i % count
        start = pl.multiple_of(block * plan.rows, plan.rows)
        rows = pl.ds(pl.multiple_of(start + near, plan.rows), plan.rows)
        keys = pl.ds(start, near + plan.rows)
        gq, gk, gv = student_block(
            plan,
            held_ref[0, head, rows, :],
            held_ref[1, head, keys, :],
            held_ref[2, head, keys, :],
            target_ref[head, rows, :],
            None,
        )
        gq_ref[head, pl.ds(start, plan.rows), :] = gq.astype(BF16)
        acc[0, head, keys, :] += gk
        acc[1, head, keys, :] += gv
        return 0

    lax.fori_loop(0, plan.heads * count, body, 0, unroll=2)


def rest_blocks(plan, place, held, target, start):
    near = plan.reach * plan.rows
    outs = [
        shape((plan.heads, plan.seg_rows - near, plan.dim)),
        shape((2, plan.heads, plan.seg_rows, plan.dim), F32),
    ]
    flops = 12 * plan.heads * (plan.seg_rows - near) * (near + plan.rows) * plan.dim
    return call(
        functools.partial(rest_kernel, plan), place, [held, target, start], outs, (), flops
    )


def finish_kernel(plan, place, gq_first, gq_rest, gkv, far, *refs):
    me = place[1]
    out_refs, (grads,) = refs[: plan.devs], refs[plan.devs :]
    near = plan.reach * plan.rows
    last = plan.seg_rows - near
    for head in range(plan.heads):
        grads[0, head, :near, :] = gq_first[head]
        grads[0, head, near:, :] = gq_rest[head]
        for at in range(2):
            grads[1 + at, head, :last, :] = gkv[at, head, :last, :].astype(BF16)
            for block in range(plan.reach):
                for part in range(plan.fold):
                    start = last + block * plan.rows + part * plan.fold_rows
                    span = slice(start, start + plan.fold_rows)
                    back = head_part(far, (block, at), head, part, plan).astype(F32)
                    grads[1 + at, head, span, :] = (gkv[at, head, span, :] + back).astype(BF16)
    for step, out_ref in enumerate(out_refs):
        first = (me ^ step) * plan.rows
        for at in range(3):
            for part in range(plan.fold):
                start = pl.multiple_of(first + part * plan.fold_rows, plan.fold_rows)
                held = [
                    grads[at, head, pl.ds(start, plan.fold_rows), :] for head in range(plan.heads)
                ]
                lane = part * plan.chunk_width
                out_ref[at, :, lane : lane + plan.chunk_width] = (
                    held[0] if plan.heads == 1 else jnp.concatenate(held, axis=1)
                )


def finish(plan, place, gq_first, gq_rest, gkv, far):
    outs = [shape((3,) + plan.piece) for _ in range(plan.devs)]
    scratch = [pltpu.VMEM((3, plan.heads, plan.seg_rows, plan.dim), BF16)]
    arrays = [gq_first, gq_rest, gkv, far]
    return call(functools.partial(finish_kernel, plan), place, arrays, outs, scratch)


def local(queries, keys, values):
    rows, width = queries.shape
    plan = Plan(rows, width, lax.axis_size("dev"))
    seg_count = lax.axis_size("seg")
    onward = [(i, i + 1) for i in range(seg_count - 1)]
    backward = [(i + 1, i) for i in range(seg_count - 1)]
    me = lax.axis_index("dev")
    place = jnp.stack([lax.axis_index("seg"), me]).astype(jnp.int32)
    arrays = [queries, keys, values]
    arrays = [queries, keys, values]
    arrived = []
    for c in range(plan.chunks):
        pieces = pack(plan, c, place, arrays)
        arrived.append(exchange(plan, pieces))
    returned = []
    for pieces in arrived:
        halo = jnp.stack(
            [
                lax.select_n((plan.devs - plan.reach + b) ^ me, *[p[1:] for p in pieces])
                for b in range(plan.reach)
            ]
        )
        halo = lax.ppermute(halo, "seg", onward)
        held, target = teacher(plan, place, pieces)
        gq_first, gkv, far = first_blocks(plan, place, held, target, halo)
        far = lax.ppermute(far, "seg", backward)
        gq_rest, gkv = rest_blocks(plan, place, held, target, gkv)
        pieces = finish(plan, place, gq_first, gq_rest, gkv, far)
        returned.append(exchange(plan, pieces))
    return tuple(unpack(plan, place, returned))


def solution(mesh):
    spec = P(("seg", "dev"), None)
    return jax.shard_map(
        local, mesh=mesh, in_specs=(spec,) * 3, out_specs=(spec,) * 3, check_vma=False
    )
```

profile of v0, /device:TPU:13, one launch (start us, length us, event | category | flops | bytes accessed | tf_op | source)
XLA Modules:
  0.0 97.6 jit_solution(12876392325486534239)
XLA Ops:
  0.7 1.0 %copy-done = bf16[128,1536]{1,0:T(8,128)(2,1)S(1)} copy-done((bf16[128,1536]{1,0:T(8,128)(2,1)S(1)}, bf16[128,1536]{1,0:T(8,128)(2,1)}, u32[]{:S(2)}) %copy-start) | copy-done | bytes 393240
  1.7 1.0 %copy-done.1 = bf16[128,1536]{1,0:T(8,128)(2,1)S(1)} copy-done((bf16[128,1536]{1,0:T(8,128)(2,1)S(1)}, bf16[128,1536]{1,0:T(8,128)(2,1)}, u32[]{:S(2)}) %copy-start.1) | copy-done | bytes 393240
  2.7 1.0 %copy-done.2 = bf16[128,1536]{1,0:T(8,128)(2,1)S(1)} copy-done((bf16[128,1536]{1,0:T(8,128)(2,1)S(1)}, bf16[128,1536]{1,0:T(8,128)(2,1)}, u32[]{:S(2)}) %copy-start.2) | copy-done | bytes 393240
  3.7 1.5 %shard_map.63 = (bf16[3,64,384]{2,1,0:T(8,128)(2,1)S(1)}, bf16[3,64,384]{2,1,0:T(8,128)(2,1)S(1)}, bf16[3,64,384]{2,1,0:T(8,128)(2,1)S(1)}, bf16[3,64,384]{2,1,0:T(8,128)(2,1)S(1)}) custom-call(s32[2]{0:T(128)S(1)} %pad_add_fusion.place, bf16[128,1536]{1,0:T(8,128)(2,1)S(1)} %copy-done, bf16[128,1536]{1,0:T(8,128)(2,1)S(1)} %copy-done.1, ...), custom_call_target="tpu_custom_call" | custom-call | bytes 1769472 | tf_op jit(solution)/shard_map/pallas_call | solution.py:29
  5.2 1.4 %collective-permute-start.10 = (bf16[3,64,384]{2,1,0:T(8,128)(2,1)S(1)}, bf16[3,64,384]{2,1,0:T(8,128)(2,1)S(1)}, u32[]{:S(2)}, u32[]{:S(2)}) collective-permute-start(bf16[3,64,384]{2,1,0:T(8,128)(2,1)S(1)} %get-tuple-element.51), channel_id=1, source_target_pairs={{0,3},{1,2},{2,1},{3,0},{4,7},{5,6},{6,5},{7,4},{8,11},{9,10},{10,... | collective-permute-start | bytes 442376 | tf_op jit(solution)/shard_map/ppermute | solution.py:137
  6.5 2.2 %collective-permute-start.8 = (bf16[3,64,384]{2,1,0:T(8,128)(2,1)S(1)}, bf16[3,64,384]{2,1,0:T(8,128)(2,1)S(1)}, u32[]{:S(2)}, u32[]{:S(2)}) collective-permute-start(bf16[3,64,384]{2,1,0:T(8,128)(2,1)S(1)} %get-tuple-element.49), channel_id=1, source_target_pairs={{0,1},{1,0},{2,3},{3,2},{4,5},{5,4},{6,7},{7,6},{8,9},{9,8},{10,11... | collective-permute-start | bytes 442376 | tf_op jit(solution)/shard_map/ppermute | solution.py:137
  8.7 1.4 %shard_map.58 = (bf16[3,64,384]{2,1,0:T(8,128)(2,1)S(1)}, bf16[3,64,384]{2,1,0:T(8,128)(2,1)S(1)}, bf16[3,64,384]{2,1,0:T(8,128)(2,1)S(1)}, bf16[3,64,384]{2,1,0:T(8,128)(2,1)S(1)}) custom-call(s32[2]{0:T(128)S(1)} %pad_add_fusion.place, bf16[128,1536]{1,0:T(8,128)(2,1)S(1)} %copy-done, bf16[128,1536]{1,0:T(8,128)(2,1)S(1)} %copy-done.1, ...), custom_call_target="tpu_custom_call" | custom-call | bytes 1769472 | tf_op jit(solution)/shard_map/pallas_call | solution.py:29
  10.6 2.1 %collective-permute-start.1 = (bf16[3,64,384]{2,1,0:T(8,128)(2,1)S(1)}, bf16[3,64,384]{2,1,0:T(8,128)(2,1)S(1)}, u32[]{:S(2)}, u32[]{:S(2)}) collective-permute-start(bf16[3,64,384]{2,1,0:T(8,128)(2,1)S(1)} %get-tuple-element.35), channel_id=1, source_target_pairs={{0,2},{1,3},{2,0},{3,1},{4,6},{5,7},{6,4},{7,5},{8,10},{9,11},{10,... | collective-permute-start | bytes 442376 | tf_op jit(solution)/shard_map/ppermute | solution.py:137
  12.7 0.6 collective-permute-done.10.refs_3_
  13.4 1.9 %collective-permute-done.8.refs_1_ = bf16[3,64,384]{2,1,0:T(8,128)(2,1)S(1)} collective-permute-done((bf16[3,64,384]{2,1,0:T(8,128)(2,1)S(1)}, bf16[3,64,384]{2,1,0:T(8,128)(2,1)S(1)}, u32[]{:S(2)}, u32[]{:S(2)}) %collective-permute-start.8) | collective-permute-done | bytes 147488 | tf_op jit(solution)/shard_map/ppermute | solution.py:137
  15.2 2.1 %collective-permute-done.9.refs_2_ = bf16[3,64,384]{2,1,0:T(8,128)(2,1)S(1)} collective-permute-done((bf16[3,64,384]{2,1,0:T(8,128)(2,1)S(1)}, bf16[3,64,384]{2,1,0:T(8,128)(2,1)S(1)}, u32[]{:S(2)}, u32[]{:S(2)}) %collective-permute-start.9) | collective-permute-done | bytes 147488 | tf_op jit(solution)/shard_map/ppermute | solution.py:137
  17.4 6.9 %collective-permute-start.11 = (bf16[2,2,64,384]{3,2,1,0:T(8,128)(2,1)S(1)}, bf16[2,2,64,384]{3,2,1,0:T(8,128)(2,1)S(1)}, u32[]{:S(2)}, u32[]{:S(2)}) collective-permute-start(bf16[2,2,64,384]{3,2,1,0:T(8,128)(2,1)S(1)} %pad_maximum_fusion.1), channel_id=1, source_target_pairs={{0,4},{4,8},{8,12},{12,16},{16,20},{20,24},{24,28},{1,5},{5,9},{9,... | collective-permute-start | bytes 589832 | tf_op jit(solution)/shard_map/ppermute | solution.py:370
  24.3 8.0 %collective-permute-done.2.refs_3_ = bf16[3,64,384]{2,1,0:T(8,128)(2,1)S(1)} collective-permute-done((bf16[3,64,384]{2,1,0:T(8,128)(2,1)S(1)}, bf16[3,64,384]{2,1,0:T(8,128)(2,1)S(1)}, u32[]{:S(2)}, u32[]{:S(2)}) %collective-permute-start.2) | collective-permute-done | bytes 147488 | tf_op jit(solution)/shard_map/ppermute | solution.py:137
  32.4 4.3 %collective-permute-start.3 = (bf16[2,2,64,384]{3,2,1,0:T(8,128)(2,1)S(1)}, bf16[2,2,64,384]{3,2,1,0:T(8,128)(2,1)S(1)}, u32[]{:S(2)}, u32[]{:S(2)}) collective-permute-start(bf16[2,2,64,384]{3,2,1,0:T(8,128)(2,1)S(1)} %pad_maximum_fusion), channel_id=1, source_target_pairs={{0,4},{4,8},{8,12},{12,16},{16,20},{20,24},{24,28},{1,5},{5,9},{9,... | collective-permute-start | bytes 589832 | tf_op jit(solution)/shard_map/ppermute | solution.py:370
  36.8 3.3 %shard_map.64 = (bf16[3,2,512,96]{3,2,1,0:T(8,128)(2,1)S(1)}, bf16[2,512,96]{2,1,0:T(8,128)(2,1)S(1)}) custom-call(s32[2]{0:T(128)S(1)} %pad_add_fusion.place, bf16[3,64,384]{2,1,0:T(8,128)(2,1)S(1)} %get-tuple-element.48.refs_0_, bf16[3,64,384]{2,1,0:T(8,128)(2,1)S(1)} %collective-permute-done.8.refs_1_, ...), custom_call_target="tpu_custom_call" | custom-call | flops 201326592 | bytes 1376256 | tf_op jit(solution)/shard_map/pallas_call | solution.py:29
  40.1 4.3 %shard_map.65 = (bf16[2,256,96]{2,1,0:T(8,128)(2,1)S(1)}, f32[2,2,256,96]{3,2,1,0:T(8,128)S(1)}, bf16[2,2,64,384]{3,2,1,0:T(8,128)(2,1)S(1)}) custom-call(s32[2]{0:T(128)S(1)} %pad_add_fusion.place, bf16[3,2,512,96]{3,2,1,0:T(8,128)(2,1)S(1)} %get-tuple-element.52.held_ref, bf16[2,512,96]{2,1,0:T(8,128)(2,1)S(1)} %get-tuple-element.53.target_ref, ...), custom_call_target="tpu_custom_call" | custom-call | flops 226492416 | bytes 1671168 | tf_op jit(solution)/shard_map/pallas_call | solution.py:29
  44.4 1.9 %collective-permute-start.12 = (bf16[2,2,64,384]{3,2,1,0:T(8,128)(2,1)S(1)}, bf16[2,2,64,384]{3,2,1,0:T(8,128)(2,1)S(1)}, u32[]{:S(2)}, u32[]{:S(2)}) collective-permute-start(bf16[2,2,64,384]{3,2,1,0:T(8,128)(2,1)S(1)} %get-tuple-element.58), channel_id=1, source_target_pairs={{4,0},{8,4},{12,8},{16,12},{20,16},{24,20},{28,24},{5,1},{9,5},{13... | collective-permute-start | bytes 589832 | tf_op jit(solution)/shard_map/ppermute | solution.py:373
  46.3 3.3 %shard_map.59 = (bf16[3,2,512,96]{3,2,1,0:T(8,128)(2,1)S(1)}, bf16[2,512,96]{2,1,0:T(8,128)(2,1)S(1)}) custom-call(s32[2]{0:T(128)S(1)} %pad_add_fusion.place, bf16[3,64,384]{2,1,0:T(8,128)(2,1)S(1)} %get-tuple-element.33.refs_0_, bf16[3,64,384]{2,1,0:T(8,128)(2,1)S(1)} %collective-permute-done.refs_1_, ...), custom_call_target="tpu_custom_call" | custom-call | flops 201326592 | bytes 1376256 | tf_op jit(solution)/shard_map/pallas_call | solution.py:29
  49.6 4.3 %shard_map.60 = (bf16[2,256,96]{2,1,0:T(8,128)(2,1)S(1)}, f32[2,2,256,96]{3,2,1,0:T(8,128)S(1)}, bf16[2,2,64,384]{3,2,1,0:T(8,128)(2,1)S(1)}) custom-call(s32[2]{0:T(128)S(1)} %pad_add_fusion.place, bf16[3,2,512,96]{3,2,1,0:T(8,128)(2,1)S(1)} %get-tuple-element.37.held_ref, bf16[2,512,96]{2,1,0:T(8,128)(2,1)S(1)} %get-tuple-element.38.target_ref, ...), custom_call_target="tpu_custom_call" | custom-call | flops 226492416 | bytes 1671168 | tf_op jit(solution)/shard_map/pallas_call | solution.py:29
  53.9 3.4 %collective-permute-start.4 = (bf16[2,2,64,384]{3,2,1,0:T(8,128)(2,1)S(1)}, bf16[2,2,64,384]{3,2,1,0:T(8,128)(2,1)S(1)}, u32[]{:S(2)}, u32[]{:S(2)}) collective-permute-start(bf16[2,2,64,384]{3,2,1,0:T(8,128)(2,1)S(1)} %get-tuple-element.43), channel_id=1, source_target_pairs={{4,0},{8,4},{12,8},{16,12},{20,16},{24,20},{28,24},{5,1},{9,5},{13... | collective-permute-start | bytes 589832 | tf_op jit(solution)/shard_map/ppermute | solution.py:373
  57.4 4.0 %shard_map.66 = (bf16[2,256,96]{2,1,0:T(8,128)(2,1)S(1)}, f32[2,2,512,96]{3,2,1,0:T(8,128)S(1)}) custom-call(s32[2]{0:T(128)S(1)} %pad_add_fusion.place, bf16[3,2,512,96]{3,2,1,0:T(8,128)(2,1)S(1)} %get-tuple-element.52.held_ref, bf16[2,512,96]{2,1,0:T(8,128)(2,1)S(1)} %get-tuple-element.53.target_ref, f32[2,2,256,96]{3,2,1,0:T(8,128)S(1)} %get-tuple-element.55.start_ref), custom_call_target="tpu_custom_call" | custom-call | flops 226492416 | bytes 2064384 | tf_op jit(solution)/shard_map/pallas_call | solution.py:29
  61.4 1.3 %shard_map.67 = (bf16[3,64,384]{2,1,0:T(8,128)(2,1)S(1)}, bf16[3,64,384]{2,1,0:T(8,128)(2,1)S(1)}, bf16[3,64,384]{2,1,0:T(8,128)(2,1)S(1)}, bf16[3,64,384]{2,1,0:T(8,128)(2,1)S(1)}) custom-call(s32[2]{0:T(128)S(1)} %pad_add_fusion.place, bf16[2,256,96]{2,1,0:T(8,128)(2,1)S(1)} %get-tuple-element.54.gq_first, ...), custom_call_target="tpu_custom_call" | custom-call | bytes 1769472 | tf_op jit(solution)/shard_map/pallas_call | solution.py:29
  62.8 4.0 %shard_map.61 = (bf16[2,256,96]{2,1,0:T(8,128)(2,1)S(1)}, f32[2,2,512,96]{3,2,1,0:T(8,128)S(1)}) custom-call(s32[2]{0:T(128)S(1)} %pad_add_fusion.place, bf16[3,2,512,96]{3,2,1,0:T(8,128)(2,1)S(1)} %get-tuple-element.37.held_ref, bf16[2,512,96]{2,1,0:T(8,128)(2,1)S(1)} %get-tuple-element.38.target_ref, f32[2,2,256,96]{3,2,1,0:T(8,128)S(1)} %get-tuple-element.40.start_ref), custom_call_target="tpu_custom_call" | custom-call | flops 226492416 | bytes 2064384 | tf_op jit(solution)/shard_map/pallas_call | solution.py:29
  66.8 2.5 %collective-permute-start.14 = (bf16[3,64,384]{2,1,0:T(8,128)(2,1)S(1)}, bf16[3,64,384]{2,1,0:T(8,128)(2,1)S(1)}, u32[]{:S(2)}, u32[]{:S(2)}) collective-permute-start(bf16[3,64,384]{2,1,0:T(8,128)(2,1)S(1)} %get-tuple-element.61), channel_id=1, source_target_pairs={{0,2},{1,3},{2,0},{3,1},{4,6},{5,7},{6,4},{7,5},{8,10},{9,11},{10,... | collective-permute-start | bytes 442376 | tf_op jit(solution)/shard_map/ppermute | solution.py:137
  69.5 1.3 %shard_map.62 = (bf16[3,64,384]{2,1,0:T(8,128)(2,1)S(1)}, bf16[3,64,384]{2,1,0:T(8,128)(2,1)S(1)}, bf16[3,64,384]{2,1,0:T(8,128)(2,1)S(1)}, bf16[3,64,384]{2,1,0:T(8,128)(2,1)S(1)}) custom-call(s32[2]{0:T(128)S(1)} %pad_add_fusion.place, bf16[2,256,96]{2,1,0:T(8,128)(2,1)S(1)} %get-tuple-element.39.gq_first, ...), custom_call_target="tpu_custom_call" | custom-call | bytes 1769472 | tf_op jit(solution)/shard_map/pallas_call | solution.py:29
  70.9 1.1 %collective-permute-start.5 = (bf16[3,64,384]{2,1,0:T(8,128)(2,1)S(1)}, bf16[3,64,384]{2,1,0:T(8,128)(2,1)S(1)}, u32[]{:S(2)}, u32[]{:S(2)}) collective-permute-start(bf16[3,64,384]{2,1,0:T(8,128)(2,1)S(1)} %get-tuple-element.45), channel_id=1, source_target_pairs={{0,1},{1,0},{2,3},{3,2},{4,5},{5,4},{6,7},{7,6},{8,9},{9,8},{10,11... | collective-permute-start | bytes 442376 | tf_op jit(solution)/shard_map/ppermute | solution.py:137
  72.0 1.4 %collective-permute-start.6 = (bf16[3,64,384]{2,1,0:T(8,128)(2,1)S(1)}, bf16[3,64,384]{2,1,0:T(8,128)(2,1)S(1)}, u32[]{:S(2)}, u32[]{:S(2)}) collective-permute-start(bf16[3,64,384]{2,1,0:T(8,128)(2,1)S(1)} %get-tuple-element.46), channel_id=1, source_target_pairs={{0,2},{1,3},{2,0},{3,1},{4,6},{5,7},{6,4},{7,5},{8,10},{9,11},{10,... | collective-permute-start | bytes 442376 | tf_op jit(solution)/shard_map/ppermute | solution.py:137
  73.6 5.3 %collective-permute-done.14.refs_6_ = bf16[3,64,384]{2,1,0:T(8,128)(2,1)S(1)} collective-permute-done((bf16[3,64,384]{2,1,0:T(8,128)(2,1)S(1)}, bf16[3,64,384]{2,1,0:T(8,128)(2,1)S(1)}, u32[]{:S(2)}, u32[]{:S(2)}) %collective-permute-start.14) | collective-permute-done | bytes 147488 | tf_op jit(solution)/shard_map/ppermute | solution.py:137
  78.9 10.6 %collective-permute-done.15.refs_7_ = bf16[3,64,384]{2,1,0:T(8,128)(2,1)S(1)} collective-permute-done((bf16[3,64,384]{2,1,0:T(8,128)(2,1)S(1)}, bf16[3,64,384]{2,1,0:T(8,128)(2,1)S(1)}, u32[]{:S(2)}, u32[]{:S(2)}) %collective-permute-start.15) | collective-permute-done | bytes 147488 | tf_op jit(solution)/shard_map/ppermute | solution.py:137
  89.5 2.1 %collective-permute-done.6.refs_2_ = bf16[3,64,384]{2,1,0:T(8,128)(2,1)S(1)} collective-permute-done((bf16[3,64,384]{2,1,0:T(8,128)(2,1)S(1)}, bf16[3,64,384]{2,1,0:T(8,128)(2,1)S(1)}, u32[]{:S(2)}, u32[]{:S(2)}) %collective-permute-start.6) | collective-permute-done | bytes 147488 | tf_op jit(solution)/shard_map/ppermute | solution.py:137
  91.7 4.2 %collective-permute-done.7.refs_3_ = bf16[3,64,384]{2,1,0:T(8,128)(2,1)S(1)} collective-permute-done((bf16[3,64,384]{2,1,0:T(8,128)(2,1)S(1)}, bf16[3,64,384]{2,1,0:T(8,128)(2,1)S(1)}, u32[]{:S(2)}, u32[]{:S(2)}) %collective-permute-start.7) | collective-permute-done | bytes 147488 | tf_op jit(solution)/shard_map/ppermute | solution.py:137
  95.8 1.8 %shard_map.68 = (bf16[128,1536]{1,0:T(8,128)(2,1)}, bf16[128,1536]{1,0:T(8,128)(2,1)}, bf16[128,1536]{1,0:T(8,128)(2,1)}) custom-call(s32[2]{0:T(128)S(1)} %pad_add_fusion.place, bf16[3,64,384]{2,1,0:T(8,128)(2,1)S(1)} %get-tuple-element.44.refs_0_, bf16[3,64,384]{2,1,0:T(8,128)(2,1)S(1)} %collective-permute-done.5.refs_1_, ...), custom_call_target="tpu_custom_call" | custom-call | bytes 2359296 | tf_op jit(solution)/shard_map/pallas_call | solution.py:29
  (22 shorter events, 1.2 us)
Async XLA Ops:
  0.7 1.0 %copy-start = (bf16[128,1536]{1,0:T(8,128)(2,1)S(1)}, bf16[128,1536]{1,0:T(8,128)(2,1)}, u32[]{:S(2)}) copy-start(bf16[128,1536]{1,0:T(8,128)(2,1)} %refs_0_.3) | copy-start | bytes 1179652
  1.7 1.0 %copy-start.1 = (bf16[128,1536]{1,0:T(8,128)(2,1)S(1)}, bf16[128,1536]{1,0:T(8,128)(2,1)}, u32[]{:S(2)}) copy-start(bf16[128,1536]{1,0:T(8,128)(2,1)} %refs_1_.3) | copy-start | bytes 1179652
  2.7 1.0 %copy-start.2 = (bf16[128,1536]{1,0:T(8,128)(2,1)S(1)}, bf16[128,1536]{1,0:T(8,128)(2,1)}, u32[]{:S(2)}) copy-start(bf16[128,1536]{1,0:T(8,128)(2,1)} %refs_2_.3) | copy-start | bytes 1179652
  5.2 8.1 %collective-permute-start.10 = (bf16[3,64,384]{2,1,0:T(8,128)(2,1)S(1)}, bf16[3,64,384]{2,1,0:T(8,128)(2,1)S(1)}, u32[]{:S(2)}, u32[]{:S(2)}) collective-permute-start(bf16[3,64,384]{2,1,0:T(8,128)(2,1)S(1)} %get-tuple-element.51), channel_id=1, source_target_pairs={{0,3},{1,2},{2,1},{3,0},{4,7},{5,6},{6,5},{7,4},{8,11},{9,10},{10,... | collective-permute-start | bytes 442376 | tf_op jit(solution)/shard_map/ppermute | solution.py:137
  6.5 8.7 %collective-permute-start.8 = (bf16[3,64,384]{2,1,0:T(8,128)(2,1)S(1)}, bf16[3,64,384]{2,1,0:T(8,128)(2,1)S(1)}, u32[]{:S(2)}, u32[]{:S(2)}) collective-permute-start(bf16[3,64,384]{2,1,0:T(8,128)(2,1)S(1)} %get-tuple-element.49), channel_id=1, source_target_pairs={{0,1},{1,0},{2,3},{3,2},{4,5},{5,4},{6,7},{7,6},{8,9},{9,8},{10,11... | collective-permute-start | bytes 442376 | tf_op jit(solution)/shard_map/ppermute | solution.py:137
  8.7 8.6 %collective-permute-start.9 = (bf16[3,64,384]{2,1,0:T(8,128)(2,1)S(1)}, bf16[3,64,384]{2,1,0:T(8,128)(2,1)S(1)}, u32[]{:S(2)}, u32[]{:S(2)}) collective-permute-start(bf16[3,64,384]{2,1,0:T(8,128)(2,1)S(1)} %get-tuple-element.50), channel_id=1, source_target_pairs={{0,2},{1,3},{2,0},{3,1},{4,6},{5,7},{6,4},{7,5},{8,10},{9,11},{10,... | collective-permute-start | bytes 442376 | tf_op jit(solution)/shard_map/ppermute | solution.py:137
  10.2 14.1 %collective-permute-start = (bf16[3,64,384]{2,1,0:T(8,128)(2,1)S(1)}, bf16[3,64,384]{2,1,0:T(8,128)(2,1)S(1)}, u32[]{:S(2)}, u32[]{:S(2)}) collective-permute-start(bf16[3,64,384]{2,1,0:T(8,128)(2,1)S(1)} %get-tuple-element.34), channel_id=1, source_target_pairs={{0,1},{1,0},{2,3},{3,2},{4,5},{5,4},{6,7},{7,6},{8,9},{9,8},{10,11... | collective-permute-start | bytes 442376 | tf_op jit(solution)/shard_map/ppermute | solution.py:137
  10.6 13.7 %collective-permute-start.1 = (bf16[3,64,384]{2,1,0:T(8,128)(2,1)S(1)}, bf16[3,64,384]{2,1,0:T(8,128)(2,1)S(1)}, u32[]{:S(2)}, u32[]{:S(2)}) collective-permute-start(bf16[3,64,384]{2,1,0:T(8,128)(2,1)S(1)} %get-tuple-element.35), channel_id=1, source_target_pairs={{0,2},{1,3},{2,0},{3,1},{4,6},{5,7},{6,4},{7,5},{8,10},{9,11},{10,... | collective-permute-start | bytes 442376 | tf_op jit(solution)/shard_map/ppermute | solution.py:137
  13.3 19.0 %collective-permute-start.2 = (bf16[3,64,384]{2,1,0:T(8,128)(2,1)S(1)}, bf16[3,64,384]{2,1,0:T(8,128)(2,1)S(1)}, u32[]{:S(2)}, u32[]{:S(2)}) collective-permute-start(bf16[3,64,384]{2,1,0:T(8,128)(2,1)S(1)} %get-tuple-element.36), channel_id=1, source_target_pairs={{0,3},{1,2},{2,1},{3,0},{4,7},{5,6},{6,5},{7,4},{8,11},{9,10},{10,... | collective-permute-start | bytes 442376 | tf_op jit(solution)/shard_map/ppermute | solution.py:137
  17.4 22.6 %collective-permute-start.11 = (bf16[2,2,64,384]{3,2,1,0:T(8,128)(2,1)S(1)}, bf16[2,2,64,384]{3,2,1,0:T(8,128)(2,1)S(1)}, u32[]{:S(2)}, u32[]{:S(2)}) collective-permute-start(bf16[2,2,64,384]{3,2,1,0:T(8,128)(2,1)S(1)} %pad_maximum_fusion.1), channel_id=1, source_target_pairs={{0,4},{4,8},{8,12},{12,16},{16,20},{20,24},{24,28},{1,5},{5,9},{9,... | collective-permute-start | bytes 589832 | tf_op jit(solution)/shard_map/ppermute | solution.py:370
  32.4 17.2 %collective-permute-start.3 = (bf16[2,2,64,384]{3,2,1,0:T(8,128)(2,1)S(1)}, bf16[2,2,64,384]{3,2,1,0:T(8,128)(2,1)S(1)}, u32[]{:S(2)}, u32[]{:S(2)}) collective-permute-start(bf16[2,2,64,384]{3,2,1,0:T(8,128)(2,1)S(1)} %pad_maximum_fusion), channel_id=1, source_target_pairs={{0,4},{4,8},{8,12},{12,16},{16,20},{20,24},{24,28},{1,5},{5,9},{9,... | collective-permute-start | bytes 589832 | tf_op jit(solution)/shard_map/ppermute | solution.py:370
  44.4 17.0 %collective-permute-start.12 = (bf16[2,2,64,384]{3,2,1,0:T(8,128)(2,1)S(1)}, bf16[2,2,64,384]{3,2,1,0:T(8,128)(2,1)S(1)}, u32[]{:S(2)}, u32[]{:S(2)}) collective-permute-start(bf16[2,2,64,384]{3,2,1,0:T(8,128)(2,1)S(1)} %get-tuple-element.58), channel_id=1, source_target_pairs={{4,0},{8,4},{12,8},{16,12},{20,16},{24,20},{28,24},{5,1},{9,5},{13... | collective-permute-start | bytes 589832 | tf_op jit(solution)/shard_map/ppermute | solution.py:373
  53.9 15.6 %collective-permute-start.4 = (bf16[2,2,64,384]{3,2,1,0:T(8,128)(2,1)S(1)}, bf16[2,2,64,384]{3,2,1,0:T(8,128)(2,1)S(1)}, u32[]{:S(2)}, u32[]{:S(2)}) collective-permute-start(bf16[2,2,64,384]{3,2,1,0:T(8,128)(2,1)S(1)} %get-tuple-element.43), channel_id=1, source_target_pairs={{4,0},{8,4},{12,8},{16,12},{20,16},{24,20},{28,24},{5,1},{9,5},{13... | collective-permute-start | bytes 589832 | tf_op jit(solution)/shard_map/ppermute | solution.py:373
  62.7 10.6 %collective-permute-start.13 = (bf16[3,64,384]{2,1,0:T(8,128)(2,1)S(1)}, bf16[3,64,384]{2,1,0:T(8,128)(2,1)S(1)}, u32[]{:S(2)}, u32[]{:S(2)}) collective-permute-start(bf16[3,64,384]{2,1,0:T(8,128)(2,1)S(1)} %get-tuple-element.60), channel_id=1, source_target_pairs={{0,1},{1,0},{2,3},{3,2},{4,5},{5,4},{6,7},{7,6},{8,9},{9,8},{10,11... | collective-permute-start | bytes 442376 | tf_op jit(solution)/shard_map/ppermute | solution.py:137
  66.8 12.1 %collective-permute-start.14 = (bf16[3,64,384]{2,1,0:T(8,128)(2,1)S(1)}, bf16[3,64,384]{2,1,0:T(8,128)(2,1)S(1)}, u32[]{:S(2)}, u32[]{:S(2)}) collective-permute-start(bf16[3,64,384]{2,1,0:T(8,128)(2,1)S(1)} %get-tuple-element.61), channel_id=1, source_target_pairs={{0,2},{1,3},{2,0},{3,1},{4,6},{5,7},{6,4},{7,5},{8,10},{9,11},{10,... | collective-permute-start | bytes 442376 | tf_op jit(solution)/shard_map/ppermute | solution.py:137
  69.3 20.2 %collective-permute-start.15 = (bf16[3,64,384]{2,1,0:T(8,128)(2,1)S(1)}, bf16[3,64,384]{2,1,0:T(8,128)(2,1)S(1)}, u32[]{:S(2)}, u32[]{:S(2)}) collective-permute-start(bf16[3,64,384]{2,1,0:T(8,128)(2,1)S(1)} %get-tuple-element.62), channel_id=1, source_target_pairs={{0,3},{1,2},{2,1},{3,0},{4,7},{5,6},{6,5},{7,4},{8,11},{9,10},{10,... | collective-permute-start | bytes 442376 | tf_op jit(solution)/shard_map/ppermute | solution.py:137
  70.9 18.6 %collective-permute-start.5 = (bf16[3,64,384]{2,1,0:T(8,128)(2,1)S(1)}, bf16[3,64,384]{2,1,0:T(8,128)(2,1)S(1)}, u32[]{:S(2)}, u32[]{:S(2)}) collective-permute-start(bf16[3,64,384]{2,1,0:T(8,128)(2,1)S(1)} %get-tuple-element.45), channel_id=1, source_target_pairs={{0,1},{1,0},{2,3},{3,2},{4,5},{5,4},{6,7},{7,6},{8,9},{9,8},{10,11... | collective-permute-start | bytes 442376 | tf_op jit(solution)/shard_map/ppermute | solution.py:137
  72.0 19.6 %collective-permute-start.6 = (bf16[3,64,384]{2,1,0:T(8,128)(2,1)S(1)}, bf16[3,64,384]{2,1,0:T(8,128)(2,1)S(1)}, u32[]{:S(2)}, u32[]{:S(2)}) collective-permute-start(bf16[3,64,384]{2,1,0:T(8,128)(2,1)S(1)} %get-tuple-element.46), channel_id=1, source_target_pairs={{0,2},{1,3},{2,0},{3,1},{4,6},{5,7},{6,4},{7,5},{8,10},{9,11},{10,... | collective-permute-start | bytes 442376 | tf_op jit(solution)/shard_map/ppermute | solution.py:137
  73.4 22.4 %collective-permute-start.7 = (bf16[3,64,384]{2,1,0:T(8,128)(2,1)S(1)}, bf16[3,64,384]{2,1,0:T(8,128)(2,1)S(1)}, u32[]{:S(2)}, u32[]{:S(2)}) collective-permute-start(bf16[3,64,384]{2,1,0:T(8,128)(2,1)S(1)} %get-tuple-element.47), channel_id=1, source_target_pairs={{0,3},{1,2},{2,1},{3,0},{4,7},{5,6},{6,5},{7,4},{8,11},{9,10},{10,... | collective-permute-start | bytes 442376 | tf_op jit(solution)/shard_map/ppermute | solution.py:137
where the time goes:
time: 97.9 us; the launch traced here: 97.6 us
  waiting for transfers between devices  34.8 us (36%)
  Pallas kernels  30.6 us (31%)
  starting transfers between devices  28.2 us (29%)
  local copies, waits for them, and re-layouts  2.99 us (3%)
    ppermute x12, waiting for transfers between devices, exchange(): got[step] = lax.ppermute(pieces[step], 'dev', pairs)  34.8 us
    pallas_call x11, Pallas kernels, call(): pl.pallas_call(kernel, out_shape=tuple(outs), in_specs=[SMEM_SPEC] + [spe...  30.6 us
    ppermute x12, starting transfers between devices, exchange(): got[step] = lax.ppermute(pieces[step], 'dev', pairs)  11.6 us
    ppermute x2, starting transfers between devices, local(): halo = lax.ppermute(halo, 'seg', onward)  11.2 us
    ppermute x2, starting transfers between devices, local(): far = lax.ppermute(far, 'seg', backward)  5.37 us
    unnamed x6, local copies, waits for them, and re-layouts  2.99 us
  transfers between devices with their start and end apart: 16, of which 8 were waited for; matrix products, arithmetic and copies ran while one was open for 0% of the time, Pallas kernels for 28%

commit v1 on v0

v1 whole, which is shorter than its diff:
```python
import functools
import math

import jax
import jax.numpy as jnp
from jax import lax
from jax.experimental import pallas as pl
from jax.experimental.pallas import tpu as pltpu
from jax.sharding import PartitionSpec as P


HEADS = 16
WINDOW = 256
CHUNKS = 2
NEGATIVE = -1e30
LOG2E = math.log2(math.e)
BF16 = jnp.bfloat16
F32 = jnp.float32


SMEM_SPEC = pl.BlockSpec(memory_space=pltpu.SMEM)
VMEM_SPEC = pl.BlockSpec(memory_space=pltpu.VMEM)
HBM_SPEC = pl.BlockSpec(memory_space=pltpu.HBM)


def call(kernel, place, arrays, outs, scratch=(), flops=0, spec=VMEM_SPEC):
    moved = sum(a.size * a.dtype.itemsize for a in arrays)
    moved += sum(math.prod(o.shape) * o.dtype.itemsize for o in outs)
    return pl.pallas_call(
        kernel,
        out_shape=tuple(outs),
        in_specs=[SMEM_SPEC] + [spec] * len(arrays),
        out_specs=tuple([VMEM_SPEC] * len(outs)),
        scratch_shapes=list(scratch),
        cost_estimate=pl.CostEstimate(flops=flops, bytes_accessed=moved, transcendentals=0),
        compiler_params=pltpu.CompilerParams(vmem_limit_bytes=48 * 1024 * 1024),
    )(place, *arrays)


def shape(dims, dtype=BF16):
    return jax.ShapeDtypeStruct(dims, dtype)


class Plan:
    def __init__(self, rows, width, devs):
        self.rows, self.width, self.devs = rows, width, devs
        self.dim = width // HEADS
        self.local_heads = HEADS // devs
        self.local_width = width // devs
        self.chunks = CHUNKS if self.local_heads % CHUNKS == 0 else 1
        self.heads = self.local_heads // self.chunks
        self.chunk_width = self.heads * self.dim
        self.fold = 128 // math.gcd(self.chunk_width, 128)
        self.fold_rows = rows // self.fold
        self.piece = (self.fold_rows, self.fold * self.chunk_width)
        self.reach = WINDOW // rows
        self.seg_rows = rows * devs
        self.near = self.reach * rows
        self.groups = self.seg_rows // self.near
        self.teacher_rows = self.seg_rows if self.seg_rows <= 512 else rows
        self.scale = self.dim ** (-0.5)


def folded(x, plan):
    full = plan.chunk_width // 128 * 128
    parts = [x[i * plan.fold_rows : (i + 1) * plan.fold_rows] for i in range(plan.fold)]
    columns = [p[:, at : at + 128] for at in range(0, full, 128) for p in parts]
    if plan.chunk_width > full:
        columns += [p[:, full:] for p in parts]
    return columns[0] if len(columns) == 1 else jnp.concatenate(columns, axis=1)


def unfolded(x, plan):
    full = plan.chunk_width // 128 * 128
    rest = plan.chunk_width - full
    groups = []
    for i in range(plan.fold):
        columns = [
            x[:, at * plan.fold + i * 128 : at * plan.fold + (i + 1) * 128]
            for at in range(0, full, 128)
        ]
        if rest:
            start = plan.fold * full + i * rest
            columns.append(x[:, start : start + rest])
        groups.append(columns[0] if len(columns) == 1 else jnp.concatenate(columns, axis=1))
    return groups


def pack_kernel(plan, chunk, place, *refs):
    me = place[1]
    in_refs, out_refs = refs[:3], refs[3 : 3 + plan.devs]
    held, sems = refs[3 + plan.devs :]
    copies = [pltpu.make_async_copy(r, held.at[i], sems.at[i]) for i, r in enumerate(in_refs)]
    for copy in copies:
        copy.start()
    for at, copy in enumerate(copies):
        copy.wait()
        for step, out_ref in enumerate(out_refs):
            start = pl.multiple_of((me ^ step) * plan.local_width, 128)
            x = held[at, :, pl.ds(start, plan.local_width)]
            x = x[:, chunk * plan.chunk_width : (chunk + 1) * plan.chunk_width]
            out_ref[at] = folded(x, plan)


def pack(plan, chunk, place, arrays):
    if plan.local_width % 128 == 0:
        outs = [shape((3,) + plan.piece) for _ in range(plan.devs)]
        scratch = [
            pltpu.VMEM((3, plan.rows, plan.width), BF16),
            pltpu.SemaphoreType.DMA((3,)),
        ]
        kernel = functools.partial(pack_kernel, plan, chunk)
        return call(kernel, place, arrays, outs, scratch, spec=HBM_SPEC)
    pieces = []
    for step in range(plan.devs):
        start = (place[1] ^ step) * plan.local_width + chunk * plan.chunk_width
        taken = [lax.dynamic_slice_in_dim(a, start, plan.chunk_width, 1) for a in arrays]
        pieces.append(jnp.stack([folded(x, plan) for x in taken]))
    return pieces


def unpack_kernel(plan, place, *refs):
    me = place[1]
    piece_refs, out_refs = refs[:-3], refs[-3:]
    for step in range(plan.devs):
        start = pl.multiple_of((me ^ step) * plan.local_width, 128)
        for at, out_ref in enumerate(out_refs):
            held = [unfolded(piece_refs[c * plan.devs + step][at], plan) for c in range(plan.chunks)]
            for part in range(plan.fold):
                rows = slice(part * plan.fold_rows, (part + 1) * plan.fold_rows)
                x = [groups[part] for groups in held]
                out_ref[rows, pl.ds(start, plan.local_width)] = (
                    x[0] if plan.chunks == 1 else jnp.concatenate(x, axis=1)
                )


def unpack(plan, place, pieces):
    if plan.local_width % 128 == 0:
        flat = [piece for chunk in pieces for piece in chunk]
        outs = [shape((plan.rows, plan.width)) for _ in range(3)]
        return call(functools.partial(unpack_kernel, plan), place, flat, outs)
    order = jnp.arange(plan.devs, dtype=jnp.int32) ^ place[1]
    chunks = []
    for chunk in pieces:
        x = jnp.take(jnp.stack(chunk), order, axis=0)
        x = [jnp.concatenate(unfolded(x[d, at], plan), 0) for d in range(plan.devs) for at in range(3)]
        x = jnp.stack(x).reshape(plan.devs, 3, plan.rows, plan.chunk_width)
        chunks.append(x.transpose(1, 2, 0, 3))
    out = jnp.concatenate(chunks, axis=3).reshape(3, plan.rows, plan.width)
    return out[0], out[1], out[2]


def exchange(plan, pieces):
    got = [pieces[0]] + [None] * (plan.devs - 1)
    for step in range(plan.devs - 1, 0, -1):
        pairs = [(i, i ^ step) for i in range(plan.devs)]
        got[step] = lax.ppermute(pieces[step], "dev", pairs)
    return got


def dot(a, b, over):
    return lax.dot_general(a, b, ((over[:1], over[1:]), ((), ())), preferred_element_type=F32)


def of_head(x, head, plan):
    if plan.heads == 1:
        return x
    lane = lax.broadcasted_iota(jnp.int32, x.shape, 1)
    own = (lane >= head * plan.dim) & (lane < (head + 1) * plan.dim)
    return jnp.where(own, x, jnp.zeros_like(x))


def block_parts(first, plan):
    for part in range(plan.fold):
        start = first + part * plan.fold_rows
        yield part, pl.ds(pl.multiple_of(start, plan.fold_rows), plan.fold_rows)


def teacher_kernel(plan, place, *refs):
    me = place[1]
    piece_refs, (q_ref, k_ref, v_ref, target_ref) = refs[: plan.devs], refs[plan.devs :]
    for step, ref in enumerate(piece_refs):
        blocks = [unfolded(ref[at], plan) for at in range(3)]
        for part, rows in block_parts((me ^ step) * plan.rows, plan):
            q_ref[rows, :] = blocks[0][part]
            for head in range(plan.heads):
                k_ref[head, rows, :] = of_head(blocks[1][part], head, plan)
                v_ref[head, rows, :] = of_head(blocks[2][part], head, plan)

    def one(start, count):
        rows = pl.ds(start, count)
        total = None
        for head in range(plan.heads):
            scores = dot(q_ref[rows, :], k_ref[head], (1, 1))
            top = scores.max(-1, keepdims=True)
            e = jnp.exp2((scores - top) * (plan.scale * LOG2E))
            out = dot(e.astype(BF16), v_ref[head], (1, 0)) / e.sum(-1, keepdims=True)
            total = out if total is None else total + out
        target_ref[rows, :] = total.astype(BF16)

    count = plan.teacher_rows
    if count == plan.seg_rows:
        one(0, count)
    else:

        def body(i, _):
            one(pl.multiple_of(i * count, count), count)
            return 0

        lax.fori_loop(0, plan.seg_rows // count, body, 0)


def teacher(plan, place, pieces):
    outs = [
        shape((plan.seg_rows, plan.chunk_width)),
        shape((plan.heads, plan.seg_rows, plan.chunk_width)),
        shape((plan.heads, plan.seg_rows, plan.chunk_width)),
        shape((plan.seg_rows, plan.chunk_width)),
    ]
    flops = 4 * plan.heads * plan.seg_rows * plan.seg_rows * plan.dim
    return call(functools.partial(teacher_kernel, plan), place, list(pieces), outs, flops=flops)


def student_group(plan, q, k, v, target, closed):
    heads = range(plan.heads)
    weights, probability = [], []
    out = None
    for head in heads:
        scores = dot(q, k[head], (1, 1))
        query_at = lax.broadcasted_iota(jnp.int32, scores.shape, 0)
        key_at = lax.broadcasted_iota(jnp.int32, scores.shape, 1)
        low = query_at if closed is None else jnp.maximum(query_at, closed)
        allowed = (key_at >= low) & (key_at <= query_at + plan.near)
        scores = jnp.where(allowed, scores, NEGATIVE)
        top = scores.max(-1, keepdims=True)
        e = jnp.exp2((scores - top) * (plan.scale * LOG2E))
        p = e * (1.0 / e.sum(-1, keepdims=True))
        probability.append(p)
        weights.append(p.astype(BF16))
        part = dot(weights[head], v[head], (1, 0))
        out = part if out is None else out + part
    d_out = (128.0 * (out - target.astype(F32))).astype(BF16)
    gq = gk = gv = None
    for head in heads:
        d_prob = dot(d_out, v[head], (1, 1))
        p = probability[head]
        inner = (p * d_prob).sum(-1, keepdims=True)
        d_scores = (p * (d_prob - inner) * plan.scale).astype(BF16)
        parts = (
            dot(d_scores, k[head], (1, 0)),
            dot(d_scores, of_head(q, head, plan), (0, 0)),
            dot(weights[head], of_head(d_out, head, plan), (0, 0)),
        )
        gq, gk, gv = parts if gq is None else (gq + parts[0], gk + parts[1], gv + parts[2])
    return gq, gk, gv


def first_kernel(
    plan, place, q_ref, k_ref, v_ref, target_ref, halo_ref, gq_ref, gk_ref, gv_ref, far_ref, ext
):
    near, heads = plan.near, range(plan.heads)
    for at, ref in enumerate((k_ref, v_ref)):
        for block in range(plan.reach):
            groups = unfolded(halo_ref[block, at], plan)
            for part, rows in block_parts(block * plan.rows, plan):
                for head in heads:
                    ext[at, head, rows, :] = of_head(groups[part], head, plan)
        for head in heads:
            ext[at, head, near:, :] = ref[head, :near, :]
    gq, gk, gv = student_group(
        plan,
        q_ref[:near, :],
        [ext[0, head] for head in heads],
        [ext[1, head] for head in heads],
        target_ref[:near, :],
        jnp.where(place[0] == 0, near, 0),
    )
    gq_ref[...] = gq.astype(BF16)
    for at, (grad, ref) in enumerate(((gk, gk_ref), (gv, gv_ref))):
        ref[...] = grad[near:]
        for block in range(plan.reach):
            rows = slice(block * plan.rows, (block + 1) * plan.rows)
            far_ref[block, at] = folded(grad[rows].astype(BF16), plan)


def first_group(plan, place, held, halo):
    near = plan.near
    outs = [
        shape((near, plan.chunk_width)),
        shape((near, plan.chunk_width), F32),
        shape((near, plan.chunk_width), F32),
        shape((plan.reach, 2) + plan.piece),
    ]
    scratch = [pltpu.VMEM((2, plan.heads, 2 * near, plan.chunk_width), BF16)]
    flops = 24 * plan.heads * near * near * plan.dim
    kernel = functools.partial(first_kernel, plan)
    return call(kernel, place, list(held) + [halo], outs, scratch, flops)


def rest_kernel(
    plan, place, q_ref, k_ref, v_ref, target_ref, k_start, v_start, gq_ref, gk_ref, gv_ref
):
    near, heads = plan.near, range(plan.heads)

    def group(start):
        rows, keys = pl.ds(start + near, near), pl.ds(start, 2 * near)
        return student_group(
            plan,
            q_ref[rows, :],
            [k_ref[head, keys, :] for head in heads],
            [v_ref[head, keys, :] for head in heads],
            target_ref[rows, :],
            None,
        )

    if plan.groups == 2:
        gq, gk, gv = group(0)
        gq_ref[...] = gq.astype(BF16)
        for grad, start, ref in ((gk, k_start, gk_ref), (gv, v_start, gv_ref)):
            ref[:near, :] = grad[:near] + start[...]
            ref[near:, :] = grad[near:]
        return
    for start, ref in ((k_start, gk_ref), (v_start, gv_ref)):
        ref[:near, :] = start[...]
        ref[near:, :] = jnp.zeros((plan.seg_rows - near, plan.chunk_width), F32)

    def body(i, _):
        start = pl.multiple_of(i * near, near)
        gq, gk, gv = group(start)
        gq_ref[pl.ds(start, near), :] = gq.astype(BF16)
        gk_ref[pl.ds(start, 2 * near), :] += gk
        gv_ref[pl.ds(start, 2 * near), :] += gv
        return 0

    lax.fori_loop(0, plan.groups - 1, body, 0)


def rest_groups(plan, place, held, starts):
    near = plan.near
    outs = [
        shape((plan.seg_rows - near, plan.chunk_width)),
        shape((plan.seg_rows, plan.chunk_width), F32),
        shape((plan.seg_rows, plan.chunk_width), F32),
    ]
    flops = 24 * plan.heads * (plan.seg_rows - near) * near * plan.dim
    kernel = functools.partial(rest_kernel, plan)
    return call(kernel, place, list(held) + list(starts), outs, (), flops)


def finish_kernel(plan, place, gq_first, gq_rest, gk, gv, far, *refs):
    me = place[1]
    out_refs, (grads,) = refs[: plan.devs], refs[plan.devs :]
    near = plan.near
    last = plan.seg_rows - near
    grads[0, :near, :] = gq_first[...]
    grads[0, near:, :] = gq_rest[...]
    for at, ref in enumerate((gk, gv)):
        grads[1 + at, :last, :] = ref[:last, :].astype(BF16)
        for block in range(plan.reach):
            groups = unfolded(far[block, at], plan)
            for part, rows in block_parts(last + block * plan.rows, plan):
                grads[1 + at, rows, :] = (ref[rows, :] + groups[part].astype(F32)).astype(BF16)
    for step, out_ref in enumerate(out_refs):
        rows = pl.ds(pl.multiple_of((me ^ step) * plan.rows, plan.rows), plan.rows)
        for at in range(3):
            out_ref[at] = folded(grads[at, rows, :], plan)


def finish(plan, place, gq_first, gq_rest, gk, gv, far):
    outs = [shape((3,) + plan.piece) for _ in range(plan.devs)]
    scratch = [pltpu.VMEM((3, plan.seg_rows, plan.chunk_width), BF16)]
    arrays = [gq_first, gq_rest, gk, gv, far]
    return call(functools.partial(finish_kernel, plan), place, arrays, outs, scratch)


def local(queries, keys, values):
    rows, width = queries.shape
    plan = Plan(rows, width, lax.axis_size("dev"))
    seg_count = lax.axis_size("seg")
    onward = [(i, i + 1) for i in range(seg_count - 1)]
    backward = [(i + 1, i) for i in range(seg_count - 1)]
    me = lax.axis_index("dev")
    place = jnp.stack([lax.axis_index("seg"), me]).astype(jnp.int32)
    arrays = [queries, keys, values]
    arrays = [queries, keys, values]
    arrived = []
    for c in range(plan.chunks):
        pieces = pack(plan, c, place, arrays)
        arrived.append(exchange(plan, pieces))
    returned = []
    for pieces in arrived:
        halo = jnp.stack(
            [
                lax.select_n((plan.devs - plan.reach + b) ^ me, *[p[1:] for p in pieces])
                for b in range(plan.reach)
            ]
        )
        halo = lax.ppermute(halo, "seg", onward)
        held = teacher(plan, place, pieces)
        gq_first, gk, gv, far = first_group(plan, place, held, halo)
        far = lax.ppermute(far, "seg", backward)
        gq_rest, gk, gv = rest_groups(plan, place, held, (gk, gv))
        pieces = finish(plan, place, gq_first, gq_rest, gk, gv, far)
        returned.append(exchange(plan, pieces))
    return tuple(unpack(plan, place, returned))


def solution(mesh):
    spec = P(("seg", "dev"), None)
    return jax.shard_map(
        local, mesh=mesh, in_specs=(spec,) * 3, out_specs=(spec,) * 3, check_vma=False
    )
```

time: 97.9 us -> 88.6 us (0.905)
  the two profiles are of different devices: /device:TPU:13 before, /device:TPU:12 now
where the time goes in v1:
time: 88.6 us; the launch traced here: 88.3 us
  waiting for transfers between devices  38 us (43%)
  starting transfers between devices  25.8 us (29%)
  Pallas kernels  20.5 us (23%)
  local copies, waits for them, and re-layouts  2.99 us (3%)
    ppermute x12, waiting for transfers between devices, exchange(): got[step] = lax.ppermute(pieces[step], 'dev', pairs)  38 us
    pallas_call x11, Pallas kernels, call(): pl.pallas_call(kernel, out_shape=tuple(outs), in_specs=[SMEM_SPEC] + [spe...  20.5 us
    ppermute x12, starting transfers between devices, exchange(): got[step] = lax.ppermute(pieces[step], 'dev', pairs)  15.3 us
    ppermute x2, starting transfers between devices, local(): far = lax.ppermute(far, 'seg', backward)  6.64 us
    ppermute x2, starting transfers between devices, local(): halo = lax.ppermute(halo, 'seg', onward)  3.84 us
    unnamed x6, local copies, waits for them, and re-layouts  2.99 us
  transfers between devices with their start and end apart: 16, of which 10 were waited for; matrix products, arithmetic and copies ran while one was open for 0% of the time, Pallas kernels for 19%

profile of v1, /device:TPU:12, one launch (start us, length us, event | category | flops | bytes accessed | tf_op | source)
XLA Modules:
  0.0 88.3 jit_solution(13802404362728507655)
XLA Ops:
  0.7 1.0 %copy-done = bf16[128,1536]{1,0:T(8,128)(2,1)S(1)} copy-done((bf16[128,1536]{1,0:T(8,128)(2,1)S(1)}, bf16[128,1536]{1,0:T(8,128)(2,1)}, u32[]{:S(2)}) %copy-start) | copy-done | bytes 393240
  1.7 1.0 %copy-done.1 = bf16[128,1536]{1,0:T(8,128)(2,1)S(1)} copy-done((bf16[128,1536]{1,0:T(8,128)(2,1)S(1)}, bf16[128,1536]{1,0:T(8,128)(2,1)}, u32[]{:S(2)}) %copy-start.1) | copy-done | bytes 393240
  2.7 1.0 %copy-done.2 = bf16[128,1536]{1,0:T(8,128)(2,1)S(1)} copy-done((bf16[128,1536]{1,0:T(8,128)(2,1)S(1)}, bf16[128,1536]{1,0:T(8,128)(2,1)}, u32[]{:S(2)}) %copy-start.2) | copy-done | bytes 393240
  3.7 1.5 %shard_map.63 = (bf16[3,64,384]{2,1,0:T(8,128)(2,1)S(1)}, bf16[3,64,384]{2,1,0:T(8,128)(2,1)S(1)}, bf16[3,64,384]{2,1,0:T(8,128)(2,1)S(1)}, bf16[3,64,384]{2,1,0:T(8,128)(2,1)S(1)}) custom-call(s32[2]{0:T(128)S(1)} %pad_add_fusion.place, bf16[128,1536]{1,0:T(8,128)(2,1)S(1)} %copy-done, bf16[128,1536]{1,0:T(8,128)(2,1)S(1)} %copy-done.1, ...), custom_call_target="tpu_custom_call" | custom-call | bytes 1769472 | tf_op jit(solution)/shard_map/pallas_call | solution.py:29
  5.2 1.6 %collective-permute-start.10 = (bf16[3,64,384]{2,1,0:T(8,128)(2,1)S(1)}, bf16[3,64,384]{2,1,0:T(8,128)(2,1)S(1)}, u32[]{:S(2)}, u32[]{:S(2)}) collective-permute-start(bf16[3,64,384]{2,1,0:T(8,128)(2,1)S(1)} %get-tuple-element.63), channel_id=1, source_target_pairs={{0,3},{1,2},{2,1},{3,0},{4,7},{5,6},{6,5},{7,4},{8,11},{9,10},{10,... | collective-permute-start | bytes 442376 | tf_op jit(solution)/shard_map/ppermute | solution.py:157
  6.9 2.5 %collective-permute-start.8 = (bf16[3,64,384]{2,1,0:T(8,128)(2,1)S(1)}, bf16[3,64,384]{2,1,0:T(8,128)(2,1)S(1)}, u32[]{:S(2)}, u32[]{:S(2)}) collective-permute-start(bf16[3,64,384]{2,1,0:T(8,128)(2,1)S(1)} %get-tuple-element.61), channel_id=1, source_target_pairs={{0,1},{1,0},{2,3},{3,2},{4,5},{5,4},{6,7},{7,6},{8,9},{9,8},{10,11... | collective-permute-start | bytes 442376 | tf_op jit(solution)/shard_map/ppermute | solution.py:157
  9.4 1.4 %shard_map.58 = (bf16[3,64,384]{2,1,0:T(8,128)(2,1)S(1)}, bf16[3,64,384]{2,1,0:T(8,128)(2,1)S(1)}, bf16[3,64,384]{2,1,0:T(8,128)(2,1)S(1)}, bf16[3,64,384]{2,1,0:T(8,128)(2,1)S(1)}) custom-call(s32[2]{0:T(128)S(1)} %pad_add_fusion.place, bf16[128,1536]{1,0:T(8,128)(2,1)S(1)} %copy-done, bf16[128,1536]{1,0:T(8,128)(2,1)S(1)} %copy-done.1, ...), custom_call_target="tpu_custom_call" | custom-call | bytes 1769472 | tf_op jit(solution)/shard_map/pallas_call | solution.py:29
  11.6 2.2 %collective-permute-start.1 = (bf16[3,64,384]{2,1,0:T(8,128)(2,1)S(1)}, bf16[3,64,384]{2,1,0:T(8,128)(2,1)S(1)}, u32[]{:S(2)}, u32[]{:S(2)}) collective-permute-start(bf16[3,64,384]{2,1,0:T(8,128)(2,1)S(1)} %get-tuple-element.43), channel_id=1, source_target_pairs={{0,2},{1,3},{2,0},{3,1},{4,6},{5,7},{6,4},{7,5},{8,10},{9,11},{10,... | collective-permute-start | bytes 442376 | tf_op jit(solution)/shard_map/ppermute | solution.py:157
  13.8 2.2 %collective-permute-done.10.refs_3_ = bf16[3,64,384]{2,1,0:T(8,128)(2,1)S(1)} collective-permute-done((bf16[3,64,384]{2,1,0:T(8,128)(2,1)S(1)}, bf16[3,64,384]{2,1,0:T(8,128)(2,1)S(1)}, u32[]{:S(2)}, u32[]{:S(2)}) %collective-permute-start.10) | collective-permute-done | bytes 147488 | tf_op jit(solution)/shard_map/ppermute | solution.py:157
  16.0 1.0 %collective-permute-start.2 = (bf16[3,64,384]{2,1,0:T(8,128)(2,1)S(1)}, bf16[3,64,384]{2,1,0:T(8,128)(2,1)S(1)}, u32[]{:S(2)}, u32[]{:S(2)}) collective-permute-start(bf16[3,64,384]{2,1,0:T(8,128)(2,1)S(1)} %get-tuple-element.44), channel_id=1, source_target_pairs={{0,3},{1,2},{2,1},{3,0},{4,7},{5,6},{6,5},{7,4},{8,11},{9,10},{10,... | collective-permute-start | bytes 442376 | tf_op jit(solution)/shard_map/ppermute | solution.py:157
  17.2 3.4 %collective-permute-done.9.refs_2_ = bf16[3,64,384]{2,1,0:T(8,128)(2,1)S(1)} collective-permute-done((bf16[3,64,384]{2,1,0:T(8,128)(2,1)S(1)}, bf16[3,64,384]{2,1,0:T(8,128)(2,1)S(1)}, u32[]{:S(2)}, u32[]{:S(2)}) %collective-permute-start.9) | collective-permute-done | bytes 147488 | tf_op jit(solution)/shard_map/ppermute | solution.py:157
  20.7 1.9 %collective-permute-start.11 = (bf16[2,2,64,384]{3,2,1,0:T(8,128)(2,1)S(1)}, bf16[2,2,64,384]{3,2,1,0:T(8,128)(2,1)S(1)}, u32[]{:S(2)}, u32[]{:S(2)}) collective-permute-start(bf16[2,2,64,384]{3,2,1,0:T(8,128)(2,1)S(1)} %pad_maximum_fusion.1), channel_id=1, source_target_pairs={{0,4},{4,8},{8,12},{12,16},{16,20},{20,24},{24,28},{1,5},{5,9},{9,... | collective-permute-start | bytes 589832 | tf_op jit(solution)/shard_map/ppermute | solution.py:398
  22.6 1.0 %collective-permute-done.refs_1_ = bf16[3,64,384]{2,1,0:T(8,128)(2,1)S(1)} collective-permute-done((bf16[3,64,384]{2,1,0:T(8,128)(2,1)S(1)}, bf16[3,64,384]{2,1,0:T(8,128)(2,1)S(1)}, u32[]{:S(2)}, u32[]{:S(2)}) %collective-permute-start) | collective-permute-done | bytes 147488 | tf_op jit(solution)/shard_map/ppermute | solution.py:157
  23.6 6.5 %collective-permute-done.1.refs_2_ = bf16[3,64,384]{2,1,0:T(8,128)(2,1)S(1)} collective-permute-done((bf16[3,64,384]{2,1,0:T(8,128)(2,1)S(1)}, bf16[3,64,384]{2,1,0:T(8,128)(2,1)S(1)}, u32[]{:S(2)}, u32[]{:S(2)}) %collective-permute-start.1) | collective-permute-done | bytes 147488 | tf_op jit(solution)/shard_map/ppermute | solution.py:157
  30.1 2.9 %collective-permute-done.2.refs_3_ = bf16[3,64,384]{2,1,0:T(8,128)(2,1)S(1)} collective-permute-done((bf16[3,64,384]{2,1,0:T(8,128)(2,1)S(1)}, bf16[3,64,384]{2,1,0:T(8,128)(2,1)S(1)}, u32[]{:S(2)}, u32[]{:S(2)}) %collective-permute-start.2) | collective-permute-done | bytes 147488 | tf_op jit(solution)/shard_map/ppermute | solution.py:157
  33.1 1.9 %collective-permute-start.3 = (bf16[2,2,64,384]{3,2,1,0:T(8,128)(2,1)S(1)}, bf16[2,2,64,384]{3,2,1,0:T(8,128)(2,1)S(1)}, u32[]{:S(2)}, u32[]{:S(2)}) collective-permute-start(bf16[2,2,64,384]{3,2,1,0:T(8,128)(2,1)S(1)} %pad_maximum_fusion), channel_id=1, source_target_pairs={{0,4},{4,8},{8,12},{12,16},{16,20},{20,24},{24,28},{1,5},{5,9},{9,... | collective-permute-start | bytes 589832 | tf_op jit(solution)/shard_map/ppermute | solution.py:398
  35.1 1.8 %shard_map.64 = (bf16[512,192]{1,0:T(8,128)(2,1)S(1)}, bf16[2,512,192]{2,1,0:T(8,128)(2,1)S(1)}, bf16[2,512,192]{2,1,0:T(8,128)(2,1)S(1)}, bf16[512,192]{1,0:T(8,128)(2,1)S(1)}) custom-call(s32[2]{0:T(128)S(1)} %pad_add_fusion.place, bf16[3,64,384]{2,1,0:T(8,128)(2,1)S(1)} %get-tuple-element.60.refs_0_, ...), custom_call_target="tpu_custom_call" | custom-call | flops 201326592 | bytes 1769472 | tf_op jit(solution)/shard_map/pallas_call | solution.py:29
  36.9 2.6 %shard_map.65 = (bf16[256,192]{1,0:T(8,128)(2,1)S(1)}, f32[256,192]{1,0:T(8,128)S(1)}, f32[256,192]{1,0:T(8,128)S(1)}, bf16[2,2,64,384]{3,2,1,0:T(8,128)(2,1)S(1)}) custom-call(s32[2]{0:T(128)S(1)} %pad_add_fusion.place, bf16[512,192]{1,0:T(8,128)(2,1)S(1)} %get-tuple-element.64.q_ref, bf16[2,512,192]{2,1,0:T(8,128)(2,1)S(1)} %get-tuple-element.65.k_ref, ...), custom_call_target="tpu_custom_call" | custom-call | flops 301989888 | bytes 2064384 | tf_op jit(solution)/shard_map/pallas_call | solution.py:29
  39.5 4.5 %collective-permute-start.12 = (bf16[2,2,64,384]{3,2,1,0:T(8,128)(2,1)S(1)}, bf16[2,2,64,384]{3,2,1,0:T(8,128)(2,1)S(1)}, u32[]{:S(2)}, u32[]{:S(2)}) collective-permute-start(bf16[2,2,64,384]{3,2,1,0:T(8,128)(2,1)S(1)} %get-tuple-element.74), channel_id=1, source_target_pairs={{4,0},{8,4},{12,8},{16,12},{20,16},{24,20},{28,24},{5,1},{9,5},{13... | collective-permute-start | bytes 589832 | tf_op jit(solution)/shard_map/ppermute | solution.py:401
  44.0 1.8 %shard_map.59 = (bf16[512,192]{1,0:T(8,128)(2,1)S(1)}, bf16[2,512,192]{2,1,0:T(8,128)(2,1)S(1)}, bf16[2,512,192]{2,1,0:T(8,128)(2,1)S(1)}, bf16[512,192]{1,0:T(8,128)(2,1)S(1)}) custom-call(s32[2]{0:T(128)S(1)} %pad_add_fusion.place, bf16[3,64,384]{2,1,0:T(8,128)(2,1)S(1)} %get-tuple-element.41.refs_0_, ...), custom_call_target="tpu_custom_call" | custom-call | flops 201326592 | bytes 1769472 | tf_op jit(solution)/shard_map/pallas_call | solution.py:29
  45.8 2.6 %shard_map.60 = (bf16[256,192]{1,0:T(8,128)(2,1)S(1)}, f32[256,192]{1,0:T(8,128)S(1)}, f32[256,192]{1,0:T(8,128)S(1)}, bf16[2,2,64,384]{3,2,1,0:T(8,128)(2,1)S(1)}) custom-call(s32[2]{0:T(128)S(1)} %pad_add_fusion.place, bf16[512,192]{1,0:T(8,128)(2,1)S(1)} %get-tuple-element.45.q_ref, bf16[2,512,192]{2,1,0:T(8,128)(2,1)S(1)} %get-tuple-element.46.k_ref, ...), custom_call_target="tpu_custom_call" | custom-call | flops 301989888 | bytes 2064384 | tf_op jit(solution)/shard_map/pallas_call | solution.py:29
  48.5 2.1 %collective-permute-start.4 = (bf16[2,2,64,384]{3,2,1,0:T(8,128)(2,1)S(1)}, bf16[2,2,64,384]{3,2,1,0:T(8,128)(2,1)S(1)}, u32[]{:S(2)}, u32[]{:S(2)}) collective-permute-start(bf16[2,2,64,384]{3,2,1,0:T(8,128)(2,1)S(1)} %get-tuple-element.55), channel_id=1, source_target_pairs={{4,0},{8,4},{12,8},{16,12},{20,16},{24,20},{28,24},{5,1},{9,5},{13... | collective-permute-start | bytes 589832 | tf_op jit(solution)/shard_map/ppermute | solution.py:401
  50.6 2.5 %shard_map.66 = (bf16[256,192]{1,0:T(8,128)(2,1)S(1)}, f32[512,192]{1,0:T(8,128)S(1)}, f32[512,192]{1,0:T(8,128)S(1)}) custom-call(s32[2]{0:T(128)S(1)} %pad_add_fusion.place, bf16[512,192]{1,0:T(8,128)(2,1)S(1)} %get-tuple-element.64.q_ref, bf16[2,512,192]{2,1,0:T(8,128)(2,1)S(1)} %get-tuple-element.65.k_ref, ...), custom_call_target="tpu_custom_call" | custom-call | flops 301989888 | bytes 2457600 | tf_op jit(solution)/shard_map/pallas_call | solution.py:29
  54.0 2.5 %shard_map.61 = (bf16[256,192]{1,0:T(8,128)(2,1)S(1)}, f32[512,192]{1,0:T(8,128)S(1)}, f32[512,192]{1,0:T(8,128)S(1)}) custom-call(s32[2]{0:T(128)S(1)} %pad_add_fusion.place, bf16[512,192]{1,0:T(8,128)(2,1)S(1)} %get-tuple-element.45.q_ref, bf16[2,512,192]{2,1,0:T(8,128)(2,1)S(1)} %get-tuple-element.46.k_ref, ...), custom_call_target="tpu_custom_call" | custom-call | flops 301989888 | bytes 2457600 | tf_op jit(solution)/shard_map/pallas_call | solution.py:29
  56.5 3.1 %collective-permute-start.14 = (bf16[3,64,384]{2,1,0:T(8,128)(2,1)S(1)}, bf16[3,64,384]{2,1,0:T(8,128)(2,1)S(1)}, u32[]{:S(2)}, u32[]{:S(2)}) collective-permute-start(bf16[3,64,384]{2,1,0:T(8,128)(2,1)S(1)} %get-tuple-element.77), channel_id=1, source_target_pairs={{0,2},{1,3},{2,0},{3,1},{4,6},{5,7},{6,4},{7,5},{8,10},{9,11},{10,... | collective-permute-start | bytes 442376 | tf_op jit(solution)/shard_map/ppermute | solution.py:157
  60.8 1.1 %collective-permute-start.5 = (bf16[3,64,384]{2,1,0:T(8,128)(2,1)S(1)}, bf16[3,64,384]{2,1,0:T(8,128)(2,1)S(1)}, u32[]{:S(2)}, u32[]{:S(2)}) collective-permute-start(bf16[3,64,384]{2,1,0:T(8,128)(2,1)S(1)} %get-tuple-element.57), channel_id=1, source_target_pairs={{0,1},{1,0},{2,3},{3,2},{4,5},{5,4},{6,7},{7,6},{8,9},{9,8},{10,11... | collective-permute-start | bytes 442376 | tf_op jit(solution)/shard_map/ppermute | solution.py:157
  62.0 1.9 %collective-permute-start.6 = (bf16[3,64,384]{2,1,0:T(8,128)(2,1)S(1)}, bf16[3,64,384]{2,1,0:T(8,128)(2,1)S(1)}, u32[]{:S(2)}, u32[]{:S(2)}) collective-permute-start(bf16[3,64,384]{2,1,0:T(8,128)(2,1)S(1)} %get-tuple-element.58), channel_id=1, source_target_pairs={{0,2},{1,3},{2,0},{3,1},{4,6},{5,7},{6,4},{7,5},{8,10},{9,11},{10,... | collective-permute-start | bytes 442376 | tf_op jit(solution)/shard_map/ppermute | solution.py:157
  64.4 5.1 %collective-permute-done.14.refs_6_ = bf16[3,64,384]{2,1,0:T(8,128)(2,1)S(1)} collective-permute-done((bf16[3,64,384]{2,1,0:T(8,128)(2,1)S(1)}, bf16[3,64,384]{2,1,0:T(8,128)(2,1)S(1)}, u32[]{:S(2)}, u32[]{:S(2)}) %collective-permute-start.14) | collective-permute-done | bytes 147488 | tf_op jit(solution)/shard_map/ppermute | solution.py:157
  69.4 10.7 %collective-permute-done.15.refs_7_ = bf16[3,64,384]{2,1,0:T(8,128)(2,1)S(1)} collective-permute-done((bf16[3,64,384]{2,1,0:T(8,128)(2,1)S(1)}, bf16[3,64,384]{2,1,0:T(8,128)(2,1)S(1)}, u32[]{:S(2)}, u32[]{:S(2)}) %collective-permute-start.15) | collective-permute-done | bytes 147488 | tf_op jit(solution)/shard_map/ppermute | solution.py:157
  80.2 1.7 %collective-permute-done.6.refs_2_ = bf16[3,64,384]{2,1,0:T(8,128)(2,1)S(1)} collective-permute-done((bf16[3,64,384]{2,1,0:T(8,128)(2,1)S(1)}, bf16[3,64,384]{2,1,0:T(8,128)(2,1)S(1)}, u32[]{:S(2)}, u32[]{:S(2)}) %collective-permute-start.6) | collective-permute-done | bytes 147488 | tf_op jit(solution)/shard_map/ppermute | solution.py:157
  81.9 4.2 %collective-permute-done.7.refs_3_ = bf16[3,64,384]{2,1,0:T(8,128)(2,1)S(1)} collective-permute-done((bf16[3,64,384]{2,1,0:T(8,128)(2,1)S(1)}, bf16[3,64,384]{2,1,0:T(8,128)(2,1)S(1)}, u32[]{:S(2)}, u32[]{:S(2)}) %collective-permute-start.7) | collective-permute-done | bytes 147488 | tf_op jit(solution)/shard_map/ppermute | solution.py:157
  86.1 2.2 %shard_map.68 = (bf16[128,1536]{1,0:T(8,128)(2,1)}, bf16[128,1536]{1,0:T(8,128)(2,1)}, bf16[128,1536]{1,0:T(8,128)(2,1)}) custom-call(s32[2]{0:T(128)S(1)} %pad_add_fusion.place, bf16[3,64,384]{2,1,0:T(8,128)(2,1)S(1)} %get-tuple-element.56.refs_0_, bf16[3,64,384]{2,1,0:T(8,128)(2,1)S(1)} %collective-permute-done.5.refs_1_, ...), custom_call_target="tpu_custom_call" | custom-call | bytes 2359296 | tf_op jit(solution)/shard_map/pallas_call | solution.py:29
  (22 shorter events, 3.8 us)
Async XLA Ops:
  0.7 1.0 %copy-start = (bf16[128,1536]{1,0:T(8,128)(2,1)S(1)}, bf16[128,1536]{1,0:T(8,128)(2,1)}, u32[]{:S(2)}) copy-start(bf16[128,1536]{1,0:T(8,128)(2,1)} %refs_0_.3) | copy-start | bytes 1179652
  1.7 1.0 %copy-start.1 = (bf16[128,1536]{1,0:T(8,128)(2,1)S(1)}, bf16[128,1536]{1,0:T(8,128)(2,1)}, u32[]{:S(2)}) copy-start(bf16[128,1536]{1,0:T(8,128)(2,1)} %refs_1_.3) | copy-start | bytes 1179652
  2.7 1.0 %copy-start.2 = (bf16[128,1536]{1,0:T(8,128)(2,1)S(1)}, bf16[128,1536]{1,0:T(8,128)(2,1)}, u32[]{:S(2)}) copy-start(bf16[128,1536]{1,0:T(8,128)(2,1)} %refs_2_.3) | copy-start | bytes 1179652
  5.2 10.8 %collective-permute-start.10 = (bf16[3,64,384]{2,1,0:T(8,128)(2,1)S(1)}, bf16[3,64,384]{2,1,0:T(8,128)(2,1)S(1)}, u32[]{:S(2)}, u32[]{:S(2)}) collective-permute-start(bf16[3,64,384]{2,1,0:T(8,128)(2,1)S(1)} %get-tuple-element.63), channel_id=1, source_target_pairs={{0,3},{1,2},{2,1},{3,0},{4,7},{5,6},{6,5},{7,4},{8,11},{9,10},{10,... | collective-permute-start | bytes 442376 | tf_op jit(solution)/shard_map/ppermute | solution.py:157
  6.9 10.3 %collective-permute-start.8 = (bf16[3,64,384]{2,1,0:T(8,128)(2,1)S(1)}, bf16[3,64,384]{2,1,0:T(8,128)(2,1)S(1)}, u32[]{:S(2)}, u32[]{:S(2)}) collective-permute-start(bf16[3,64,384]{2,1,0:T(8,128)(2,1)S(1)} %get-tuple-element.61), channel_id=1, source_target_pairs={{0,1},{1,0},{2,3},{3,2},{4,5},{5,4},{6,7},{7,6},{8,9},{9,8},{10,11... | collective-permute-start | bytes 442376 | tf_op jit(solution)/shard_map/ppermute | solution.py:157
  9.4 11.2 %collective-permute-start.9 = (bf16[3,64,384]{2,1,0:T(8,128)(2,1)S(1)}, bf16[3,64,384]{2,1,0:T(8,128)(2,1)S(1)}, u32[]{:S(2)}, u32[]{:S(2)}) collective-permute-start(bf16[3,64,384]{2,1,0:T(8,128)(2,1)S(1)} %get-tuple-element.62), channel_id=1, source_target_pairs={{0,2},{1,3},{2,0},{3,1},{4,6},{5,7},{6,4},{7,5},{8,10},{9,11},{10,... | collective-permute-start | bytes 442376 | tf_op jit(solution)/shard_map/ppermute | solution.py:157
  10.8 12.8 %collective-permute-start = (bf16[3,64,384]{2,1,0:T(8,128)(2,1)S(1)}, bf16[3,64,384]{2,1,0:T(8,128)(2,1)S(1)}, u32[]{:S(2)}, u32[]{:S(2)}) collective-permute-start(bf16[3,64,384]{2,1,0:T(8,128)(2,1)S(1)} %get-tuple-element.42), channel_id=1, source_target_pairs={{0,1},{1,0},{2,3},{3,2},{4,5},{5,4},{6,7},{7,6},{8,9},{9,8},{10,11... | collective-permute-start | bytes 442376 | tf_op jit(solution)/shard_map/ppermute | solution.py:157
  11.6 18.5 %collective-permute-start.1 = (bf16[3,64,384]{2,1,0:T(8,128)(2,1)S(1)}, bf16[3,64,384]{2,1,0:T(8,128)(2,1)S(1)}, u32[]{:S(2)}, u32[]{:S(2)}) collective-permute-start(bf16[3,64,384]{2,1,0:T(8,128)(2,1)S(1)} %get-tuple-element.43), channel_id=1, source_target_pairs={{0,2},{1,3},{2,0},{3,1},{4,6},{5,7},{6,4},{7,5},{8,10},{9,11},{10,... | collective-permute-start | bytes 442376 | tf_op jit(solution)/shard_map/ppermute | solution.py:157
  16.0 17.0 %collective-permute-start.2 = (bf16[3,64,384]{2,1,0:T(8,128)(2,1)S(1)}, bf16[3,64,384]{2,1,0:T(8,128)(2,1)S(1)}, u32[]{:S(2)}, u32[]{:S(2)}) collective-permute-start(bf16[3,64,384]{2,1,0:T(8,128)(2,1)S(1)} %get-tuple-element.44), channel_id=1, source_target_pairs={{0,3},{1,2},{2,1},{3,0},{4,7},{5,6},{6,5},{7,4},{8,11},{9,10},{10,... | collective-permute-start | bytes 442376 | tf_op jit(solution)/shard_map/ppermute | solution.py:157
  20.7 16.2 %collective-permute-start.11 = (bf16[2,2,64,384]{3,2,1,0:T(8,128)(2,1)S(1)}, bf16[2,2,64,384]{3,2,1,0:T(8,128)(2,1)S(1)}, u32[]{:S(2)}, u32[]{:S(2)}) collective-permute-start(bf16[2,2,64,384]{3,2,1,0:T(8,128)(2,1)S(1)} %pad_maximum_fusion.1), channel_id=1, source_target_pairs={{0,4},{4,8},{8,12},{12,16},{16,20},{20,24},{24,28},{1,5},{5,9},{9,... | collective-permute-start | bytes 589832 | tf_op jit(solution)/shard_map/ppermute | solution.py:398
  33.1 12.7 %collective-permute-start.3 = (bf16[2,2,64,384]{3,2,1,0:T(8,128)(2,1)S(1)}, bf16[2,2,64,384]{3,2,1,0:T(8,128)(2,1)S(1)}, u32[]{:S(2)}, u32[]{:S(2)}) collective-permute-start(bf16[2,2,64,384]{3,2,1,0:T(8,128)(2,1)S(1)} %pad_maximum_fusion), channel_id=1, source_target_pairs={{0,4},{4,8},{8,12},{12,16},{16,20},{20,24},{24,28},{1,5},{5,9},{9,... | collective-permute-start | bytes 589832 | tf_op jit(solution)/shard_map/ppermute | solution.py:398
  39.5 13.6 %collective-permute-start.12 = (bf16[2,2,64,384]{3,2,1,0:T(8,128)(2,1)S(1)}, bf16[2,2,64,384]{3,2,1,0:T(8,128)(2,1)S(1)}, u32[]{:S(2)}, u32[]{:S(2)}) collective-permute-start(bf16[2,2,64,384]{3,2,1,0:T(8,128)(2,1)S(1)} %get-tuple-element.74), channel_id=1, source_target_pairs={{4,0},{8,4},{12,8},{16,12},{20,16},{24,20},{28,24},{5,1},{9,5},{13... | collective-permute-start | bytes 589832 | tf_op jit(solution)/shard_map/ppermute | solution.py:401
  48.5 11.6 %collective-permute-start.4 = (bf16[2,2,64,384]{3,2,1,0:T(8,128)(2,1)S(1)}, bf16[2,2,64,384]{3,2,1,0:T(8,128)(2,1)S(1)}, u32[]{:S(2)}, u32[]{:S(2)}) collective-permute-start(bf16[2,2,64,384]{3,2,1,0:T(8,128)(2,1)S(1)} %get-tuple-element.55), channel_id=1, source_target_pairs={{4,0},{8,4},{12,8},{16,12},{20,16},{24,20},{28,24},{5,1},{9,5},{13... | collective-permute-start | bytes 589832 | tf_op jit(solution)/shard_map/ppermute | solution.py:401
  53.9 10.0 %collective-permute-start.13 = (bf16[3,64,384]{2,1,0:T(8,128)(2,1)S(1)}, bf16[3,64,384]{2,1,0:T(8,128)(2,1)S(1)}, u32[]{:S(2)}, u32[]{:S(2)}) collective-permute-start(bf16[3,64,384]{2,1,0:T(8,128)(2,1)S(1)} %get-tuple-element.76), channel_id=1, source_target_pairs={{0,1},{1,0},{2,3},{3,2},{4,5},{5,4},{6,7},{7,6},{8,9},{9,8},{10,11... | collective-permute-start | bytes 442376 | tf_op jit(solution)/shard_map/ppermute | solution.py:157
  56.5 13.0 %collective-permute-start.14 = (bf16[3,64,384]{2,1,0:T(8,128)(2,1)S(1)}, bf16[3,64,384]{2,1,0:T(8,128)(2,1)S(1)}, u32[]{:S(2)}, u32[]{:S(2)}) collective-permute-start(bf16[3,64,384]{2,1,0:T(8,128)(2,1)S(1)} %get-tuple-element.77), channel_id=1, source_target_pairs={{0,2},{1,3},{2,0},{3,1},{4,6},{5,7},{6,4},{7,5},{8,10},{9,11},{10,... | collective-permute-start | bytes 442376 | tf_op jit(solution)/shard_map/ppermute | solution.py:157
  59.6 20.6 %collective-permute-start.15 = (bf16[3,64,384]{2,1,0:T(8,128)(2,1)S(1)}, bf16[3,64,384]{2,1,0:T(8,128)(2,1)S(1)}, u32[]{:S(2)}, u32[]{:S(2)}) collective-permute-start(bf16[3,64,384]{2,1,0:T(8,128)(2,1)S(1)} %get-tuple-element.78), channel_id=1, source_target_pairs={{0,3},{1,2},{2,1},{3,0},{4,7},{5,6},{6,5},{7,4},{8,11},{9,10},{10,... | collective-permute-start | bytes 442376 | tf_op jit(solution)/shard_map/ppermute | solution.py:157
  60.8 19.3 %collective-permute-start.5 = (bf16[3,64,384]{2,1,0:T(8,128)(2,1)S(1)}, bf16[3,64,384]{2,1,0:T(8,128)(2,1)S(1)}, u32[]{:S(2)}, u32[]{:S(2)}) collective-permute-start(bf16[3,64,384]{2,1,0:T(8,128)(2,1)S(1)} %get-tuple-element.57), channel_id=1, source_target_pairs={{0,1},{1,0},{2,3},{3,2},{4,5},{5,4},{6,7},{7,6},{8,9},{9,8},{10,11... | collective-permute-start | bytes 442376 | tf_op jit(solution)/shard_map/ppermute | solution.py:157
  62.0 19.9 %collective-permute-start.6 = (bf16[3,64,384]{2,1,0:T(8,128)(2,1)S(1)}, bf16[3,64,384]{2,1,0:T(8,128)(2,1)S(1)}, u32[]{:S(2)}, u32[]{:S(2)}) collective-permute-start(bf16[3,64,384]{2,1,0:T(8,128)(2,1)S(1)} %get-tuple-element.58), channel_id=1, source_target_pairs={{0,2},{1,3},{2,0},{3,1},{4,6},{5,7},{6,4},{7,5},{8,10},{9,11},{10,... | collective-permute-start | bytes 442376 | tf_op jit(solution)/shard_map/ppermute | solution.py:157
  63.9 22.2 %collective-permute-start.7 = (bf16[3,64,384]{2,1,0:T(8,128)(2,1)S(1)}, bf16[3,64,384]{2,1,0:T(8,128)(2,1)S(1)}, u32[]{:S(2)}, u32[]{:S(2)}) collective-permute-start(bf16[3,64,384]{2,1,0:T(8,128)(2,1)S(1)} %get-tuple-element.59), channel_id=1, source_target_pairs={{0,3},{1,2},{2,1},{3,0},{4,7},{5,6},{6,5},{7,4},{8,11},{9,10},{10,... | collective-permute-start | bytes 442376 | tf_op jit(solution)/shard_map/ppermute | solution.py:157

commit v2 on v1

--- a/solution.py
+++ b/solution.py
@@ -12,6 +12,7 @@
 HEADS = 16
 WINDOW = 256
 CHUNKS = 2
+PACK_MIB = 58
 NEGATIVE = -1e30
 LOG2E = math.log2(math.e)
 BF16 = jnp.bfloat16
@@ -23,17 +24,17 @@
 HBM_SPEC = pl.BlockSpec(memory_space=pltpu.HBM)
 
 
-def call(kernel, place, arrays, outs, scratch=(), flops=0, spec=VMEM_SPEC):
+def call(kernel, place, arrays, outs, scratch=(), flops=0, spec=VMEM_SPEC, out_spec=VMEM_SPEC, vmem=48):
     moved = sum(a.size * a.dtype.itemsize for a in arrays)
     moved += sum(math.prod(o.shape) * o.dtype.itemsize for o in outs)
     return pl.pallas_call(
         kernel,
         out_shape=tuple(outs),
         in_specs=[SMEM_SPEC] + [spec] * len(arrays),
-        out_specs=tuple([VMEM_SPEC] * len(outs)),
+        out_specs=tuple([out_spec] * len(outs)),
         scratch_shapes=list(scratch),
         cost_estimate=pl.CostEstimate(flops=flops, bytes_accessed=moved, transcendentals=0),
-        compiler_params=pltpu.CompilerParams(vmem_limit_bytes=48 * 1024 * 1024),
+        compiler_params=pltpu.CompilerParams(vmem_limit_bytes=vmem * 1024 * 1024),
     )(place, *arrays)
 
 
@@ -57,7 +58,6 @@
         self.seg_rows = rows * devs
         self.near = self.reach * rows
         self.groups = self.seg_rows // self.near
-        self.teacher_rows = self.seg_rows if self.seg_rows <= 512 else rows
         self.scale = self.dim ** (-0.5)
 
 
@@ -88,8 +88,7 @@
 
 def pack_kernel(plan, chunk, place, *refs):
     me = place[1]
-    in_refs, out_refs = refs[:3], refs[3 : 3 + plan.devs]
-    held, sems = refs[3 + plan.devs :]
+    in_refs, out_refs, (held, sems) = refs[:3], refs[3:-2], refs[-2:]
     copies = [pltpu.make_async_copy(r, held.at[i], sems.at[i]) for i, r in enumerate(in_refs)]
     for copy in copies:
         copy.start()
@@ -105,12 +104,13 @@
 def pack(plan, chunk, place, arrays):
     if plan.local_width % 128 == 0:
         outs = [shape((3,) + plan.piece) for _ in range(plan.devs)]
+        kernel = functools.partial(pack_kernel, plan, chunk)
         scratch = [
             pltpu.VMEM((3, plan.rows, plan.width), BF16),
             pltpu.SemaphoreType.DMA((3,)),
         ]
-        kernel = functools.partial(pack_kernel, plan, chunk)
-        return call(kernel, place, arrays, outs, scratch, spec=HBM_SPEC)
+        vmem = PACK_MIB if chunk == 0 else 48
+        return call(kernel, place, arrays, outs, scratch, spec=HBM_SPEC, vmem=vmem)
     pieces = []
     for step in range(plan.devs):
         start = (place[1] ^ step) * plan.local_width + chunk * plan.chunk_width
@@ -121,24 +121,33 @@
 
 def unpack_kernel(plan, place, *refs):
     me = place[1]
-    piece_refs, out_refs = refs[:-3], refs[-3:]
-    for step in range(plan.devs):
-        start = pl.multiple_of((me ^ step) * plan.local_width, 128)
-        for at, out_ref in enumerate(out_refs):
-            held = [unfolded(piece_refs[c * plan.devs + step][at], plan) for c in range(plan.chunks)]
+    piece_refs, out_refs, (held, sems) = refs[:-5], refs[-5:-2], refs[-2:]
+    copies = [pltpu.make_async_copy(held.at[i], r, sems.at[i]) for i, r in enumerate(out_refs)]
+    for at in range(3):
+        for step in range(plan.devs):
+            start = pl.multiple_of((me ^ step) * plan.local_width, 128)
+            got = [unfolded(piece_refs[c * plan.devs + step][at], plan) for c in range(plan.chunks)]
             for part in range(plan.fold):
                 rows = slice(part * plan.fold_rows, (part + 1) * plan.fold_rows)
-                x = [groups[part] for groups in held]
-                out_ref[rows, pl.ds(start, plan.local_width)] = (
+                x = [groups[part] for groups in got]
+                held[at, rows, pl.ds(start, plan.local_width)] = (
                     x[0] if plan.chunks == 1 else jnp.concatenate(x, axis=1)
                 )
+        copies[at].start()
+    for copy in copies:
+        copy.wait()
 
 
 def unpack(plan, place, pieces):
     if plan.local_width % 128 == 0:
         flat = [piece for chunk in pieces for piece in chunk]
         outs = [shape((plan.rows, plan.width)) for _ in range(3)]
-        return call(functools.partial(unpack_kernel, plan), place, flat, outs)
+        scratch = [
+            pltpu.VMEM((3, plan.rows, plan.width), BF16),
+            pltpu.SemaphoreType.DMA((3,)),
+        ]
+        kernel = functools.partial(unpack_kernel, plan)
+        return call(kernel, place, flat, outs, scratch, out_spec=HBM_SPEC)
     order = jnp.arange(plan.devs, dtype=jnp.int32) ^ place[1]
     chunks = []
     for chunk in pieces:
@@ -170,111 +179,114 @@
     return jnp.where(own, x, jnp.zeros_like(x))
 
 
+def joined(parts, plan):
+    columns = []
+    for first in range(0, plan.chunk_width, 128):
+        end = min(first + 128, plan.chunk_width)
+        out = None
+        for head in range(plan.heads):
+            if head * plan.dim >= end or (head + 1) * plan.dim <= first:
+                continue
+            x = parts[head][:, first:end]
+            if out is None:
+                out = x
+            else:
+                lane = first + lax.broadcasted_iota(jnp.int32, x.shape, 1)
+                out = jnp.where(lane < head * plan.dim, out, x)
+        columns.append(out)
+    return columns[0] if len(columns) == 1 else jnp.concatenate(columns, axis=1)
+
+
 def block_parts(first, plan):
     for part in range(plan.fold):
         start = first + part * plan.fold_rows
         yield part, pl.ds(pl.multiple_of(start, plan.fold_rows), plan.fold_rows)
 
 
-def teacher_kernel(plan, place, *refs):
-    me = place[1]
-    piece_refs, (q_ref, k_ref, v_ref, target_ref) = refs[: plan.devs], refs[plan.devs :]
-    for step, ref in enumerate(piece_refs):
-        blocks = [unfolded(ref[at], plan) for at in range(3)]
-        for part, rows in block_parts((me ^ step) * plan.rows, plan):
-            q_ref[rows, :] = blocks[0][part]
-            for head in range(plan.heads):
-                k_ref[head, rows, :] = of_head(blocks[1][part], head, plan)
-                v_ref[head, rows, :] = of_head(blocks[2][part], head, plan)
-
-    def one(start, count):
-        rows = pl.ds(start, count)
-        total = None
-        for head in range(plan.heads):
-            scores = dot(q_ref[rows, :], k_ref[head], (1, 1))
-            top = scores.max(-1, keepdims=True)
-            e = jnp.exp2((scores - top) * (plan.scale * LOG2E))
-            out = dot(e.astype(BF16), v_ref[head], (1, 0)) / e.sum(-1, keepdims=True)
-            total = out if total is None else total + out
-        target_ref[rows, :] = total.astype(BF16)
-
-    count = plan.teacher_rows
-    if count == plan.seg_rows:
-        one(0, count)
-    else:
-
-        def body(i, _):
-            one(pl.multiple_of(i * count, count), count)
-            return 0
-
-        lax.fori_loop(0, plan.seg_rows // count, body, 0)
-
-
-def teacher(plan, place, pieces):
-    outs = [
-        shape((plan.seg_rows, plan.chunk_width)),
-        shape((plan.heads, plan.seg_rows, plan.chunk_width)),
-        shape((plan.heads, plan.seg_rows, plan.chunk_width)),
-        shape((plan.seg_rows, plan.chunk_width)),
-    ]
-    flops = 4 * plan.heads * plan.seg_rows * plan.seg_rows * plan.dim
-    return call(functools.partial(teacher_kernel, plan), place, list(pieces), outs, flops=flops)
-
-
-def student_group(plan, q, k, v, target, closed):
-    heads = range(plan.heads)
-    weights, probability = [], []
-    out = None
-    for head in heads:
-        scores = dot(q, k[head], (1, 1))
-        query_at = lax.broadcasted_iota(jnp.int32, scores.shape, 0)
-        key_at = lax.broadcasted_iota(jnp.int32, scores.shape, 1)
-        low = query_at if closed is None else jnp.maximum(query_at, closed)
-        allowed = (key_at >= low) & (key_at <= query_at + plan.near)
-        scores = jnp.where(allowed, scores, NEGATIVE)
+def teacher_rows(plan, q, k, v):
+    parts = []
+    for head in range(plan.heads):
+        scores = dot(of_head(q, head, plan), k, (1, 1))
         top = scores.max(-1, keepdims=True)
         e = jnp.exp2((scores - top) * (plan.scale * LOG2E))
-        p = e * (1.0 / e.sum(-1, keepdims=True))
-        probability.append(p)
-        weights.append(p.astype(BF16))
-        part = dot(weights[head], v[head], (1, 0))
-        out = part if out is None else out + part
-    d_out = (128.0 * (out - target.astype(F32))).astype(BF16)
-    gq = gk = gv = None
+        parts.append(dot(e.astype(BF16), v, (1, 0)) * (1.0 / e.sum(-1, keepdims=True)))
+    return joined(parts, plan).astype(BF16)
+
+
+def student_group(plan, q, k, v, target, open_far):
+    rows, reach, heads = plan.rows, plan.reach, range(plan.heads)
+    at_query = lax.broadcasted_iota(jnp.int32, (rows, rows), 0)
+    at_key = lax.broadcasted_iota(jnp.int32, (rows, rows), 1)
+    late, early = at_key >= at_query, at_key <= at_query
+
+    def seen(i, block, j):
+        mask = None
+        if j == i:
+            mask = late
+        elif j == i + reach:
+            mask = early
+        if open_far is not None and j < reach:
+            mask = jnp.broadcast_to(open_far, (rows, rows)) if mask is None else mask & open_far
+        return block if mask is None else jnp.where(mask, block, NEGATIVE)
+
+    def window(x, i):
+        return x[i * rows : (i + 1) * rows, i * rows : (i + reach + 1) * rows]
+
+    def whole(parts):
+        lines = []
+        for i, x in enumerate(parts):
+            left = [jnp.zeros((rows, i * rows), x.dtype)] if i else []
+            right = [jnp.zeros((rows, (reach - 1 - i) * rows), x.dtype)] if i < reach - 1 else []
+            lines.append(jnp.concatenate(left + [x] + right, axis=1))
+        return lines[0] if reach == 1 else jnp.concatenate(lines, axis=0)
+
+    weights, probability, outs = [], [], []
     for head in heads:
-        d_prob = dot(d_out, v[head], (1, 1))
-        p = probability[head]
-        inner = (p * d_prob).sum(-1, keepdims=True)
-        d_scores = (p * (d_prob - inner) * plan.scale).astype(BF16)
-        parts = (
-            dot(d_scores, k[head], (1, 0)),
-            dot(d_scores, of_head(q, head, plan), (0, 0)),
-            dot(weights[head], of_head(d_out, head, plan), (0, 0)),
-        )
-        gq, gk, gv = parts if gq is None else (gq + parts[0], gk + parts[1], gv + parts[2])
-    return gq, gk, gv
-
-
-def first_kernel(
-    plan, place, q_ref, k_ref, v_ref, target_ref, halo_ref, gq_ref, gk_ref, gv_ref, far_ref, ext
-):
-    near, heads = plan.near, range(plan.heads)
+        scores = dot(of_head(q, head, plan), k, (1, 1))
+        ps = []
+        for i in range(reach):
+            s = window(scores, i)
+            s = [seen(i, s[:, j * rows : (j + 1) * rows], i + j) for j in range(reach + 1)]
+            s = jnp.concatenate(s, axis=1)
+            top = s.max(-1, keepdims=True)
+            e = jnp.exp2((s - top) * (plan.scale * LOG2E))
+            ps.append(e * (1.0 / e.sum(-1, keepdims=True)))
+        probability.append(ps)
+        weights.append(whole([p.astype(BF16) for p in ps]))
+        outs.append(dot(weights[head], v, (1, 0)))
+    d_out = (128.0 * (joined(outs, plan) - target.astype(F32))).astype(BF16)
+    gq, gk, gv = [], [], []
+    for head in heads:
+        d_prob = dot(of_head(d_out, head, plan), v, (1, 1))
+        ds = []
+        for i, p in enumerate(probability[head]):
+            d = window(d_prob, i)
+            inner = (p * d).sum(-1, keepdims=True)
+            ds.append((p * (d - inner) * plan.scale).astype(BF16))
+        d_scores = whole(ds)
+        gq.append(dot(d_scores, k, (1, 0)))
+        gk.append(dot(d_scores, q, (0, 0)))
+        gv.append(dot(weights[head], d_out, (0, 0)))
+    return joined(gq, plan), joined(gk, plan), joined(gv, plan)
+
+
+def first_kernel(plan, place, *refs):
+    me, near = place[1], plan.near
+    piece_refs, halo_ref = refs[: plan.devs], refs[plan.devs]
+    q_ref, k_ref, v_ref, gq_ref, gk_ref, gv_ref, far_ref, ext = refs[plan.devs + 1 :]
+    for step, ref in enumerate(piece_refs):
+        for at, to in enumerate((q_ref, k_ref, v_ref)):
+            groups = unfolded(ref[at], plan)
+            for part, rows in block_parts((me ^ step) * plan.rows, plan):
+                to[rows, :] = groups[part]
+    target = teacher_rows(plan, q_ref[:near, :], k_ref[...], v_ref[...])
     for at, ref in enumerate((k_ref, v_ref)):
         for block in range(plan.reach):
             groups = unfolded(halo_ref[block, at], plan)
             for part, rows in block_parts(block * plan.rows, plan):
-                for head in heads:
-                    ext[at, head, rows, :] = of_head(groups[part], head, plan)
-        for head in heads:
-            ext[at, head, near:, :] = ref[head, :near, :]
-    gq, gk, gv = student_group(
-        plan,
-        q_ref[:near, :],
-        [ext[0, head] for head in heads],
-        [ext[1, head] for head in heads],
-        target_ref[:near, :],
-        jnp.where(place[0] == 0, near, 0),
-    )
+                ext[at, rows, :] = groups[part]
+        ext[at, near:, :] = ref[:near, :]
+    gq, gk, gv = student_group(plan, q_ref[:near, :], ext[0], ext[1], target, place[0] > 0)
     gq_ref[...] = gq.astype(BF16)
     for at, (grad, ref) in enumerate(((gk, gk_ref), (gv, gv_ref))):
         ref[...] = grad[near:]
@@ -283,35 +295,29 @@
             far_ref[block, at] = folded(grad[rows].astype(BF16), plan)
 
 
-def first_group(plan, place, held, halo):
-    near = plan.near
-    outs = [
-        shape((near, plan.chunk_width)),
-        shape((near, plan.chunk_width), F32),
-        shape((near, plan.chunk_width), F32),
+def first_group(plan, place, pieces, halo):
+    near, width = plan.near, plan.chunk_width
+    outs = [shape((plan.seg_rows, width))] * 3 + [
+        shape((near, width)),
+        shape((near, width), F32),
+        shape((near, width), F32),
         shape((plan.reach, 2) + plan.piece),
     ]
-    scratch = [pltpu.VMEM((2, plan.heads, 2 * near, plan.chunk_width), BF16)]
-    flops = 24 * plan.heads * near * near * plan.dim
+    scratch = [pltpu.VMEM((2, 2 * near, width), BF16)]
+    flops = plan.heads * near * plan.dim * (24 * near + 4 * plan.seg_rows)
     kernel = functools.partial(first_kernel, plan)
-    return call(kernel, place, list(held) + [halo], outs, scratch, flops)
-
-
-def rest_kernel(
-    plan, place, q_ref, k_ref, v_ref, target_ref, k_start, v_start, gq_ref, gk_ref, gv_ref
-):
-    near, heads = plan.near, range(plan.heads)
+    out = call(kernel, place, list(pieces) + [halo], outs, scratch, flops)
+    return out[:3], out[3:]
+
+
+def rest_kernel(plan, place, q_ref, k_ref, v_ref, k_start, v_start, gq_ref, gk_ref, gv_ref):
+    near = plan.near
 
     def group(start):
         rows, keys = pl.ds(start + near, near), pl.ds(start, 2 * near)
-        return student_group(
-            plan,
-            q_ref[rows, :],
-            [k_ref[head, keys, :] for head in heads],
-            [v_ref[head, keys, :] for head in heads],
-            target_ref[rows, :],
-            None,
-        )
+        q = q_ref[rows, :]
+        target = teacher_rows(plan, q, k_ref[...], v_ref[...])
+        return student_group(plan, q, k_ref[keys, :], v_ref[keys, :], target, None)
 
     if plan.groups == 2:
         gq, gk, gv = group(0)
@@ -336,13 +342,14 @@
 
 
 def rest_groups(plan, place, held, starts):
-    near = plan.near
+    near, width = plan.near, plan.chunk_width
     outs = [
-        shape((plan.seg_rows - near, plan.chunk_width)),
-        shape((plan.seg_rows, plan.chunk_width), F32),
-        shape((plan.seg_rows, plan.chunk_width), F32),
+        shape((plan.seg_rows - near, width)),
+        shape((plan.seg_rows, width), F32),
+        shape((plan.seg_rows, width), F32),
     ]
-    flops = 24 * plan.heads * (plan.seg_rows - near) * near * plan.dim
+    count = plan.seg_rows - near
+    flops = plan.heads * count * plan.dim * (24 * near + 4 * plan.seg_rows)
     kernel = functools.partial(rest_kernel, plan)
     return call(kernel, place, list(held) + list(starts), outs, (), flops)
 
@@ -396,8 +403,7 @@
             ]
         )
         halo = lax.ppermute(halo, "seg", onward)
-        held = teacher(plan, place, pieces)
-        gq_first, gk, gv, far = first_group(plan, place, held, halo)
+        held, (gq_first, gk, gv, far) = first_group(plan, place, pieces, halo)
         far = lax.ppermute(far, "seg", backward)
         gq_rest, gk, gv = rest_groups(plan, place, held, (gk, gv))
         pieces = finish(plan, place, gq_first, gq_rest, gk, gv, far)

time: 88.6 us -> 85.7 us (0.967)
  the two profiles are of different devices: /device:TPU:12 before, /device:TPU:21 now
where the time goes in v2:
time: 85.7 us; the launch traced here: 85.4 us
  waiting for transfers between devices  34.8 us (41%)
  starting transfers between devices  27.3 us (32%)
  Pallas kernels  19.2 us (22%)
  local copies, waits for them, and re-layouts  3 us (4%)
    ppermute x12, waiting for transfers between devices, exchange(): got[step] = lax.ppermute(pieces[step], 'dev', pairs)  34.8 us
    pallas_call x9, Pallas kernels, call(): pl.pallas_call(kernel, out_shape=tuple(outs), in_specs=[SMEM_SPEC] + [spe...  19.2 us
    ppermute x12, starting transfers between devices, exchange(): got[step] = lax.ppermute(pieces[step], 'dev', pairs)  11.7 us
    ppermute x2, starting transfers between devices, local(): halo = lax.ppermute(halo, 'seg', onward)  10.2 us
    ppermute x2, starting transfers between devices, local(): far = lax.ppermute(far, 'seg', backward)  5.36 us
    unnamed x12, local copies, waits for them, and re-layouts  3 us
  transfers between devices with their start and end apart: 16, of which 7 were waited for; matrix products, arithmetic and copies ran while one was open for 0% of the time, Pallas kernels for 18%

profile of v2, /device:TPU:21, one launch (start us, length us, event | category | flops | bytes accessed | tf_op | source)
XLA Modules:
  0.0 85.4 jit_solution(12418212363371875755)
XLA Ops:
  0.7 1.0 %copy-done = bf16[128,1536]{1,0:T(8,128)(2,1)S(1)} copy-done((bf16[128,1536]{1,0:T(8,128)(2,1)S(1)}, bf16[128,1536]{1,0:T(8,128)(2,1)}, u32[]{:S(2)}) %copy-start) | copy-done | bytes 393240
  1.7 1.0 %copy-done.1 = bf16[128,1536]{1,0:T(8,128)(2,1)S(1)} copy-done((bf16[128,1536]{1,0:T(8,128)(2,1)S(1)}, bf16[128,1536]{1,0:T(8,128)(2,1)}, u32[]{:S(2)}) %copy-start.1) | copy-done | bytes 393240
  2.7 1.0 %copy-done.2 = bf16[128,1536]{1,0:T(8,128)(2,1)S(1)} copy-done((bf16[128,1536]{1,0:T(8,128)(2,1)S(1)}, bf16[128,1536]{1,0:T(8,128)(2,1)}, u32[]{:S(2)}) %copy-start.2) | copy-done | bytes 393240
  3.7 1.5 %shard_map.62 = (bf16[3,64,384]{2,1,0:T(8,128)(2,1)S(1)}, bf16[3,64,384]{2,1,0:T(8,128)(2,1)S(1)}, bf16[3,64,384]{2,1,0:T(8,128)(2,1)S(1)}, bf16[3,64,384]{2,1,0:T(8,128)(2,1)S(1)}) custom-call(s32[2]{0:T(128)S(1)} %pad_add_fusion.place, bf16[128,1536]{1,0:T(8,128)(2,1)S(1)} %copy-done, bf16[128,1536]{1,0:T(8,128)(2,1)S(1)} %copy-done.1, ...), custom_call_target="tpu_custom_call" | custom-call | bytes 1769472 | tf_op jit(solution)/shard_map/pallas_call | solution.py:30
  5.5 1.2 %collective-permute-start.8 = (bf16[3,64,384]{2,1,0:T(8,128)(2,1)S(1)}, bf16[3,64,384]{2,1,0:T(8,128)(2,1)S(1)}, u32[]{:S(2)}, u32[]{:S(2)}) collective-permute-start(bf16[3,64,384]{2,1,0:T(8,128)(2,1)S(1)} %get-tuple-element.58), channel_id=1, source_target_pairs={{0,1},{1,0},{2,3},{3,2},{4,5},{5,4},{6,7},{7,6},{8,9},{9,8},{10,11... | collective-permute-start | bytes 442376 | tf_op jit(solution)/shard_map/ppermute | solution.py:166
  6.7 2.0 %collective-permute-start.9 = (bf16[3,64,384]{2,1,0:T(8,128)(2,1)S(1)}, bf16[3,64,384]{2,1,0:T(8,128)(2,1)S(1)}, u32[]{:S(2)}, u32[]{:S(2)}) collective-permute-start(bf16[3,64,384]{2,1,0:T(8,128)(2,1)S(1)} %get-tuple-element.59), channel_id=1, source_target_pairs={{0,2},{1,3},{2,0},{3,1},{4,6},{5,7},{6,4},{7,5},{8,10},{9,11},{10,... | collective-permute-start | bytes 442376 | tf_op jit(solution)/shard_map/ppermute | solution.py:166
  8.7 2.8 %shard_map.58 = (bf16[3,64,384]{2,1,0:T(8,128)(2,1)}, bf16[3,64,384]{2,1,0:T(8,128)(2,1)}, bf16[3,64,384]{2,1,0:T(8,128)(2,1)}, bf16[3,64,384]{2,1,0:T(8,128)(2,1)}) custom-call(s32[2]{0:T(128)} %copy-done.4, bf16[128,1536]{1,0:T(8,128)(2,1)} %refs_0_.3, bf16[128,1536]{1,0:T(8,128)(2,1)} %refs_1_.3, bf16[128,1536]{1,0:T(8,128)(2,1)} %refs_2_.3), custom_call_target="tpu_custom_call" | custom-call | bytes 1769472 | tf_op jit(solution)/shard_map/pallas_call | solution.py:30
  11.5 1.5 %collective-permute-start = (bf16[3,64,384]{2,1,0:T(8,128)(2,1)}, bf16[3,64,384]{2,1,0:T(8,128)(2,1)S(1)}, u32[]{:S(2)}, u32[]{:S(2)}) collective-permute-start(bf16[3,64,384]{2,1,0:T(8,128)(2,1)} %get-tuple-element.40), channel_id=1, source_target_pairs={{0,1},{1,0},{2,3},{3,2},{4,5},{5,4},{6,7},{7,6},{8,9},{9,8},{10,11... | collective-permute-start | bytes 442376 | tf_op jit(solution)/shard_map/ppermute | solution.py:166
  13.1 1.3 %collective-permute-start.2 = (bf16[3,64,384]{2,1,0:T(8,128)(2,1)}, bf16[3,64,384]{2,1,0:T(8,128)(2,1)S(1)}, u32[]{:S(2)}, u32[]{:S(2)}) collective-permute-start(bf16[3,64,384]{2,1,0:T(8,128)(2,1)} %get-tuple-element.42), channel_id=1, source_target_pairs={{0,3},{1,2},{2,1},{3,0},{4,7},{5,6},{6,5},{7,4},{8,11},{9,10},{10,... | collective-permute-start | bytes 442376 | tf_op jit(solution)/shard_map/ppermute | solution.py:166
  14.3 4.1 %collective-permute-done.9.refs_2_ = bf16[3,64,384]{2,1,0:T(8,128)(2,1)S(1)} collective-permute-done((bf16[3,64,384]{2,1,0:T(8,128)(2,1)S(1)}, bf16[3,64,384]{2,1,0:T(8,128)(2,1)S(1)}, u32[]{:S(2)}, u32[]{:S(2)}) %collective-permute-start.9) | collective-permute-done | bytes 147488 | tf_op jit(solution)/shard_map/ppermute | solution.py:166
  18.5 5.7 %collective-permute-start.11 = (bf16[2,2,64,384]{3,2,1,0:T(8,128)(2,1)S(1)}, bf16[2,2,64,384]{3,2,1,0:T(8,128)(2,1)S(1)}, u32[]{:S(2)}, u32[]{:S(2)}) collective-permute-start(bf16[2,2,64,384]{3,2,1,0:T(8,128)(2,1)S(1)} %pad_maximum_fusion.1), channel_id=1, source_target_pairs={{0,4},{4,8},{8,12},{12,16},{16,20},{20,24},{24,28},{1,5},{5,9},{9,... | collective-permute-start | bytes 589832 | tf_op jit(solution)/shard_map/ppermute | solution.py:405
  24.2 3.1 %collective-permute-done.1.refs_2_ = bf16[3,64,384]{2,1,0:T(8,128)(2,1)S(1)} collective-permute-done((bf16[3,64,384]{2,1,0:T(8,128)(2,1)}, bf16[3,64,384]{2,1,0:T(8,128)(2,1)S(1)}, u32[]{:S(2)}, u32[]{:S(2)}) %collective-permute-start.1) | collective-permute-done | bytes 147488 | tf_op jit(solution)/shard_map/ppermute | solution.py:166
  27.3 4.9 %collective-permute-done.2.refs_3_ = bf16[3,64,384]{2,1,0:T(8,128)(2,1)S(1)} collective-permute-done((bf16[3,64,384]{2,1,0:T(8,128)(2,1)}, bf16[3,64,384]{2,1,0:T(8,128)(2,1)S(1)}, u32[]{:S(2)}, u32[]{:S(2)}) %collective-permute-start.2) | collective-permute-done | bytes 147488 | tf_op jit(solution)/shard_map/ppermute | solution.py:166
  32.3 4.5 %collective-permute-start.3 = (bf16[2,2,64,384]{3,2,1,0:T(8,128)(2,1)S(1)}, bf16[2,2,64,384]{3,2,1,0:T(8,128)(2,1)S(1)}, u32[]{:S(2)}, u32[]{:S(2)}) collective-permute-start(bf16[2,2,64,384]{3,2,1,0:T(8,128)(2,1)S(1)} %pad_maximum_fusion), channel_id=1, source_target_pairs={{0,4},{4,8},{8,12},{12,16},{16,20},{20,24},{24,28},{1,5},{5,9},{9,... | collective-permute-start | bytes 589832 | tf_op jit(solution)/shard_map/ppermute | solution.py:405
  36.9 3.0 %shard_map.63 = (bf16[512,192]{1,0:T(8,128)(2,1)S(1)}, bf16[512,192]{1,0:T(8,128)(2,1)S(1)}, bf16[512,192]{1,0:T(8,128)(2,1)S(1)}, bf16[256,192]{1,0:T(8,128)(2,...) custom-call(s32[2]{0:T(128)S(1)} %copy-done.5, ...), custom_call_target="tpu_custom_call" | custom-call | flops 402653184 | bytes 2064384 | tf_op jit(solution)/shard_map/pallas_call | solution.py:30
  39.8 1.9 %collective-permute-start.12 = (bf16[2,2,64,384]{3,2,1,0:T(8,128)(2,1)S(1)}, bf16[2,2,64,384]{3,2,1,0:T(8,128)(2,1)S(1)}, u32[]{:S(2)}, u32[]{:S(2)}) collective-permute-start(bf16[2,2,64,384]{3,2,1,0:T(8,128)(2,1)S(1)} %get-tuple-element.70), channel_id=1, source_target_pairs={{4,0},{8,4},{12,8},{16,12},{20,16},{24,20},{28,24},{5,1},{9,5},{13... | collective-permute-start | bytes 589832 | tf_op jit(solution)/shard_map/ppermute | solution.py:407
  41.8 3.0 %shard_map.59 = (bf16[512,192]{1,0:T(8,128)(2,1)S(1)}, bf16[512,192]{1,0:T(8,128)(2,1)S(1)}, bf16[512,192]{1,0:T(8,128)(2,1)S(1)}, bf16[256,192]{1,0:T(8,128)(2,...) custom-call(s32[2]{0:T(128)S(1)} %copy-done.5, ...), custom_call_target="tpu_custom_call" | custom-call | flops 402653184 | bytes 2064384 | tf_op jit(solution)/shard_map/pallas_call | solution.py:30
  44.8 3.4 %collective-permute-start.4 = (bf16[2,2,64,384]{3,2,1,0:T(8,128)(2,1)S(1)}, bf16[2,2,64,384]{3,2,1,0:T(8,128)(2,1)S(1)}, u32[]{:S(2)}, u32[]{:S(2)}) collective-permute-start(bf16[2,2,64,384]{3,2,1,0:T(8,128)(2,1)S(1)} %get-tuple-element.52), channel_id=1, source_target_pairs={{4,0},{8,4},{12,8},{16,12},{20,16},{24,20},{28,24},{5,1},{9,5},{13... | collective-permute-start | bytes 589832 | tf_op jit(solution)/shard_map/ppermute | solution.py:407
  48.2 2.7 %shard_map.64 = (bf16[256,192]{1,0:T(8,128)(2,1)S(1)}, f32[512,192]{1,0:T(8,128)S(1)}, f32[512,192]{1,0:T(8,128)S(1)}) custom-call(s32[2]{0:T(128)S(1)} %copy-done.5, bf16[512,192]{1,0:T(8,128)(2,1)S(1)} %get-tuple-element.62.q_ref, bf16[512,192]{1,0:T(8,128)(2,1)S(1)} %get-tuple-element.63.k_ref, bf16[512,192]{1,0:T(8,128)(2,1)S(1)} %get-tuple-element.64.v_ref, ...), custom_call_target="tpu_custom_call" | custom-call | flops 402653184 | bytes 1867776 | tf_op jit(solution)/shard_map/pallas_call | solution.py:30
  50.9 0.8 shard_map.65
  51.7 2.7 %shard_map.60 = (bf16[256,192]{1,0:T(8,128)(2,1)S(1)}, f32[512,192]{1,0:T(8,128)S(1)}, f32[512,192]{1,0:T(8,128)S(1)}) custom-call(s32[2]{0:T(128)S(1)} %copy-done.5, bf16[512,192]{1,0:T(8,128)(2,1)S(1)} %get-tuple-element.44.q_ref, bf16[512,192]{1,0:T(8,128)(2,1)S(1)} %get-tuple-element.45.k_ref, bf16[512,192]{1,0:T(8,128)(2,1)S(1)} %get-tuple-element.46.v_ref, ...), custom_call_target="tpu_custom_call" | custom-call | flops 402653184 | bytes 1867776 | tf_op jit(solution)/shard_map/pallas_call | solution.py:30
  54.4 1.4 %collective-permute-start.14 = (bf16[3,64,384]{2,1,0:T(8,128)(2,1)S(1)}, bf16[3,64,384]{2,1,0:T(8,128)(2,1)S(1)}, u32[]{:S(2)}, u32[]{:S(2)}) collective-permute-start(bf16[3,64,384]{2,1,0:T(8,128)(2,1)S(1)} %get-tuple-element.73), channel_id=1, source_target_pairs={{0,2},{1,3},{2,0},{3,1},{4,6},{5,7},{6,4},{7,5},{8,10},{9,11},{10,... | collective-permute-start | bytes 442376 | tf_op jit(solution)/shard_map/ppermute | solution.py:166
  55.8 1.3 %collective-permute-start.15 = (bf16[3,64,384]{2,1,0:T(8,128)(2,1)S(1)}, bf16[3,64,384]{2,1,0:T(8,128)(2,1)S(1)}, u32[]{:S(2)}, u32[]{:S(2)}) collective-permute-start(bf16[3,64,384]{2,1,0:T(8,128)(2,1)S(1)} %get-tuple-element.74), channel_id=1, source_target_pairs={{0,3},{1,2},{2,1},{3,0},{4,7},{5,6},{6,5},{7,4},{8,11},{9,10},{10,... | collective-permute-start | bytes 442376 | tf_op jit(solution)/shard_map/ppermute | solution.py:166
  57.1 0.8 shard_map.61
  57.9 1.0 %collective-permute-start.5 = (bf16[3,64,384]{2,1,0:T(8,128)(2,1)S(1)}, bf16[3,64,384]{2,1,0:T(8,128)(2,1)S(1)}, u32[]{:S(2)}, u32[]{:S(2)}) collective-permute-start(bf16[3,64,384]{2,1,0:T(8,128)(2,1)S(1)} %get-tuple-element.54), channel_id=1, source_target_pairs={{0,1},{1,0},{2,3},{3,2},{4,5},{5,4},{6,7},{7,6},{8,9},{9,8},{10,11... | collective-permute-start | bytes 442376 | tf_op jit(solution)/shard_map/ppermute | solution.py:166
  58.9 0.4 collective-permute-start.6
  59.3 1.3 %collective-permute-start.7 = (bf16[3,64,384]{2,1,0:T(8,128)(2,1)S(1)}, bf16[3,64,384]{2,1,0:T(8,128)(2,1)S(1)}, u32[]{:S(2)}, u32[]{:S(2)}) collective-permute-start(bf16[3,64,384]{2,1,0:T(8,128)(2,1)S(1)} %get-tuple-element.56), channel_id=1, source_target_pairs={{0,3},{1,2},{2,1},{3,0},{4,7},{5,6},{6,5},{7,4},{8,11},{9,10},{10,... | collective-permute-start | bytes 442376 | tf_op jit(solution)/shard_map/ppermute | solution.py:166
  60.6 4.8 %collective-permute-done.14.refs_6_ = bf16[3,64,384]{2,1,0:T(8,128)(2,1)S(1)} collective-permute-done((bf16[3,64,384]{2,1,0:T(8,128)(2,1)S(1)}, bf16[3,64,384]{2,1,0:T(8,128)(2,1)S(1)}, u32[]{:S(2)}, u32[]{:S(2)}) %collective-permute-start.14) | collective-permute-done | bytes 147488 | tf_op jit(solution)/shard_map/ppermute | solution.py:166
  65.4 11.7 %collective-permute-done.15.refs_7_ = bf16[3,64,384]{2,1,0:T(8,128)(2,1)S(1)} collective-permute-done((bf16[3,64,384]{2,1,0:T(8,128)(2,1)S(1)}, bf16[3,64,384]{2,1,0:T(8,128)(2,1)S(1)}, u32[]{:S(2)}, u32[]{:S(2)}) %collective-permute-start.15) | collective-permute-done | bytes 147488 | tf_op jit(solution)/shard_map/ppermute | solution.py:166
  77.0 1.0 %collective-permute-done.6.refs_2_ = bf16[3,64,384]{2,1,0:T(8,128)(2,1)S(1)} collective-permute-done((bf16[3,64,384]{2,1,0:T(8,128)(2,1)S(1)}, bf16[3,64,384]{2,1,0:T(8,128)(2,1)S(1)}, u32[]{:S(2)}, u32[]{:S(2)}) %collective-permute-start.6) | collective-permute-done | bytes 147488 | tf_op jit(solution)/shard_map/ppermute | solution.py:166
  78.0 5.3 %collective-permute-done.7.refs_3_ = bf16[3,64,384]{2,1,0:T(8,128)(2,1)S(1)} collective-permute-done((bf16[3,64,384]{2,1,0:T(8,128)(2,1)S(1)}, bf16[3,64,384]{2,1,0:T(8,128)(2,1)S(1)}, u32[]{:S(2)}, u32[]{:S(2)}) %collective-permute-start.7) | collective-permute-done | bytes 147488 | tf_op jit(solution)/shard_map/ppermute | solution.py:166
  83.3 2.0 %shard_map.66 = (bf16[128,1536]{1,0:T(8,128)(2,1)}, bf16[128,1536]{1,0:T(8,128)(2,1)}, bf16[128,1536]{1,0:T(8,128)(2,1)}) custom-call(s32[2]{0:T(128)S(1)} %copy-done.5, bf16[3,64,384]{2,1,0:T(8,128)(2,1)S(1)} %get-tuple-element.53.refs_0_, bf16[3,64,384]{2,1,0:T(8,128)(2,1)S(1)} %collective-permute-done.5.refs_1_, ...), custom_call_target="tpu_custom_call" | custom-call | bytes 2359296 | tf_op jit(solution)/shard_map/pallas_call | solution.py:30
  (26 shorter events, 0.6 us)
Async XLA Ops:
  0.7 1.0 %copy-start = (bf16[128,1536]{1,0:T(8,128)(2,1)S(1)}, bf16[128,1536]{1,0:T(8,128)(2,1)}, u32[]{:S(2)}) copy-start(bf16[128,1536]{1,0:T(8,128)(2,1)} %refs_0_.3) | copy-start | bytes 1179652
  1.7 1.0 %copy-start.1 = (bf16[128,1536]{1,0:T(8,128)(2,1)S(1)}, bf16[128,1536]{1,0:T(8,128)(2,1)}, u32[]{:S(2)}) copy-start(bf16[128,1536]{1,0:T(8,128)(2,1)} %refs_1_.3) | copy-start | bytes 1179652
  2.7 1.0 %copy-start.2 = (bf16[128,1536]{1,0:T(8,128)(2,1)S(1)}, bf16[128,1536]{1,0:T(8,128)(2,1)}, u32[]{:S(2)}) copy-start(bf16[128,1536]{1,0:T(8,128)(2,1)} %refs_2_.3) | copy-start | bytes 1179652
  3.7 1.6 %copy-start.4 = (s32[2]{0:T(128)}, s32[2]{0:T(128)S(1)}, u32[]{:S(2)}) copy-start(s32[2]{0:T(128)S(1)} %pad_add_fusion.place) | copy-start | bytes 28
  5.3 7.8 %collective-permute-start.10 = (bf16[3,64,384]{2,1,0:T(8,128)(2,1)S(1)}, bf16[3,64,384]{2,1,0:T(8,128)(2,1)S(1)}, u32[]{:S(2)}, u32[]{:S(2)}) collective-permute-start(bf16[3,64,384]{2,1,0:T(8,128)(2,1)S(1)} %get-tuple-element.60), channel_id=1, source_target_pairs={{0,3},{1,2},{2,1},{3,0},{4,7},{5,6},{6,5},{7,4},{8,11},{9,10},{10,... | collective-permute-start | bytes 442376 | tf_op jit(solution)/shard_map/ppermute | solution.py:166
  5.5 8.8 %collective-permute-start.8 = (bf16[3,64,384]{2,1,0:T(8,128)(2,1)S(1)}, bf16[3,64,384]{2,1,0:T(8,128)(2,1)S(1)}, u32[]{:S(2)}, u32[]{:S(2)}) collective-permute-start(bf16[3,64,384]{2,1,0:T(8,128)(2,1)S(1)} %get-tuple-element.58), channel_id=1, source_target_pairs={{0,1},{1,0},{2,3},{3,2},{4,5},{5,4},{6,7},{7,6},{8,9},{9,8},{10,11... | collective-permute-start | bytes 442376 | tf_op jit(solution)/shard_map/ppermute | solution.py:166
  6.7 11.7 %collective-permute-start.9 = (bf16[3,64,384]{2,1,0:T(8,128)(2,1)S(1)}, bf16[3,64,384]{2,1,0:T(8,128)(2,1)S(1)}, u32[]{:S(2)}, u32[]{:S(2)}) collective-permute-start(bf16[3,64,384]{2,1,0:T(8,128)(2,1)S(1)} %get-tuple-element.59), channel_id=1, source_target_pairs={{0,2},{1,3},{2,0},{3,1},{4,6},{5,7},{6,4},{7,5},{8,10},{9,11},{10,... | collective-permute-start | bytes 442376 | tf_op jit(solution)/shard_map/ppermute | solution.py:166
  11.5 12.7 %collective-permute-start = (bf16[3,64,384]{2,1,0:T(8,128)(2,1)}, bf16[3,64,384]{2,1,0:T(8,128)(2,1)S(1)}, u32[]{:S(2)}, u32[]{:S(2)}) collective-permute-start(bf16[3,64,384]{2,1,0:T(8,128)(2,1)} %get-tuple-element.40), channel_id=1, source_target_pairs={{0,1},{1,0},{2,3},{3,2},{4,5},{5,4},{6,7},{7,6},{8,9},{9,8},{10,11... | collective-permute-start | bytes 442376 | tf_op jit(solution)/shard_map/ppermute | solution.py:166
  13.1 14.3 %collective-permute-start.1 = (bf16[3,64,384]{2,1,0:T(8,128)(2,1)}, bf16[3,64,384]{2,1,0:T(8,128)(2,1)S(1)}, u32[]{:S(2)}, u32[]{:S(2)}) collective-permute-start(bf16[3,64,384]{2,1,0:T(8,128)(2,1)} %get-tuple-element.41), channel_id=1, source_target_pairs={{0,2},{1,3},{2,0},{3,1},{4,6},{5,7},{6,4},{7,5},{8,10},{9,11},{10,... | collective-permute-start | bytes 442376 | tf_op jit(solution)/shard_map/ppermute | solution.py:166
  13.1 19.1 %collective-permute-start.2 = (bf16[3,64,384]{2,1,0:T(8,128)(2,1)}, bf16[3,64,384]{2,1,0:T(8,128)(2,1)S(1)}, u32[]{:S(2)}, u32[]{:S(2)}) collective-permute-start(bf16[3,64,384]{2,1,0:T(8,128)(2,1)} %get-tuple-element.42), channel_id=1, source_target_pairs={{0,3},{1,2},{2,1},{3,0},{4,7},{5,6},{6,5},{7,4},{8,11},{9,10},{10,... | collective-permute-start | bytes 442376 | tf_op jit(solution)/shard_map/ppermute | solution.py:166
  18.5 13.7 %copy-start.3 = (bf16[3,64,384]{2,1,0:T(8,128)(2,1)S(1)}, bf16[3,64,384]{2,1,0:T(8,128)(2,1)}, u32[]{:S(2)}) copy-start(bf16[3,64,384]{2,1,0:T(8,128)(2,1)} %get-tuple-element.39.refs_0_) | copy-start | bytes 442372
  18.5 18.3 %collective-permute-start.11 = (bf16[2,2,64,384]{3,2,1,0:T(8,128)(2,1)S(1)}, bf16[2,2,64,384]{3,2,1,0:T(8,128)(2,1)S(1)}, u32[]{:S(2)}, u32[]{:S(2)}) collective-permute-start(bf16[2,2,64,384]{3,2,1,0:T(8,128)(2,1)S(1)} %pad_maximum_fusion.1), channel_id=1, source_target_pairs={{0,4},{4,8},{8,12},{12,16},{16,20},{20,24},{24,28},{1,5},{5,9},{9,... | collective-permute-start | bytes 589832 | tf_op jit(solution)/shard_map/ppermute | solution.py:405
  32.3 4.6 %copy-start.5 = (s32[2]{0:T(128)S(1)}, s32[2]{0:T(128)}, u32[]{:S(2)}) copy-start(s32[2]{0:T(128)} %copy-done.4) | copy-start | bytes 28
  32.3 9.5 %collective-permute-start.3 = (bf16[2,2,64,384]{3,2,1,0:T(8,128)(2,1)S(1)}, bf16[2,2,64,384]{3,2,1,0:T(8,128)(2,1)S(1)}, u32[]{:S(2)}, u32[]{:S(2)}) collective-permute-start(bf16[2,2,64,384]{3,2,1,0:T(8,128)(2,1)S(1)} %pad_maximum_fusion), channel_id=1, source_target_pairs={{0,4},{4,8},{8,12},{12,16},{16,20},{20,24},{24,28},{1,5},{5,9},{9,... | collective-permute-start | bytes 589832 | tf_op jit(solution)/shard_map/ppermute | solution.py:405
  39.8 11.0 %collective-permute-start.12 = (bf16[2,2,64,384]{3,2,1,0:T(8,128)(2,1)S(1)}, bf16[2,2,64,384]{3,2,1,0:T(8,128)(2,1)S(1)}, u32[]{:S(2)}, u32[]{:S(2)}) collective-permute-start(bf16[2,2,64,384]{3,2,1,0:T(8,128)(2,1)S(1)} %get-tuple-element.70), channel_id=1, source_target_pairs={{4,0},{8,4},{12,8},{16,12},{20,16},{24,20},{28,24},{5,1},{9,5},{13... | collective-permute-start | bytes 589832 | tf_op jit(solution)/shard_map/ppermute | solution.py:407
  44.8 12.3 %collective-permute-start.4 = (bf16[2,2,64,384]{3,2,1,0:T(8,128)(2,1)S(1)}, bf16[2,2,64,384]{3,2,1,0:T(8,128)(2,1)S(1)}, u32[]{:S(2)}, u32[]{:S(2)}) collective-permute-start(bf16[2,2,64,384]{3,2,1,0:T(8,128)(2,1)S(1)} %get-tuple-element.52), channel_id=1, source_target_pairs={{4,0},{8,4},{12,8},{16,12},{20,16},{24,20},{28,24},{5,1},{9,5},{13... | collective-permute-start | bytes 589832 | tf_op jit(solution)/shard_map/ppermute | solution.py:407
  51.7 7.6 %collective-permute-start.13 = (bf16[3,64,384]{2,1,0:T(8,128)(2,1)S(1)}, bf16[3,64,384]{2,1,0:T(8,128)(2,1)S(1)}, u32[]{:S(2)}, u32[]{:S(2)}) collective-permute-start(bf16[3,64,384]{2,1,0:T(8,128)(2,1)S(1)} %get-tuple-element.72), channel_id=1, source_target_pairs={{0,1},{1,0},{2,3},{3,2},{4,5},{5,4},{6,7},{7,6},{8,9},{9,8},{10,11... | collective-permute-start | bytes 442376 | tf_op jit(solution)/shard_map/ppermute | solution.py:166
  54.4 10.9 %collective-permute-start.14 = (bf16[3,64,384]{2,1,0:T(8,128)(2,1)S(1)}, bf16[3,64,384]{2,1,0:T(8,128)(2,1)S(1)}, u32[]{:S(2)}, u32[]{:S(2)}) collective-permute-start(bf16[3,64,384]{2,1,0:T(8,128)(2,1)S(1)} %get-tuple-element.73), channel_id=1, source_target_pairs={{0,2},{1,3},{2,0},{3,1},{4,6},{5,7},{6,4},{7,5},{8,10},{9,11},{10,... | collective-permute-start | bytes 442376 | tf_op jit(solution)/shard_map/ppermute | solution.py:166
  55.8 21.2 %collective-permute-start.15 = (bf16[3,64,384]{2,1,0:T(8,128)(2,1)S(1)}, bf16[3,64,384]{2,1,0:T(8,128)(2,1)S(1)}, u32[]{:S(2)}, u32[]{:S(2)}) collective-permute-start(bf16[3,64,384]{2,1,0:T(8,128)(2,1)S(1)} %get-tuple-element.74), channel_id=1, source_target_pairs={{0,3},{1,2},{2,1},{3,0},{4,7},{5,6},{6,5},{7,4},{8,11},{9,10},{10,... | collective-permute-start | bytes 442376 | tf_op jit(solution)/shard_map/ppermute | solution.py:166
  57.9 19.1 %collective-permute-start.5 = (bf16[3,64,384]{2,1,0:T(8,128)(2,1)S(1)}, bf16[3,64,384]{2,1,0:T(8,128)(2,1)S(1)}, u32[]{:S(2)}, u32[]{:S(2)}) collective-permute-start(bf16[3,64,384]{2,1,0:T(8,128)(2,1)S(1)} %get-tuple-element.54), channel_id=1, source_target_pairs={{0,1},{1,0},{2,3},{3,2},{4,5},{5,4},{6,7},{7,6},{8,9},{9,8},{10,11... | collective-permute-start | bytes 442376 | tf_op jit(solution)/shard_map/ppermute | solution.py:166
  58.9 19.1 %collective-permute-start.6 = (bf16[3,64,384]{2,1,0:T(8,128)(2,1)S(1)}, bf16[3,64,384]{2,1,0:T(8,128)(2,1)S(1)}, u32[]{:S(2)}, u32[]{:S(2)}) collective-permute-start(bf16[3,64,384]{2,1,0:T(8,128)(2,1)S(1)} %get-tuple-element.55), channel_id=1, source_target_pairs={{0,2},{1,3},{2,0},{3,1},{4,6},{5,7},{6,4},{7,5},{8,10},{9,11},{10,... | collective-permute-start | bytes 442376 | tf_op jit(solution)/shard_map/ppermute | solution.py:166
  59.3 24.0 %collective-permute-start.7 = (bf16[3,64,384]{2,1,0:T(8,128)(2,1)S(1)}, bf16[3,64,384]{2,1,0:T(8,128)(2,1)S(1)}, u32[]{:S(2)}, u32[]{:S(2)}) collective-permute-start(bf16[3,64,384]{2,1,0:T(8,128)(2,1)S(1)} %get-tuple-element.56), channel_id=1, source_target_pairs={{0,3},{1,2},{2,1},{3,0},{4,7},{5,6},{6,5},{7,4},{8,11},{9,10},{10,... | collective-permute-start | bytes 442376 | tf_op jit(solution)/shard_map/ppermute | solution.py:166

commit v3 on v2

--- a/solution.py
+++ b/solution.py
@@ -19,23 +19,22 @@
 F32 = jnp.float32
 
 
-SMEM_SPEC = pl.BlockSpec(memory_space=pltpu.SMEM)
 VMEM_SPEC = pl.BlockSpec(memory_space=pltpu.VMEM)
 HBM_SPEC = pl.BlockSpec(memory_space=pltpu.HBM)
 
 
-def call(kernel, place, arrays, outs, scratch=(), flops=0, spec=VMEM_SPEC, out_spec=VMEM_SPEC, vmem=48):
+def call(kernel, arrays, outs, scratch=(), flops=0, spec=VMEM_SPEC, out_spec=VMEM_SPEC, vmem=48):
     moved = sum(a.size * a.dtype.itemsize for a in arrays)
     moved += sum(math.prod(o.shape) * o.dtype.itemsize for o in outs)
     return pl.pallas_call(
         kernel,
         out_shape=tuple(outs),
-        in_specs=[SMEM_SPEC] + [spec] * len(arrays),
+        in_specs=[spec] * len(arrays),
         out_specs=tuple([out_spec] * len(outs)),
         scratch_shapes=list(scratch),
         cost_estimate=pl.CostEstimate(flops=flops, bytes_accessed=moved, transcendentals=0),
         compiler_params=pltpu.CompilerParams(vmem_limit_bytes=vmem * 1024 * 1024),
-    )(place, *arrays)
+    )(*arrays)
 
 
 def shape(dims, dtype=BF16):
@@ -58,6 +57,7 @@
         self.seg_rows = rows * devs
         self.near = self.reach * rows
         self.groups = self.seg_rows // self.near
+        self.teacher_rows = self.seg_rows if self.seg_rows <= 512 else rows
         self.scale = self.dim ** (-0.5)
 
 
@@ -86,69 +86,116 @@
     return groups
 
 
-def pack_kernel(plan, chunk, place, *refs):
-    me = place[1]
-    in_refs, out_refs, (held, sems) = refs[:3], refs[3:-2], refs[-2:]
-    copies = [pltpu.make_async_copy(r, held.at[i], sems.at[i]) for i, r in enumerate(in_refs)]
-    for copy in copies:
-        copy.start()
-    for at, copy in enumerate(copies):
-        copy.wait()
-        for step, out_ref in enumerate(out_refs):
-            start = pl.multiple_of((me ^ step) * plan.local_width, 128)
-            x = held[at, :, pl.ds(start, plan.local_width)]
-            x = x[:, chunk * plan.chunk_width : (chunk + 1) * plan.chunk_width]
-            out_ref[at] = folded(x, plan)
-
-
-def pack(plan, chunk, place, arrays):
-    if plan.local_width % 128 == 0:
-        outs = [shape((3,) + plan.piece) for _ in range(plan.devs)]
-        kernel = functools.partial(pack_kernel, plan, chunk)
-        scratch = [
-            pltpu.VMEM((3, plan.rows, plan.width), BF16),
-            pltpu.SemaphoreType.DMA((3,)),
-        ]
-        vmem = PACK_MIB if chunk == 0 else 48
-        return call(kernel, place, arrays, outs, scratch, spec=HBM_SPEC, vmem=vmem)
-    pieces = []
-    for step in range(plan.devs):
-        start = (place[1] ^ step) * plan.local_width + chunk * plan.chunk_width
-        taken = [lax.dynamic_slice_in_dim(a, start, plan.chunk_width, 1) for a in arrays]
-        pieces.append(jnp.stack([folded(x, plan) for x in taken]))
-    return pieces
-
-
-def unpack_kernel(plan, place, *refs):
-    me = place[1]
-    piece_refs, out_refs, (held, sems) = refs[:-5], refs[-5:-2], refs[-2:]
-    copies = [pltpu.make_async_copy(held.at[i], r, sems.at[i]) for i, r in enumerate(out_refs)]
+def columns_of(x, chunk, plan):
+    return folded(x[:, chunk * plan.chunk_width : (chunk + 1) * plan.chunk_width], plan)
+
+
+def pack_first_kernel(plan, *refs):
+    me = lax.axis_index("dev")
+    in_refs, out_refs, (held, made, in_sems, out_sems) = refs[:3], refs[3:-4], refs[-4:]
+    steps = range(plan.devs - 1, 0, -1)
+
+    def taken(step, at):
+        start = pl.multiple_of((me ^ step) * plan.local_width, 128)
+        block = in_refs[at].at[:, pl.ds(start, plan.local_width)]
+        return pltpu.make_async_copy(block, held.at[step - 1, at], in_sems.at[step - 1, at])
+
+    def given(step):
+        return pltpu.make_async_copy(
+            made.at[step - 1], out_refs[step - 1], out_sems.at[step - 1]
+        )
+
+    for step in steps:
+        for at in range(3):
+            taken(step, at).start()
+    for step in steps:
+        for at in range(3):
+            taken(step, at).wait()
+            made[step - 1, at] = columns_of(held[step - 1, at], 0, plan)
+        given(step).start()
+    for step in steps:
+        given(step).wait()
+
+
+def pack_rest_kernel(plan, chunk, *refs):
+    me = lax.axis_index("dev")
+    in_refs, out_refs = refs[:3], refs[3:]
     for at in range(3):
         for step in range(plan.devs):
             start = pl.multiple_of((me ^ step) * plan.local_width, 128)
+            x = in_refs[at][:, pl.ds(start, plan.local_width)]
+            out_refs[step][at] = columns_of(x, chunk, plan)
+            if chunk == 1 and step == 0:
+                out_refs[plan.devs][at] = columns_of(x, 0, plan)
+
+
+def pack(plan, arrays):
+    piece = shape((3,) + plan.piece)
+    chunks = []
+    if plan.local_width % 128 == 0 and plan.chunks > 1:
+        others = plan.devs - 1
+        scratch = [
+            pltpu.VMEM((others, 3, plan.rows, plan.local_width), BF16),
+            pltpu.VMEM((others, 3) + plan.piece, BF16),
+            pltpu.SemaphoreType.DMA((others, 3)),
+            pltpu.SemaphoreType.DMA((others,)),
+        ]
+        kernel = functools.partial(pack_first_kernel, plan)
+        sent = call(
+            kernel, arrays, [piece] * others, scratch, spec=HBM_SPEC, out_spec=HBM_SPEC, vmem=PACK_MIB
+        )
+        chunks.append([None] + list(sent))
+        for chunk in range(1, plan.chunks):
+            kernel = functools.partial(pack_rest_kernel, plan, chunk)
+            got = list(call(kernel, arrays, [piece] * (plan.devs + (chunk == 1))))
+            if chunk == 1:
+                chunks[0][0] = got.pop()
+            chunks.append(got)
+        return chunks
+    me = lax.axis_index("dev")
+    for chunk in range(plan.chunks):
+        pieces = []
+        for step in range(plan.devs):
+            start = (me ^ step) * plan.local_width + chunk * plan.chunk_width
+            taken = [lax.dynamic_slice_in_dim(a, start, plan.chunk_width, 1) for a in arrays]
+            pieces.append(jnp.stack([folded(x, plan) for x in taken]))
+        chunks.append(pieces)
+    return chunks
+
+
+def unpack_kernel(plan, *refs):
+    me = lax.axis_index("dev")
+    piece_refs, out_refs, (held, sems) = refs[:-5], refs[-5:-2], refs[-2:]
+
+    def given(step, at):
+        start = pl.multiple_of((me ^ step) * plan.local_width, 128)
+        block = out_refs[at].at[:, pl.ds(start, plan.local_width)]
+        return pltpu.make_async_copy(held.at[step, at], block, sems.at[step, at])
+
+    for step in range(plan.devs):
+        for at in range(3):
             got = [unfolded(piece_refs[c * plan.devs + step][at], plan) for c in range(plan.chunks)]
             for part in range(plan.fold):
                 rows = slice(part * plan.fold_rows, (part + 1) * plan.fold_rows)
                 x = [groups[part] for groups in got]
-                held[at, rows, pl.ds(start, plan.local_width)] = (
-                    x[0] if plan.chunks == 1 else jnp.concatenate(x, axis=1)
-                )
-        copies[at].start()
-    for copy in copies:
-        copy.wait()
-
-
-def unpack(plan, place, pieces):
+                held[step, at, rows, :] = x[0] if plan.chunks == 1 else jnp.concatenate(x, axis=1)
+            given(step, at).start()
+    for step in range(plan.devs):
+        for at in range(3):
+            given(step, at).wait()
+
+
+def unpack(plan, pieces):
     if plan.local_width % 128 == 0:
         flat = [piece for chunk in pieces for piece in chunk]
         outs = [shape((plan.rows, plan.width)) for _ in range(3)]
         scratch = [
-            pltpu.VMEM((3, plan.rows, plan.width), BF16),
-            pltpu.SemaphoreType.DMA((3,)),
+            pltpu.VMEM((plan.devs, 3, plan.rows, plan.local_width), BF16),
+            pltpu.SemaphoreType.DMA((plan.devs, 3)),
         ]
         kernel = functools.partial(unpack_kernel, plan)
-        return call(kernel, place, flat, outs, scratch, out_spec=HBM_SPEC)
-    order = jnp.arange(plan.devs, dtype=jnp.int32) ^ place[1]
+        return call(kernel, flat, outs, scratch, out_spec=HBM_SPEC)
+    order = jnp.arange(plan.devs, dtype=jnp.int32) ^ lax.axis_index("dev")
     chunks = []
     for chunk in pieces:
         x = jnp.take(jnp.stack(chunk), order, axis=0)
@@ -270,23 +317,43 @@
     return joined(gq, plan), joined(gk, plan), joined(gv, plan)
 
 
-def first_kernel(plan, place, *refs):
-    me, near = place[1], plan.near
-    piece_refs, halo_ref = refs[: plan.devs], refs[plan.devs]
-    q_ref, k_ref, v_ref, gq_ref, gk_ref, gv_ref, far_ref, ext = refs[plan.devs + 1 :]
+def teacher_kernel(plan, *refs):
+    me = lax.axis_index("dev")
+    piece_refs, (q_ref, k_ref, v_ref, target_ref) = refs[: plan.devs], refs[plan.devs :]
     for step, ref in enumerate(piece_refs):
         for at, to in enumerate((q_ref, k_ref, v_ref)):
             groups = unfolded(ref[at], plan)
             for part, rows in block_parts((me ^ step) * plan.rows, plan):
                 to[rows, :] = groups[part]
-    target = teacher_rows(plan, q_ref[:near, :], k_ref[...], v_ref[...])
+    count = plan.teacher_rows
+    if count == plan.seg_rows:
+        target_ref[...] = teacher_rows(plan, q_ref[...], k_ref[...], v_ref[...])
+        return
+
+    def body(i, _):
+        rows = pl.ds(pl.multiple_of(i * count, count), count)
+        target_ref[rows, :] = teacher_rows(plan, q_ref[rows, :], k_ref[...], v_ref[...])
+        return 0
+
+    lax.fori_loop(0, plan.seg_rows // count, body, 0)
+
+
+def teacher(plan, pieces):
+    outs = [shape((plan.seg_rows, plan.chunk_width))] * 4
+    flops = 4 * plan.heads * plan.seg_rows * plan.seg_rows * plan.dim
+    return call(functools.partial(teacher_kernel, plan), list(pieces), outs, (), flops)
+
+
+def first_kernel(plan, q_ref, k_ref, v_ref, target_ref, halo_ref, gq_ref, gk_ref, gv_ref, far_ref, ext):
+    near = plan.near
     for at, ref in enumerate((k_ref, v_ref)):
         for block in range(plan.reach):
             groups = unfolded(halo_ref[block, at], plan)
             for part, rows in block_parts(block * plan.rows, plan):
                 ext[at, rows, :] = groups[part]
         ext[at, near:, :] = ref[:near, :]
-    gq, gk, gv = student_group(plan, q_ref[:near, :], ext[0], ext[1], target, place[0] > 0)
+    open_far = lax.axis_index("seg") > 0
+    gq, gk, gv = student_group(plan, q_ref[:near, :], ext[0], ext[1], target_ref[:near, :], open_far)
     gq_ref[...] = gq.astype(BF16)
     for at, (grad, ref) in enumerate(((gk, gk_ref), (gv, gv_ref))):
         ref[...] = grad[near:]
@@ -295,29 +362,26 @@
             far_ref[block, at] = folded(grad[rows].astype(BF16), plan)
 
 
-def first_group(plan, place, pieces, halo):
+def first_group(plan, held, halo):
     near, width = plan.near, plan.chunk_width
-    outs = [shape((plan.seg_rows, width))] * 3 + [
+    outs = [
         shape((near, width)),
         shape((near, width), F32),
         shape((near, width), F32),
         shape((plan.reach, 2) + plan.piece),
     ]
     scratch = [pltpu.VMEM((2, 2 * near, width), BF16)]
-    flops = plan.heads * near * plan.dim * (24 * near + 4 * plan.seg_rows)
-    kernel = functools.partial(first_kernel, plan)
-    out = call(kernel, place, list(pieces) + [halo], outs, scratch, flops)
-    return out[:3], out[3:]
-
-
-def rest_kernel(plan, place, q_ref, k_ref, v_ref, k_start, v_start, gq_ref, gk_ref, gv_ref):
+    flops = 24 * plan.heads * near * near * plan.dim
+    return call(functools.partial(first_kernel, plan), list(held) + [halo], outs, scratch, flops)
+
+
+def rest_kernel(plan, q_ref, k_ref, v_ref, target_ref, k_start, v_start, gq_ref, gk_ref, gv_ref):
     near = plan.near
 
     def group(start):
         rows, keys = pl.ds(start + near, near), pl.ds(start, 2 * near)
-        q = q_ref[rows, :]
-        target = teacher_rows(plan, q, k_ref[...], v_ref[...])
-        return student_group(plan, q, k_ref[keys, :], v_ref[keys, :], target, None)
+        args = (q_ref[rows, :], k_ref[keys, :], v_ref[keys, :], target_ref[rows, :])
+        return student_group(plan, *args, None)
 
     if plan.groups == 2:
         gq, gk, gv = group(0)
@@ -341,21 +405,20 @@
     lax.fori_loop(0, plan.groups - 1, body, 0)
 
 
-def rest_groups(plan, place, held, starts):
+def rest_groups(plan, held, starts):
     near, width = plan.near, plan.chunk_width
+    count = plan.seg_rows - near
     outs = [
-        shape((plan.seg_rows - near, width)),
+        shape((count, width)),
         shape((plan.seg_rows, width), F32),
         shape((plan.seg_rows, width), F32),
     ]
-    count = plan.seg_rows - near
-    flops = plan.heads * count * plan.dim * (24 * near + 4 * plan.seg_rows)
-    kernel = functools.partial(rest_kernel, plan)
-    return call(kernel, place, list(held) + list(starts), outs, (), flops)
-
-
-def finish_kernel(plan, place, gq_first, gq_rest, gk, gv, far, *refs):
-    me = place[1]
+    flops = 24 * plan.heads * count * near * plan.dim
+    return call(functools.partial(rest_kernel, plan), list(held) + list(starts), outs, (), flops)
+
+
+def finish_kernel(plan, gq_first, gq_rest, gk, gv, far, *refs):
+    me = lax.axis_index("dev")
     out_refs, (grads,) = refs[: plan.devs], refs[plan.devs :]
     near = plan.near
     last = plan.seg_rows - near
@@ -373,11 +436,11 @@
             out_ref[at] = folded(grads[at, rows, :], plan)
 
 
-def finish(plan, place, gq_first, gq_rest, gk, gv, far):
+def finish(plan, gq_first, gq_rest, gk, gv, far):
     outs = [shape((3,) + plan.piece) for _ in range(plan.devs)]
     scratch = [pltpu.VMEM((3, plan.seg_rows, plan.chunk_width), BF16)]
     arrays = [gq_first, gq_rest, gk, gv, far]
-    return call(functools.partial(finish_kernel, plan), place, arrays, outs, scratch)
+    return call(functools.partial(finish_kernel, plan), arrays, outs, scratch)
 
 
 def local(queries, keys, values):
@@ -387,12 +450,9 @@
     onward = [(i, i + 1) for i in range(seg_count - 1)]
     backward = [(i + 1, i) for i in range(seg_count - 1)]
     me = lax.axis_index("dev")
-    place = jnp.stack([lax.axis_index("seg"), me]).astype(jnp.int32)
-    arrays = [queries, keys, values]
-    arrays = [queries, keys, values]
+    packed = pack(plan, [queries, keys, values])
     arrived = []
-    for c in range(plan.chunks):
-        pieces = pack(plan, c, place, arrays)
+    for pieces in packed:
         arrived.append(exchange(plan, pieces))
     returned = []
     for pieces in arrived:
@@ -403,12 +463,13 @@
             ]
         )
         halo = lax.ppermute(halo, "seg", onward)
-        held, (gq_first, gk, gv, far) = first_group(plan, place, pieces, halo)
+        held = teacher(plan, pieces)
+        gq_first, gk, gv, far = first_group(plan, held, halo)
         far = lax.ppermute(far, "seg", backward)
-        gq_rest, gk, gv = rest_groups(plan, place, held, (gk, gv))
-        pieces = finish(plan, place, gq_first, gq_rest, gk, gv, far)
+        gq_rest, gk, gv = rest_groups(plan, held, (gk, gv))
+        pieces = finish(plan, gq_first, gq_rest, gk, gv, far)
         returned.append(exchange(plan, pieces))
-    return tuple(unpack(plan, place, returned))
+    return tuple(unpack(plan, returned))
 
 
 def solution(mesh):

time: 85.7 us -> 82.6 us (0.964)
  Pallas kernels: 19.2 us -> 15.1 us
  waiting for transfers between devices: 34.8 us -> 36.1 us
    pallas_call x9 -> x11, Pallas kernels: 19.2 us -> 15.1 us  [call(): pl.pallas_call(kernel, out_shape=tuple(outs), in_specs=[spec] * len(array...]
    ppermute x12, waiting for transfers between devices: 34.8 us -> 36 us  [exchange(): got[step] = lax.ppermute(pieces[step], 'dev', pairs)]
    unnamed x12 -> x6, local copies, waits for them, and re-layouts: 3 us -> 2.98 us
  transfers between devices with their start and end apart: 16 -> 16, of which waited for: 7 -> 7; matrix products, arithmetic and copies ran while one was open for 0% -> 0% of each run, Pallas kernels for 18% -> 16%
where the time goes in v3:
time: 82.6 us; the launch traced here: 82.2 us
  waiting for transfers between devices  36.1 us (44%)
  starting transfers between devices  27.2 us (33%)
  Pallas kernels  15.1 us (18%)
  local copies, waits for them, and re-layouts  2.98 us (4%)
    ppermute x12, waiting for transfers between devices, exchange(): got[step] = lax.ppermute(pieces[step], 'dev', pairs)  36 us
    pallas_call x11, Pallas kernels, call(): pl.pallas_call(kernel, out_shape=tuple(outs), in_specs=[spec] * len(array...  15.1 us
    ppermute x12, starting transfers between devices, exchange(): got[step] = lax.ppermute(pieces[step], 'dev', pairs)  11.7 us
    ppermute x2, starting transfers between devices, local(): halo = lax.ppermute(halo, 'seg', onward)  10.1 us
    ppermute x2, starting transfers between devices, local(): far = lax.ppermute(far, 'seg', backward)  5.37 us
    unnamed x6, local copies, waits for them, and re-layouts  2.98 us
  transfers between devices with their start and end apart: 16, of which 7 were waited for; matrix products, arithmetic and copies ran while one was open for 0% of the time, Pallas kernels for 16%

profile of v3, /device:TPU:21, one launch (start us, length us, event | category | flops | bytes accessed | tf_op | source)
XLA Modules:
  0.0 82.2 jit_solution(4309553752769017381)
XLA Ops:
  0.6 1.0 %copy-done = bf16[128,1536]{1,0:T(8,128)(2,1)S(1)} copy-done((bf16[128,1536]{1,0:T(8,128)(2,1)S(1)}, bf16[128,1536]{1,0:T(8,128)(2,1)}, u32[]{:S(2)}) %copy-start) | copy-done | bytes 393240
  1.6 1.0 %copy-done.1 = bf16[128,1536]{1,0:T(8,128)(2,1)S(1)} copy-done((bf16[128,1536]{1,0:T(8,128)(2,1)S(1)}, bf16[128,1536]{1,0:T(8,128)(2,1)}, u32[]{:S(2)}) %copy-start.1) | copy-done | bytes 393240
  2.6 1.0 %copy-done.2 = bf16[128,1536]{1,0:T(8,128)(2,1)S(1)} copy-done((bf16[128,1536]{1,0:T(8,128)(2,1)S(1)}, bf16[128,1536]{1,0:T(8,128)(2,1)}, u32[]{:S(2)}) %copy-start.2) | copy-done | bytes 393240
  3.6 0.3 shard_map.58
  4.1 1.2 %collective-permute-start.8 = (bf16[3,64,384]{2,1,0:T(8,128)(2,1)S(1)}, bf16[3,64,384]{2,1,0:T(8,128)(2,1)S(1)}, u32[]{:S(2)}, u32[]{:S(2)}) collective-permute-start(bf16[3,64,384]{2,1,0:T(8,128)(2,1)S(1)} %get-tuple-element.61), channel_id=1, source_target_pairs={{0,1},{1,0},{2,3},{3,2},{4,5},{5,4},{6,7},{7,6},{8,9},{9,8},{10,11... | collective-permute-start | bytes 442376 | tf_op jit(solution)/shard_map/ppermute | solution.py:213
  5.3 2.0 %collective-permute-start.9 = (bf16[3,64,384]{2,1,0:T(8,128)(2,1)S(1)}, bf16[3,64,384]{2,1,0:T(8,128)(2,1)S(1)}, u32[]{:S(2)}, u32[]{:S(2)}) collective-permute-start(bf16[3,64,384]{2,1,0:T(8,128)(2,1)S(1)} %get-tuple-element.62), channel_id=1, source_target_pairs={{0,2},{1,3},{2,0},{3,1},{4,6},{5,7},{6,4},{7,5},{8,10},{9,11},{10,... | collective-permute-start | bytes 442376 | tf_op jit(solution)/shard_map/ppermute | solution.py:213
  7.3 2.3 %shard_map.59 = (bf16[3,64,384]{2,1,0:T(8,128)(2,1)}, bf16[3,64,384]{2,1,0:T(8,128)(2,1)}, bf16[3,64,384]{2,1,0:T(8,128)(2,1)}) custom-call(bf16[128,1536]{1,0:T(8,128)(2,1)} %refs_0_.3, bf16[128,1536]{1,0:T(8,128)(2,1)} %refs_1_.3, bf16[128,1536]{1,0:T(8,128)(2,1)} %refs_2_.3), custom_call_target="tpu_custom_call" | custom-call | bytes 1622016 | tf_op jit(solution)/shard_map/pallas_call | solution.py:29
  9.7 1.5 %collective-permute-start = (bf16[3,64,384]{2,1,0:T(8,128)(2,1)}, bf16[3,64,384]{2,1,0:T(8,128)(2,1)S(1)}, u32[]{:S(2)}, u32[]{:S(2)}) collective-permute-start(bf16[3,64,384]{2,1,0:T(8,128)(2,1)} %get-tuple-element.42), channel_id=1, source_target_pairs={{0,1},{1,0},{2,3},{3,2},{4,5},{5,4},{6,7},{7,6},{8,9},{9,8},{10,11... | collective-permute-start | bytes 442376 | tf_op jit(solution)/shard_map/ppermute | solution.py:213
  11.2 1.3 %collective-permute-start.2 = (bf16[3,64,384]{2,1,0:T(8,128)(2,1)}, bf16[3,64,384]{2,1,0:T(8,128)(2,1)S(1)}, u32[]{:S(2)}, u32[]{:S(2)}) collective-permute-start(bf16[3,64,384]{2,1,0:T(8,128)(2,1)} %get-tuple-element.44), channel_id=1, source_target_pairs={{0,3},{1,2},{2,1},{3,0},{4,7},{5,6},{6,5},{7,4},{8,11},{9,10},{10,... | collective-permute-start | bytes 442376 | tf_op jit(solution)/shard_map/ppermute | solution.py:213
  12.5 4.6 %collective-permute-done.9.refs_2_ = bf16[3,64,384]{2,1,0:T(8,128)(2,1)S(1)} collective-permute-done((bf16[3,64,384]{2,1,0:T(8,128)(2,1)S(1)}, bf16[3,64,384]{2,1,0:T(8,128)(2,1)S(1)}, u32[]{:S(2)}, u32[]{:S(2)}) %collective-permute-start.9) | collective-permute-done | bytes 147488 | tf_op jit(solution)/shard_map/ppermute | solution.py:213
  17.1 5.6 %collective-permute-start.11 = (bf16[2,2,64,384]{3,2,1,0:T(8,128)(2,1)S(1)}, bf16[2,2,64,384]{3,2,1,0:T(8,128)(2,1)S(1)}, u32[]{:S(2)}, u32[]{:S(2)}) collective-permute-start(bf16[2,2,64,384]{3,2,1,0:T(8,128)(2,1)S(1)} %pad_maximum_fusion.1), channel_id=1, source_target_pairs={{0,4},{4,8},{8,12},{12,16},{16,20},{20,24},{24,28},{1,5},{5,9},{9,... | collective-permute-start | bytes 589832 | tf_op jit(solution)/shard_map/ppermute | solution.py:465
  22.7 3.2 %collective-permute-done.1.refs_2_ = bf16[3,64,384]{2,1,0:T(8,128)(2,1)S(1)} collective-permute-done((bf16[3,64,384]{2,1,0:T(8,128)(2,1)}, bf16[3,64,384]{2,1,0:T(8,128)(2,1)S(1)}, u32[]{:S(2)}, u32[]{:S(2)}) %collective-permute-start.1) | collective-permute-done | bytes 147488 | tf_op jit(solution)/shard_map/ppermute | solution.py:213
  26.0 4.9 %collective-permute-done.2.refs_3_ = bf16[3,64,384]{2,1,0:T(8,128)(2,1)S(1)} collective-permute-done((bf16[3,64,384]{2,1,0:T(8,128)(2,1)}, bf16[3,64,384]{2,1,0:T(8,128)(2,1)S(1)}, u32[]{:S(2)}, u32[]{:S(2)}) %collective-permute-start.2) | collective-permute-done | bytes 147488 | tf_op jit(solution)/shard_map/ppermute | solution.py:213
  30.9 4.5 %collective-permute-start.3 = (bf16[2,2,64,384]{3,2,1,0:T(8,128)(2,1)S(1)}, bf16[2,2,64,384]{3,2,1,0:T(8,128)(2,1)S(1)}, u32[]{:S(2)}, u32[]{:S(2)}) collective-permute-start(bf16[2,2,64,384]{3,2,1,0:T(8,128)(2,1)S(1)} %pad_maximum_fusion), channel_id=1, source_target_pairs={{0,4},{4,8},{8,12},{12,16},{16,20},{20,24},{24,28},{1,5},{5,9},{9,... | collective-permute-start | bytes 589832 | tf_op jit(solution)/shard_map/ppermute | solution.py:465
  35.5 1.2 %shard_map.64 = (bf16[512,192]{1,0:T(8,128)(2,1)S(1)}, bf16[512,192]{1,0:T(8,128)(2,1)S(1)}, bf16[512,192]{1,0:T(8,128)(2,1)S(1)}, bf16[512,192]{1,0:T(8,128)(2,1)S(1)}) custom-call(bf16[3,64,384]{2,1,0:T(8,128)(2,1)S(1)} %get-tuple-element.60.refs_0_, bf16[3,64,384]{2,1,0:T(8,128)(2,1)S(1)} %collective-permute-done.8.refs_1_, ...), custom_call_target="tpu_custom_call" | custom-call | flops 201326592 | bytes 1376256 | tf_op jit(solution)/shard_map/pallas_call | solution.py:29
  36.7 2.1 %shard_map.65 = (bf16[256,192]{1,0:T(8,128)(2,1)S(1)}, f32[256,192]{1,0:T(8,128)S(1)}, f32[256,192]{1,0:T(8,128)S(1)}, bf16[2,2,64,384]{3,2,1,0:T(8,128)(2,1)S(1)}) custom-call(bf16[512,192]{1,0:T(8,128)(2,1)S(1)} %get-tuple-element.64.q_ref, bf16[512,192]{1,0:T(8,128)(2,1)S(1)} %get-tuple-element.65.k_ref, bf16[512,192]{1,0:T(8,128)(2,1)S(1)} %get-tuple-element.66.v_ref, ...), custom_call_target="tpu_custom_call" | custom-call | flops 301989888 | bytes 1671168 | tf_op jit(solution)/shard_map/pallas_call | solution.py:29
  38.8 1.9 %collective-permute-start.12 = (bf16[2,2,64,384]{3,2,1,0:T(8,128)(2,1)S(1)}, bf16[2,2,64,384]{3,2,1,0:T(8,128)(2,1)S(1)}, u32[]{:S(2)}, u32[]{:S(2)}) collective-permute-start(bf16[2,2,64,384]{3,2,1,0:T(8,128)(2,1)S(1)} %get-tuple-element.74), channel_id=1, source_target_pairs={{4,0},{8,4},{12,8},{16,12},{20,16},{24,20},{28,24},{5,1},{9,5},{13... | collective-permute-start | bytes 589832 | tf_op jit(solution)/shard_map/ppermute | solution.py:468
  40.7 1.2 %shard_map.60 = (bf16[512,192]{1,0:T(8,128)(2,1)S(1)}, bf16[512,192]{1,0:T(8,128)(2,1)S(1)}, bf16[512,192]{1,0:T(8,128)(2,1)S(1)}, bf16[512,192]{1,0:T(8,128)(2,1)S(1)}) custom-call(bf16[3,64,384]{2,1,0:T(8,128)(2,1)S(1)} %get-tuple-element.41.refs_0_, bf16[3,64,384]{2,1,0:T(8,128)(2,1)S(1)} %collective-permute-done.refs_1_, ...), custom_call_target="tpu_custom_call" | custom-call | flops 201326592 | bytes 1376256 | tf_op jit(solution)/shard_map/pallas_call | solution.py:29
  41.9 2.1 %shard_map.61 = (bf16[256,192]{1,0:T(8,128)(2,1)S(1)}, f32[256,192]{1,0:T(8,128)S(1)}, f32[256,192]{1,0:T(8,128)S(1)}, bf16[2,2,64,384]{3,2,1,0:T(8,128)(2,1)S(1)}) custom-call(bf16[512,192]{1,0:T(8,128)(2,1)S(1)} %get-tuple-element.45.q_ref, bf16[512,192]{1,0:T(8,128)(2,1)S(1)} %get-tuple-element.46.k_ref, bf16[512,192]{1,0:T(8,128)(2,1)S(1)} %get-tuple-element.47.v_ref, ...), custom_call_target="tpu_custom_call" | custom-call | flops 301989888 | bytes 1671168 | tf_op jit(solution)/shard_map/pallas_call | solution.py:29
  44.0 3.4 %collective-permute-start.4 = (bf16[2,2,64,384]{3,2,1,0:T(8,128)(2,1)S(1)}, bf16[2,2,64,384]{3,2,1,0:T(8,128)(2,1)S(1)}, u32[]{:S(2)}, u32[]{:S(2)}) collective-permute-start(bf16[2,2,64,384]{3,2,1,0:T(8,128)(2,1)S(1)} %get-tuple-element.55), channel_id=1, source_target_pairs={{4,0},{8,4},{12,8},{16,12},{20,16},{24,20},{28,24},{5,1},{9,5},{13... | collective-permute-start | bytes 589832 | tf_op jit(solution)/shard_map/ppermute | solution.py:468
  47.5 2.0 %shard_map.66 = (bf16[256,192]{1,0:T(8,128)(2,1)S(1)}, f32[512,192]{1,0:T(8,128)S(1)}, f32[512,192]{1,0:T(8,128)S(1)}) custom-call(bf16[512,192]{1,0:T(8,128)(2,1)S(1)} %get-tuple-element.64.q_ref, bf16[512,192]{1,0:T(8,128)(2,1)S(1)} %get-tuple-element.65.k_ref, bf16[512,192]{1,0:T(8,128)(2,1)S(1)} %get-tuple-element.66.v_ref, ...), custom_call_target="tpu_custom_call" | custom-call | flops 301989888 | bytes 2064384 | tf_op jit(solution)/shard_map/pallas_call | solution.py:29
  49.8 2.0 %shard_map.62 = (bf16[256,192]{1,0:T(8,128)(2,1)S(1)}, f32[512,192]{1,0:T(8,128)S(1)}, f32[512,192]{1,0:T(8,128)S(1)}) custom-call(bf16[512,192]{1,0:T(8,128)(2,1)S(1)} %get-tuple-element.45.q_ref, bf16[512,192]{1,0:T(8,128)(2,1)S(1)} %get-tuple-element.46.k_ref, bf16[512,192]{1,0:T(8,128)(2,1)S(1)} %get-tuple-element.47.v_ref, ...), custom_call_target="tpu_custom_call" | custom-call | flops 301989888 | bytes 2064384 | tf_op jit(solution)/shard_map/pallas_call | solution.py:29
  51.8 1.4 %collective-permute-start.14 = (bf16[3,64,384]{2,1,0:T(8,128)(2,1)S(1)}, bf16[3,64,384]{2,1,0:T(8,128)(2,1)S(1)}, u32[]{:S(2)}, u32[]{:S(2)}) collective-permute-start(bf16[3,64,384]{2,1,0:T(8,128)(2,1)S(1)} %get-tuple-element.77), channel_id=1, source_target_pairs={{0,2},{1,3},{2,0},{3,1},{4,6},{5,7},{6,4},{7,5},{8,10},{9,11},{10,... | collective-permute-start | bytes 442376 | tf_op jit(solution)/shard_map/ppermute | solution.py:213
  53.2 1.3 %collective-permute-start.15 = (bf16[3,64,384]{2,1,0:T(8,128)(2,1)S(1)}, bf16[3,64,384]{2,1,0:T(8,128)(2,1)S(1)}, u32[]{:S(2)}, u32[]{:S(2)}) collective-permute-start(bf16[3,64,384]{2,1,0:T(8,128)(2,1)S(1)} %get-tuple-element.78), channel_id=1, source_target_pairs={{0,3},{1,2},{2,1},{3,0},{4,7},{5,6},{6,5},{7,4},{8,11},{9,10},{10,... | collective-permute-start | bytes 442376 | tf_op jit(solution)/shard_map/ppermute | solution.py:213
  54.7 1.0 %collective-permute-start.5 = (bf16[3,64,384]{2,1,0:T(8,128)(2,1)S(1)}, bf16[3,64,384]{2,1,0:T(8,128)(2,1)S(1)}, u32[]{:S(2)}, u32[]{:S(2)}) collective-permute-start(bf16[3,64,384]{2,1,0:T(8,128)(2,1)S(1)} %get-tuple-element.57), channel_id=1, source_target_pairs={{0,1},{1,0},{2,3},{3,2},{4,5},{5,4},{6,7},{7,6},{8,9},{9,8},{10,11... | collective-permute-start | bytes 442376 | tf_op jit(solution)/shard_map/ppermute | solution.py:213
  55.7 0.4 collective-permute-start.6
  56.2 1.3 %collective-permute-start.7 = (bf16[3,64,384]{2,1,0:T(8,128)(2,1)S(1)}, bf16[3,64,384]{2,1,0:T(8,128)(2,1)S(1)}, u32[]{:S(2)}, u32[]{:S(2)}) collective-permute-start(bf16[3,64,384]{2,1,0:T(8,128)(2,1)S(1)} %get-tuple-element.59), channel_id=1, source_target_pairs={{0,3},{1,2},{2,1},{3,0},{4,7},{5,6},{6,5},{7,4},{8,11},{9,10},{10,... | collective-permute-start | bytes 442376 | tf_op jit(solution)/shard_map/ppermute | solution.py:213
  57.4 5.2 %collective-permute-done.14.refs_6_ = bf16[3,64,384]{2,1,0:T(8,128)(2,1)S(1)} collective-permute-done((bf16[3,64,384]{2,1,0:T(8,128)(2,1)S(1)}, bf16[3,64,384]{2,1,0:T(8,128)(2,1)S(1)}, u32[]{:S(2)}, u32[]{:S(2)}) %collective-permute-start.14) | collective-permute-done | bytes 147488 | tf_op jit(solution)/shard_map/ppermute | solution.py:213
  62.6 11.8 %collective-permute-done.15.refs_7_ = bf16[3,64,384]{2,1,0:T(8,128)(2,1)S(1)} collective-permute-done((bf16[3,64,384]{2,1,0:T(8,128)(2,1)S(1)}, bf16[3,64,384]{2,1,0:T(8,128)(2,1)S(1)}, u32[]{:S(2)}, u32[]{:S(2)}) %collective-permute-start.15) | collective-permute-done | bytes 147488 | tf_op jit(solution)/shard_map/ppermute | solution.py:213
  74.5 0.8 collective-permute-done.6.refs_2_
  75.3 5.5 %collective-permute-done.7.refs_3_ = bf16[3,64,384]{2,1,0:T(8,128)(2,1)S(1)} collective-permute-done((bf16[3,64,384]{2,1,0:T(8,128)(2,1)S(1)}, bf16[3,64,384]{2,1,0:T(8,128)(2,1)S(1)}, u32[]{:S(2)}, u32[]{:S(2)}) %collective-permute-start.7) | collective-permute-done | bytes 147488 | tf_op jit(solution)/shard_map/ppermute | solution.py:213
  80.8 1.4 %shard_map.68 = (bf16[128,1536]{1,0:T(8,128)(2,1)}, bf16[128,1536]{1,0:T(8,128)(2,1)}, bf16[128,1536]{1,0:T(8,128)(2,1)}) custom-call(bf16[3,64,384]{2,1,0:T(8,128)(2,1)S(1)} %get-tuple-element.56.refs_0_, bf16[3,64,384]{2,1,0:T(8,128)(2,1)S(1)} %collective-permute-done.5.refs_1_, bf16[3,64,384]{2,1,0:T(8,128)(2,1)S(1)} %collective-permute-done.6.refs_2_, ...), custom_call_target="tpu_custom_call" | custom-call | bytes 2359296 | tf_op jit(solution)/shard_map/pallas_call | solution.py:29
  (21 shorter events, 1.0 us)
Async XLA Ops:
  0.6 1.0 %copy-start = (bf16[128,1536]{1,0:T(8,128)(2,1)S(1)}, bf16[128,1536]{1,0:T(8,128)(2,1)}, u32[]{:S(2)}) copy-start(bf16[128,1536]{1,0:T(8,128)(2,1)} %refs_0_.3) | copy-start | bytes 1179652
  1.6 1.0 %copy-start.1 = (bf16[128,1536]{1,0:T(8,128)(2,1)S(1)}, bf16[128,1536]{1,0:T(8,128)(2,1)}, u32[]{:S(2)}) copy-start(bf16[128,1536]{1,0:T(8,128)(2,1)} %refs_1_.3) | copy-start | bytes 1179652
  2.6 1.0 %copy-start.2 = (bf16[128,1536]{1,0:T(8,128)(2,1)S(1)}, bf16[128,1536]{1,0:T(8,128)(2,1)}, u32[]{:S(2)}) copy-start(bf16[128,1536]{1,0:T(8,128)(2,1)} %refs_2_.3) | copy-start | bytes 1179652
  3.9 7.3 %collective-permute-start.10 = (bf16[3,64,384]{2,1,0:T(8,128)(2,1)S(1)}, bf16[3,64,384]{2,1,0:T(8,128)(2,1)S(1)}, u32[]{:S(2)}, u32[]{:S(2)}) collective-permute-start(bf16[3,64,384]{2,1,0:T(8,128)(2,1)S(1)} %get-tuple-element.63), channel_id=1, source_target_pairs={{0,3},{1,2},{2,1},{3,0},{4,7},{5,6},{6,5},{7,4},{8,11},{9,10},{10,... | collective-permute-start | bytes 442376 | tf_op jit(solution)/shard_map/ppermute | solution.py:213
  4.1 8.3 %collective-permute-start.8 = (bf16[3,64,384]{2,1,0:T(8,128)(2,1)S(1)}, bf16[3,64,384]{2,1,0:T(8,128)(2,1)S(1)}, u32[]{:S(2)}, u32[]{:S(2)}) collective-permute-start(bf16[3,64,384]{2,1,0:T(8,128)(2,1)S(1)} %get-tuple-element.61), channel_id=1, source_target_pairs={{0,1},{1,0},{2,3},{3,2},{4,5},{5,4},{6,7},{7,6},{8,9},{9,8},{10,11... | collective-permute-start | bytes 442376 | tf_op jit(solution)/shard_map/ppermute | solution.py:213
  5.3 11.7 %collective-permute-start.9 = (bf16[3,64,384]{2,1,0:T(8,128)(2,1)S(1)}, bf16[3,64,384]{2,1,0:T(8,128)(2,1)S(1)}, u32[]{:S(2)}, u32[]{:S(2)}) collective-permute-start(bf16[3,64,384]{2,1,0:T(8,128)(2,1)S(1)} %get-tuple-element.62), channel_id=1, source_target_pairs={{0,2},{1,3},{2,0},{3,1},{4,6},{5,7},{6,4},{7,5},{8,10},{9,11},{10,... | collective-permute-start | bytes 442376 | tf_op jit(solution)/shard_map/ppermute | solution.py:213
  9.7 13.0 %collective-permute-start = (bf16[3,64,384]{2,1,0:T(8,128)(2,1)}, bf16[3,64,384]{2,1,0:T(8,128)(2,1)S(1)}, u32[]{:S(2)}, u32[]{:S(2)}) collective-permute-start(bf16[3,64,384]{2,1,0:T(8,128)(2,1)} %get-tuple-element.42), channel_id=1, source_target_pairs={{0,1},{1,0},{2,3},{3,2},{4,5},{5,4},{6,7},{7,6},{8,9},{9,8},{10,11... | collective-permute-start | bytes 442376 | tf_op jit(solution)/shard_map/ppermute | solution.py:213
  11.2 14.7 %collective-permute-start.1 = (bf16[3,64,384]{2,1,0:T(8,128)(2,1)}, bf16[3,64,384]{2,1,0:T(8,128)(2,1)S(1)}, u32[]{:S(2)}, u32[]{:S(2)}) collective-permute-start(bf16[3,64,384]{2,1,0:T(8,128)(2,1)} %get-tuple-element.43), channel_id=1, source_target_pairs={{0,2},{1,3},{2,0},{3,1},{4,6},{5,7},{6,4},{7,5},{8,10},{9,11},{10,... | collective-permute-start | bytes 442376 | tf_op jit(solution)/shard_map/ppermute | solution.py:213
  11.2 19.6 %collective-permute-start.2 = (bf16[3,64,384]{2,1,0:T(8,128)(2,1)}, bf16[3,64,384]{2,1,0:T(8,128)(2,1)S(1)}, u32[]{:S(2)}, u32[]{:S(2)}) collective-permute-start(bf16[3,64,384]{2,1,0:T(8,128)(2,1)} %get-tuple-element.44), channel_id=1, source_target_pairs={{0,3},{1,2},{2,1},{3,0},{4,7},{5,6},{6,5},{7,4},{8,11},{9,10},{10,... | collective-permute-start | bytes 442376 | tf_op jit(solution)/shard_map/ppermute | solution.py:213
  17.1 19.5 %collective-permute-start.11 = (bf16[2,2,64,384]{3,2,1,0:T(8,128)(2,1)S(1)}, bf16[2,2,64,384]{3,2,1,0:T(8,128)(2,1)S(1)}, u32[]{:S(2)}, u32[]{:S(2)}) collective-permute-start(bf16[2,2,64,384]{3,2,1,0:T(8,128)(2,1)S(1)} %pad_maximum_fusion.1), channel_id=1, source_target_pairs={{0,4},{4,8},{8,12},{12,16},{16,20},{20,24},{24,28},{1,5},{5,9},{9,... | collective-permute-start | bytes 589832 | tf_op jit(solution)/shard_map/ppermute | solution.py:465
  30.9 11.0 %collective-permute-start.3 = (bf16[2,2,64,384]{3,2,1,0:T(8,128)(2,1)S(1)}, bf16[2,2,64,384]{3,2,1,0:T(8,128)(2,1)S(1)}, u32[]{:S(2)}, u32[]{:S(2)}) collective-permute-start(bf16[2,2,64,384]{3,2,1,0:T(8,128)(2,1)S(1)} %pad_maximum_fusion), channel_id=1, source_target_pairs={{0,4},{4,8},{8,12},{12,16},{16,20},{20,24},{24,28},{1,5},{5,9},{9,... | collective-permute-start | bytes 589832 | tf_op jit(solution)/shard_map/ppermute | solution.py:465
  38.8 10.7 %collective-permute-start.12 = (bf16[2,2,64,384]{3,2,1,0:T(8,128)(2,1)S(1)}, bf16[2,2,64,384]{3,2,1,0:T(8,128)(2,1)S(1)}, u32[]{:S(2)}, u32[]{:S(2)}) collective-permute-start(bf16[2,2,64,384]{3,2,1,0:T(8,128)(2,1)S(1)} %get-tuple-element.74), channel_id=1, source_target_pairs={{4,0},{8,4},{12,8},{16,12},{20,16},{24,20},{28,24},{5,1},{9,5},{13... | collective-permute-start | bytes 589832 | tf_op jit(solution)/shard_map/ppermute | solution.py:468
  44.0 10.5 %collective-permute-start.4 = (bf16[2,2,64,384]{3,2,1,0:T(8,128)(2,1)S(1)}, bf16[2,2,64,384]{3,2,1,0:T(8,128)(2,1)S(1)}, u32[]{:S(2)}, u32[]{:S(2)}) collective-permute-start(bf16[2,2,64,384]{3,2,1,0:T(8,128)(2,1)S(1)} %get-tuple-element.55), channel_id=1, source_target_pairs={{4,0},{8,4},{12,8},{16,12},{20,16},{24,20},{28,24},{5,1},{9,5},{13... | collective-permute-start | bytes 589832 | tf_op jit(solution)/shard_map/ppermute | solution.py:468
  49.7 6.5 %collective-permute-start.13 = (bf16[3,64,384]{2,1,0:T(8,128)(2,1)S(1)}, bf16[3,64,384]{2,1,0:T(8,128)(2,1)S(1)}, u32[]{:S(2)}, u32[]{:S(2)}) collective-permute-start(bf16[3,64,384]{2,1,0:T(8,128)(2,1)S(1)} %get-tuple-element.76), channel_id=1, source_target_pairs={{0,1},{1,0},{2,3},{3,2},{4,5},{5,4},{6,7},{7,6},{8,9},{9,8},{10,11... | collective-permute-start | bytes 442376 | tf_op jit(solution)/shard_map/ppermute | solution.py:213
  51.8 10.8 %collective-permute-start.14 = (bf16[3,64,384]{2,1,0:T(8,128)(2,1)S(1)}, bf16[3,64,384]{2,1,0:T(8,128)(2,1)S(1)}, u32[]{:S(2)}, u32[]{:S(2)}) collective-permute-start(bf16[3,64,384]{2,1,0:T(8,128)(2,1)S(1)} %get-tuple-element.77), channel_id=1, source_target_pairs={{0,2},{1,3},{2,0},{3,1},{4,6},{5,7},{6,4},{7,5},{8,10},{9,11},{10,... | collective-permute-start | bytes 442376 | tf_op jit(solution)/shard_map/ppermute | solution.py:213
  53.2 21.3 %collective-permute-start.15 = (bf16[3,64,384]{2,1,0:T(8,128)(2,1)S(1)}, bf16[3,64,384]{2,1,0:T(8,128)(2,1)S(1)}, u32[]{:S(2)}, u32[]{:S(2)}) collective-permute-start(bf16[3,64,384]{2,1,0:T(8,128)(2,1)S(1)} %get-tuple-element.78), channel_id=1, source_target_pairs={{0,3},{1,2},{2,1},{3,0},{4,7},{5,6},{6,5},{7,4},{8,11},{9,10},{10,... | collective-permute-start | bytes 442376 | tf_op jit(solution)/shard_map/ppermute | solution.py:213
  54.7 19.7 %collective-permute-start.5 = (bf16[3,64,384]{2,1,0:T(8,128)(2,1)S(1)}, bf16[3,64,384]{2,1,0:T(8,128)(2,1)S(1)}, u32[]{:S(2)}, u32[]{:S(2)}) collective-permute-start(bf16[3,64,384]{2,1,0:T(8,128)(2,1)S(1)} %get-tuple-element.57), channel_id=1, source_target_pairs={{0,1},{1,0},{2,3},{3,2},{4,5},{5,4},{6,7},{7,6},{8,9},{9,8},{10,11... | collective-permute-start | bytes 442376 | tf_op jit(solution)/shard_map/ppermute | solution.py:213
  55.7 19.6 %collective-permute-start.6 = (bf16[3,64,384]{2,1,0:T(8,128)(2,1)S(1)}, bf16[3,64,384]{2,1,0:T(8,128)(2,1)S(1)}, u32[]{:S(2)}, u32[]{:S(2)}) collective-permute-start(bf16[3,64,384]{2,1,0:T(8,128)(2,1)S(1)} %get-tuple-element.58), channel_id=1, source_target_pairs={{0,2},{1,3},{2,0},{3,1},{4,6},{5,7},{6,4},{7,5},{8,10},{9,11},{10,... | collective-permute-start | bytes 442376 | tf_op jit(solution)/shard_map/ppermute | solution.py:213
  56.2 24.6 %collective-permute-start.7 = (bf16[3,64,384]{2,1,0:T(8,128)(2,1)S(1)}, bf16[3,64,384]{2,1,0:T(8,128)(2,1)S(1)}, u32[]{:S(2)}, u32[]{:S(2)}) collective-permute-start(bf16[3,64,384]{2,1,0:T(8,128)(2,1)S(1)} %get-tuple-element.59), channel_id=1, source_target_pairs={{0,3},{1,2},{2,1},{3,0},{4,7},{5,6},{6,5},{7,4},{8,11},{9,10},{10,... | collective-permute-start | bytes 442376 | tf_op jit(solution)/shard_map/ppermute | solution.py:213

commit v4 on v3

--- a/solution.py
+++ b/solution.py
@@ -218,6 +218,13 @@
     return lax.dot_general(a, b, ((over[:1], over[1:]), ((), ())), preferred_element_type=F32)
 
 
+def dot_heads(parts, b, over):
+    axis = 1 - over[0]
+    count = parts[0].shape[axis]
+    out = dot(jnp.concatenate(parts, axis=axis), b, over)
+    return [out[i * count : (i + 1) * count] for i in range(len(parts))]
+
+
 def of_head(x, head, plan):
     if plan.heads == 1:
         return x
@@ -252,10 +259,9 @@
 
 def teacher_rows(plan, q, k, v):
     parts = []
-    for head in range(plan.heads):
-        scores = dot(of_head(q, head, plan), k, (1, 1))
-        top = scores.max(-1, keepdims=True)
-        e = jnp.exp2((scores - top) * (plan.scale * LOG2E))
+    scores = [dot(of_head(q, head, plan), k, (1, 1)) for head in range(plan.heads)]
+    for s in scores:
+        e = jnp.exp2((s - s.max(-1, keepdims=True)) * (plan.scale * LOG2E))
         parts.append(dot(e.astype(BF16), v, (1, 0)) * (1.0 / e.sum(-1, keepdims=True)))
     return joined(parts, plan).astype(BF16)
 
@@ -287,12 +293,12 @@
             lines.append(jnp.concatenate(left + [x] + right, axis=1))
         return lines[0] if reach == 1 else jnp.concatenate(lines, axis=0)
 
+    scores = [dot(of_head(q, head, plan), k, (1, 1)) for head in heads]
     weights, probability, outs = [], [], []
     for head in heads:
-        scores = dot(of_head(q, head, plan), k, (1, 1))
         ps = []
         for i in range(reach):
-            s = window(scores, i)
+            s = window(scores[head], i)
             s = [seen(i, s[:, j * rows : (j + 1) * rows], i + j) for j in range(reach + 1)]
             s = jnp.concatenate(s, axis=1)
             top = s.max(-1, keepdims=True)
@@ -302,18 +308,18 @@
         weights.append(whole([p.astype(BF16) for p in ps]))
         outs.append(dot(weights[head], v, (1, 0)))
     d_out = (128.0 * (joined(outs, plan) - target.astype(F32))).astype(BF16)
-    gq, gk, gv = [], [], []
+    d_prob = [dot(of_head(d_out, head, plan), v, (1, 1)) for head in heads]
+    gv = dot_heads(weights, d_out, (0, 0))
+    d_scores = []
     for head in heads:
-        d_prob = dot(of_head(d_out, head, plan), v, (1, 1))
         ds = []
         for i, p in enumerate(probability[head]):
-            d = window(d_prob, i)
+            d = window(d_prob[head], i)
             inner = (p * d).sum(-1, keepdims=True)
             ds.append((p * (d - inner) * plan.scale).astype(BF16))
-        d_scores = whole(ds)
-        gq.append(dot(d_scores, k, (1, 0)))
-        gk.append(dot(d_scores, q, (0, 0)))
-        gv.append(dot(weights[head], d_out, (0, 0)))
+        d_scores.append(whole(ds))
+    gk = dot_heads(d_scores, q, (0, 0))
+    gq = dot_heads(d_scores, k, (1, 0))
     return joined(gq, plan), joined(gk, plan), joined(gv, plan)
 
 

time: 82.6 us -> 80 us (0.969)
  the two profiles are of different devices: /device:TPU:21 before, /device:TPU:12 now
where the time goes in v4:
time: 80 us; the launch traced here: 79.6 us
  waiting for transfers between devices  37.6 us (47%)
  starting transfers between devices  25.6 us (32%)
  Pallas kernels  12.5 us (16%)
  local copies, waits for them, and re-layouts  2.98 us (4%)
  between operations  0.8 us (1%)
    ppermute x12, waiting for transfers between devices, exchange(): got[step] = lax.ppermute(pieces[step], 'dev', pairs)  37.6 us
    ppermute x12, starting transfers between devices, exchange(): got[step] = lax.ppermute(pieces[step], 'dev', pairs)  15.3 us
    pallas_call x11, Pallas kernels, call(): pl.pallas_call(kernel, out_shape=tuple(outs), in_specs=[spec] * len(array...  12.5 us
    ppermute x2, starting transfers between devices, local(): far = lax.ppermute(far, 'seg', backward)  6.46 us
    ppermute x2, starting transfers between devices, local(): halo = lax.ppermute(halo, 'seg', onward)  3.84 us
    unnamed x6, local copies, waits for them, and re-layouts  2.98 us
  transfers between devices with their start and end apart: 16, of which 10 were waited for; matrix products, arithmetic and copies ran while one was open for 0% of the time, Pallas kernels for 14%

profile of v4, /device:TPU:12, one launch (start us, length us, event | category | flops | bytes accessed | tf_op | source)
XLA Modules:
  0.0 79.6 jit_solution(13545245771383009274)
XLA Ops:
  0.6 1.0 %copy-done = bf16[128,1536]{1,0:T(8,128)(2,1)S(1)} copy-done((bf16[128,1536]{1,0:T(8,128)(2,1)S(1)}, bf16[128,1536]{1,0:T(8,128)(2,1)}, u32[]{:S(2)}) %copy-start) | copy-done | bytes 393240
  1.6 1.0 %copy-done.1 = bf16[128,1536]{1,0:T(8,128)(2,1)S(1)} copy-done((bf16[128,1536]{1,0:T(8,128)(2,1)S(1)}, bf16[128,1536]{1,0:T(8,128)(2,1)}, u32[]{:S(2)}) %copy-start.1) | copy-done | bytes 393240
  2.6 1.0 %copy-done.2 = bf16[128,1536]{1,0:T(8,128)(2,1)S(1)} copy-done((bf16[128,1536]{1,0:T(8,128)(2,1)S(1)}, bf16[128,1536]{1,0:T(8,128)(2,1)}, u32[]{:S(2)}) %copy-start.2) | copy-done | bytes 393240
  3.9 1.6 %collective-permute-start.10 = (bf16[3,64,384]{2,1,0:T(8,128)(2,1)S(1)}, bf16[3,64,384]{2,1,0:T(8,128)(2,1)S(1)}, u32[]{:S(2)}, u32[]{:S(2)}) collective-permute-start(bf16[3,64,384]{2,1,0:T(8,128)(2,1)S(1)} %get-tuple-element.63), channel_id=1, source_target_pairs={{0,3},{1,2},{2,1},{3,0},{4,7},{5,6},{6,5},{7,4},{8,11},{9,10},{10,... | collective-permute-start | bytes 442376 | tf_op jit(solution)/shard_map/ppermute | solution.py:213
  5.5 2.5 %collective-permute-start.8 = (bf16[3,64,384]{2,1,0:T(8,128)(2,1)S(1)}, bf16[3,64,384]{2,1,0:T(8,128)(2,1)S(1)}, u32[]{:S(2)}, u32[]{:S(2)}) collective-permute-start(bf16[3,64,384]{2,1,0:T(8,128)(2,1)S(1)} %get-tuple-element.61), channel_id=1, source_target_pairs={{0,1},{1,0},{2,3},{3,2},{4,5},{5,4},{6,7},{7,6},{8,9},{9,8},{10,11... | collective-permute-start | bytes 442376 | tf_op jit(solution)/shard_map/ppermute | solution.py:213
  8.0 2.3 %shard_map.59 = (bf16[3,64,384]{2,1,0:T(8,128)(2,1)}, bf16[3,64,384]{2,1,0:T(8,128)(2,1)}, bf16[3,64,384]{2,1,0:T(8,128)(2,1)}) custom-call(bf16[128,1536]{1,0:T(8,128)(2,1)} %refs_0_.3, bf16[128,1536]{1,0:T(8,128)(2,1)} %refs_1_.3, bf16[128,1536]{1,0:T(8,128)(2,1)} %refs_2_.3), custom_call_target="tpu_custom_call" | custom-call | bytes 1622016 | tf_op jit(solution)/shard_map/pallas_call | solution.py:29
  10.4 0.8 %collective-permute-start = (bf16[3,64,384]{2,1,0:T(8,128)(2,1)}, bf16[3,64,384]{2,1,0:T(8,128)(2,1)S(1)}, u32[]{:S(2)}, u32[]{:S(2)}) collective-permute-start(bf16[3,64,384]{2,1,0:T(8,128)(2,1)} %get-tuple-element.42), channel_id=1, source_target_pairs={{0,1},{1,0},{2,3},{3,2},{4,5},{5,4},{6,7},{7,6},{8,9},{9,8},{10,11... | collective-permute-start | bytes 442376 | tf_op jit(solution)/shard_map/ppermute | solution.py:213
  11.2 2.2 %collective-permute-start.1 = (bf16[3,64,384]{2,1,0:T(8,128)(2,1)}, bf16[3,64,384]{2,1,0:T(8,128)(2,1)S(1)}, u32[]{:S(2)}, u32[]{:S(2)}) collective-permute-start(bf16[3,64,384]{2,1,0:T(8,128)(2,1)} %get-tuple-element.43), channel_id=1, source_target_pairs={{0,2},{1,3},{2,0},{3,1},{4,6},{5,7},{6,4},{7,5},{8,10},{9,11},{10,... | collective-permute-start | bytes 442376 | tf_op jit(solution)/shard_map/ppermute | solution.py:213
  13.4 1.3 %collective-permute-done.10.refs_3_ = bf16[3,64,384]{2,1,0:T(8,128)(2,1)S(1)} collective-permute-done((bf16[3,64,384]{2,1,0:T(8,128)(2,1)S(1)}, bf16[3,64,384]{2,1,0:T(8,128)(2,1)S(1)}, u32[]{:S(2)}, u32[]{:S(2)}) %collective-permute-start.10) | collective-permute-done | bytes 147488 | tf_op jit(solution)/shard_map/ppermute | solution.py:213
  14.7 1.0 %collective-permute-start.2 = (bf16[3,64,384]{2,1,0:T(8,128)(2,1)}, bf16[3,64,384]{2,1,0:T(8,128)(2,1)S(1)}, u32[]{:S(2)}, u32[]{:S(2)}) collective-permute-start(bf16[3,64,384]{2,1,0:T(8,128)(2,1)} %get-tuple-element.44), channel_id=1, source_target_pairs={{0,3},{1,2},{2,1},{3,0},{4,7},{5,6},{6,5},{7,4},{8,11},{9,10},{10,... | collective-permute-start | bytes 442376 | tf_op jit(solution)/shard_map/ppermute | solution.py:213
  15.9 3.4 %collective-permute-done.9.refs_2_ = bf16[3,64,384]{2,1,0:T(8,128)(2,1)S(1)} collective-permute-done((bf16[3,64,384]{2,1,0:T(8,128)(2,1)S(1)}, bf16[3,64,384]{2,1,0:T(8,128)(2,1)S(1)}, u32[]{:S(2)}, u32[]{:S(2)}) %collective-permute-start.9) | collective-permute-done | bytes 147488 | tf_op jit(solution)/shard_map/ppermute | solution.py:213
  19.3 1.9 %collective-permute-start.11 = (bf16[2,2,64,384]{3,2,1,0:T(8,128)(2,1)S(1)}, bf16[2,2,64,384]{3,2,1,0:T(8,128)(2,1)S(1)}, u32[]{:S(2)}, u32[]{:S(2)}) collective-permute-start(bf16[2,2,64,384]{3,2,1,0:T(8,128)(2,1)S(1)} %pad_maximum_fusion.1), channel_id=1, source_target_pairs={{0,4},{4,8},{8,12},{12,16},{16,20},{20,24},{24,28},{1,5},{5,9},{9,... | collective-permute-start | bytes 589832 | tf_op jit(solution)/shard_map/ppermute | solution.py:471
  21.3 1.0 %collective-permute-done.refs_1_ = bf16[3,64,384]{2,1,0:T(8,128)(2,1)S(1)} collective-permute-done((bf16[3,64,384]{2,1,0:T(8,128)(2,1)}, bf16[3,64,384]{2,1,0:T(8,128)(2,1)S(1)}, u32[]{:S(2)}, u32[]{:S(2)}) %collective-permute-start) | collective-permute-done | bytes 147488 | tf_op jit(solution)/shard_map/ppermute | solution.py:213
  22.2 6.6 %collective-permute-done.1.refs_2_ = bf16[3,64,384]{2,1,0:T(8,128)(2,1)S(1)} collective-permute-done((bf16[3,64,384]{2,1,0:T(8,128)(2,1)}, bf16[3,64,384]{2,1,0:T(8,128)(2,1)S(1)}, u32[]{:S(2)}, u32[]{:S(2)}) %collective-permute-start.1) | collective-permute-done | bytes 147488 | tf_op jit(solution)/shard_map/ppermute | solution.py:213
  28.9 2.8 %collective-permute-done.2.refs_3_ = bf16[3,64,384]{2,1,0:T(8,128)(2,1)S(1)} collective-permute-done((bf16[3,64,384]{2,1,0:T(8,128)(2,1)}, bf16[3,64,384]{2,1,0:T(8,128)(2,1)S(1)}, u32[]{:S(2)}, u32[]{:S(2)}) %collective-permute-start.2) | collective-permute-done | bytes 147488 | tf_op jit(solution)/shard_map/ppermute | solution.py:213
  31.8 1.9 %collective-permute-start.3 = (bf16[2,2,64,384]{3,2,1,0:T(8,128)(2,1)S(1)}, bf16[2,2,64,384]{3,2,1,0:T(8,128)(2,1)S(1)}, u32[]{:S(2)}, u32[]{:S(2)}) collective-permute-start(bf16[2,2,64,384]{3,2,1,0:T(8,128)(2,1)S(1)} %pad_maximum_fusion), channel_id=1, source_target_pairs={{0,4},{4,8},{8,12},{12,16},{16,20},{20,24},{24,28},{1,5},{5,9},{9,... | collective-permute-start | bytes 589832 | tf_op jit(solution)/shard_map/ppermute | solution.py:471
  33.7 1.0 %shard_map.64 = (bf16[512,192]{1,0:T(8,128)(2,1)S(1)}, bf16[512,192]{1,0:T(8,128)(2,1)S(1)}, bf16[512,192]{1,0:T(8,128)(2,1)S(1)}, bf16[512,192]{1,0:T(8,128)(2,1)S(1)}) custom-call(bf16[3,64,384]{2,1,0:T(8,128)(2,1)S(1)} %get-tuple-element.60.refs_0_, bf16[3,64,384]{2,1,0:T(8,128)(2,1)S(1)} %collective-permute-done.8.refs_1_, ...), custom_call_target="tpu_custom_call" | custom-call | flops 201326592 | bytes 1376256 | tf_op jit(solution)/shard_map/pallas_call | solution.py:29
  34.8 1.5 %shard_map.65 = (bf16[256,192]{1,0:T(8,128)(2,1)S(1)}, f32[256,192]{1,0:T(8,128)S(1)}, f32[256,192]{1,0:T(8,128)S(1)}, bf16[2,2,64,384]{3,2,1,0:T(8,128)(2,1)S(1)}) custom-call(bf16[512,192]{1,0:T(8,128)(2,1)S(1)} %get-tuple-element.64.q_ref, bf16[512,192]{1,0:T(8,128)(2,1)S(1)} %get-tuple-element.65.k_ref, bf16[512,192]{1,0:T(8,128)(2,1)S(1)} %get-tuple-element.66.v_ref, ...), custom_call_target="tpu_custom_call" | custom-call | flops 301989888 | bytes 1671168 | tf_op jit(solution)/shard_map/pallas_call | solution.py:29
  36.3 4.5 %collective-permute-start.12 = (bf16[2,2,64,384]{3,2,1,0:T(8,128)(2,1)S(1)}, bf16[2,2,64,384]{3,2,1,0:T(8,128)(2,1)S(1)}, u32[]{:S(2)}, u32[]{:S(2)}) collective-permute-start(bf16[2,2,64,384]{3,2,1,0:T(8,128)(2,1)S(1)} %get-tuple-element.74), channel_id=1, source_target_pairs={{4,0},{8,4},{12,8},{16,12},{20,16},{24,20},{28,24},{5,1},{9,5},{13... | collective-permute-start | bytes 589832 | tf_op jit(solution)/shard_map/ppermute | solution.py:474
  40.8 1.0 %shard_map.60 = (bf16[512,192]{1,0:T(8,128)(2,1)S(1)}, bf16[512,192]{1,0:T(8,128)(2,1)S(1)}, bf16[512,192]{1,0:T(8,128)(2,1)S(1)}, bf16[512,192]{1,0:T(8,128)(2,1)S(1)}) custom-call(bf16[3,64,384]{2,1,0:T(8,128)(2,1)S(1)} %get-tuple-element.41.refs_0_, bf16[3,64,384]{2,1,0:T(8,128)(2,1)S(1)} %collective-permute-done.refs_1_, ...), custom_call_target="tpu_custom_call" | custom-call | flops 201326592 | bytes 1376256 | tf_op jit(solution)/shard_map/pallas_call | solution.py:29
  41.9 1.5 %shard_map.61 = (bf16[256,192]{1,0:T(8,128)(2,1)S(1)}, f32[256,192]{1,0:T(8,128)S(1)}, f32[256,192]{1,0:T(8,128)S(1)}, bf16[2,2,64,384]{3,2,1,0:T(8,128)(2,1)S(1)}) custom-call(bf16[512,192]{1,0:T(8,128)(2,1)S(1)} %get-tuple-element.45.q_ref, bf16[512,192]{1,0:T(8,128)(2,1)S(1)} %get-tuple-element.46.k_ref, bf16[512,192]{1,0:T(8,128)(2,1)S(1)} %get-tuple-element.47.v_ref, ...), custom_call_target="tpu_custom_call" | custom-call | flops 301989888 | bytes 1671168 | tf_op jit(solution)/shard_map/pallas_call | solution.py:29
  43.4 1.9 %collective-permute-start.4 = (bf16[2,2,64,384]{3,2,1,0:T(8,128)(2,1)S(1)}, bf16[2,2,64,384]{3,2,1,0:T(8,128)(2,1)S(1)}, u32[]{:S(2)}, u32[]{:S(2)}) collective-permute-start(bf16[2,2,64,384]{3,2,1,0:T(8,128)(2,1)S(1)} %get-tuple-element.55), channel_id=1, source_target_pairs={{4,0},{8,4},{12,8},{16,12},{20,16},{24,20},{28,24},{5,1},{9,5},{13... | collective-permute-start | bytes 589832 | tf_op jit(solution)/shard_map/ppermute | solution.py:474
  45.3 1.4 %shard_map.66 = (bf16[256,192]{1,0:T(8,128)(2,1)S(1)}, f32[512,192]{1,0:T(8,128)S(1)}, f32[512,192]{1,0:T(8,128)S(1)}) custom-call(bf16[512,192]{1,0:T(8,128)(2,1)S(1)} %get-tuple-element.64.q_ref, bf16[512,192]{1,0:T(8,128)(2,1)S(1)} %get-tuple-element.65.k_ref, bf16[512,192]{1,0:T(8,128)(2,1)S(1)} %get-tuple-element.66.v_ref, ...), custom_call_target="tpu_custom_call" | custom-call | flops 301989888 | bytes 2064384 | tf_op jit(solution)/shard_map/pallas_call | solution.py:29
  47.1 1.4 %shard_map.62 = (bf16[256,192]{1,0:T(8,128)(2,1)S(1)}, f32[512,192]{1,0:T(8,128)S(1)}, f32[512,192]{1,0:T(8,128)S(1)}) custom-call(bf16[512,192]{1,0:T(8,128)(2,1)S(1)} %get-tuple-element.45.q_ref, bf16[512,192]{1,0:T(8,128)(2,1)S(1)} %get-tuple-element.46.k_ref, bf16[512,192]{1,0:T(8,128)(2,1)S(1)} %get-tuple-element.47.v_ref, ...), custom_call_target="tpu_custom_call" | custom-call | flops 301989888 | bytes 2064384 | tf_op jit(solution)/shard_map/pallas_call | solution.py:29
  48.5 3.1 %collective-permute-start.14 = (bf16[3,64,384]{2,1,0:T(8,128)(2,1)S(1)}, bf16[3,64,384]{2,1,0:T(8,128)(2,1)S(1)}, u32[]{:S(2)}, u32[]{:S(2)}) collective-permute-start(bf16[3,64,384]{2,1,0:T(8,128)(2,1)S(1)} %get-tuple-element.77), channel_id=1, source_target_pairs={{0,2},{1,3},{2,0},{3,1},{4,6},{5,7},{6,4},{7,5},{8,10},{9,11},{10,... | collective-permute-start | bytes 442376 | tf_op jit(solution)/shard_map/ppermute | solution.py:213
  52.3 1.1 %collective-permute-start.5 = (bf16[3,64,384]{2,1,0:T(8,128)(2,1)S(1)}, bf16[3,64,384]{2,1,0:T(8,128)(2,1)S(1)}, u32[]{:S(2)}, u32[]{:S(2)}) collective-permute-start(bf16[3,64,384]{2,1,0:T(8,128)(2,1)S(1)} %get-tuple-element.57), channel_id=1, source_target_pairs={{0,1},{1,0},{2,3},{3,2},{4,5},{5,4},{6,7},{7,6},{8,9},{9,8},{10,11... | collective-permute-start | bytes 442376 | tf_op jit(solution)/shard_map/ppermute | solution.py:213
  53.5 1.9 %collective-permute-start.6 = (bf16[3,64,384]{2,1,0:T(8,128)(2,1)S(1)}, bf16[3,64,384]{2,1,0:T(8,128)(2,1)S(1)}, u32[]{:S(2)}, u32[]{:S(2)}) collective-permute-start(bf16[3,64,384]{2,1,0:T(8,128)(2,1)S(1)} %get-tuple-element.58), channel_id=1, source_target_pairs={{0,2},{1,3},{2,0},{3,1},{4,6},{5,7},{6,4},{7,5},{8,10},{9,11},{10,... | collective-permute-start | bytes 442376 | tf_op jit(solution)/shard_map/ppermute | solution.py:213
  55.9 5.8 %collective-permute-done.14.refs_6_ = bf16[3,64,384]{2,1,0:T(8,128)(2,1)S(1)} collective-permute-done((bf16[3,64,384]{2,1,0:T(8,128)(2,1)S(1)}, bf16[3,64,384]{2,1,0:T(8,128)(2,1)S(1)}, u32[]{:S(2)}, u32[]{:S(2)}) %collective-permute-start.14) | collective-permute-done | bytes 147488 | tf_op jit(solution)/shard_map/ppermute | solution.py:213
  61.7 10.9 %collective-permute-done.15.refs_7_ = bf16[3,64,384]{2,1,0:T(8,128)(2,1)S(1)} collective-permute-done((bf16[3,64,384]{2,1,0:T(8,128)(2,1)S(1)}, bf16[3,64,384]{2,1,0:T(8,128)(2,1)S(1)}, u32[]{:S(2)}, u32[]{:S(2)}) %collective-permute-start.15) | collective-permute-done | bytes 147488 | tf_op jit(solution)/shard_map/ppermute | solution.py:213
  72.6 1.8 %collective-permute-done.6.refs_2_ = bf16[3,64,384]{2,1,0:T(8,128)(2,1)S(1)} collective-permute-done((bf16[3,64,384]{2,1,0:T(8,128)(2,1)S(1)}, bf16[3,64,384]{2,1,0:T(8,128)(2,1)S(1)}, u32[]{:S(2)}, u32[]{:S(2)}) %collective-permute-start.6) | collective-permute-done | bytes 147488 | tf_op jit(solution)/shard_map/ppermute | solution.py:213
  74.4 3.7 %collective-permute-done.7.refs_3_ = bf16[3,64,384]{2,1,0:T(8,128)(2,1)S(1)} collective-permute-done((bf16[3,64,384]{2,1,0:T(8,128)(2,1)S(1)}, bf16[3,64,384]{2,1,0:T(8,128)(2,1)S(1)}, u32[]{:S(2)}, u32[]{:S(2)}) %collective-permute-start.7) | collective-permute-done | bytes 147488 | tf_op jit(solution)/shard_map/ppermute | solution.py:213
  78.2 1.4 %shard_map.68 = (bf16[128,1536]{1,0:T(8,128)(2,1)}, bf16[128,1536]{1,0:T(8,128)(2,1)}, bf16[128,1536]{1,0:T(8,128)(2,1)}) custom-call(bf16[3,64,384]{2,1,0:T(8,128)(2,1)S(1)} %get-tuple-element.56.refs_0_, bf16[3,64,384]{2,1,0:T(8,128)(2,1)S(1)} %collective-permute-done.5.refs_1_, bf16[3,64,384]{2,1,0:T(8,128)(2,1)S(1)} %collective-permute-done.6.refs_2_, ...), custom_call_target="tpu_custom_call" | custom-call | bytes 2359296 | tf_op jit(solution)/shard_map/pallas_call | solution.py:29
  (21 shorter events, 2.1 us)
Async XLA Ops:
  0.6 1.0 %copy-start = (bf16[128,1536]{1,0:T(8,128)(2,1)S(1)}, bf16[128,1536]{1,0:T(8,128)(2,1)}, u32[]{:S(2)}) copy-start(bf16[128,1536]{1,0:T(8,128)(2,1)} %refs_0_.3) | copy-start | bytes 1179652
  1.6 1.0 %copy-start.1 = (bf16[128,1536]{1,0:T(8,128)(2,1)S(1)}, bf16[128,1536]{1,0:T(8,128)(2,1)}, u32[]{:S(2)}) copy-start(bf16[128,1536]{1,0:T(8,128)(2,1)} %refs_1_.3) | copy-start | bytes 1179652
  2.6 1.0 %copy-start.2 = (bf16[128,1536]{1,0:T(8,128)(2,1)S(1)}, bf16[128,1536]{1,0:T(8,128)(2,1)}, u32[]{:S(2)}) copy-start(bf16[128,1536]{1,0:T(8,128)(2,1)} %refs_2_.3) | copy-start | bytes 1179652
  3.9 10.8 %collective-permute-start.10 = (bf16[3,64,384]{2,1,0:T(8,128)(2,1)S(1)}, bf16[3,64,384]{2,1,0:T(8,128)(2,1)S(1)}, u32[]{:S(2)}, u32[]{:S(2)}) collective-permute-start(bf16[3,64,384]{2,1,0:T(8,128)(2,1)S(1)} %get-tuple-element.63), channel_id=1, source_target_pairs={{0,3},{1,2},{2,1},{3,0},{4,7},{5,6},{6,5},{7,4},{8,11},{9,10},{10,... | collective-permute-start | bytes 442376 | tf_op jit(solution)/shard_map/ppermute | solution.py:213
  5.5 10.3 %collective-permute-start.8 = (bf16[3,64,384]{2,1,0:T(8,128)(2,1)S(1)}, bf16[3,64,384]{2,1,0:T(8,128)(2,1)S(1)}, u32[]{:S(2)}, u32[]{:S(2)}) collective-permute-start(bf16[3,64,384]{2,1,0:T(8,128)(2,1)S(1)} %get-tuple-element.61), channel_id=1, source_target_pairs={{0,1},{1,0},{2,3},{3,2},{4,5},{5,4},{6,7},{7,6},{8,9},{9,8},{10,11... | collective-permute-start | bytes 442376 | tf_op jit(solution)/shard_map/ppermute | solution.py:213
  8.0 11.2 %collective-permute-start.9 = (bf16[3,64,384]{2,1,0:T(8,128)(2,1)S(1)}, bf16[3,64,384]{2,1,0:T(8,128)(2,1)S(1)}, u32[]{:S(2)}, u32[]{:S(2)}) collective-permute-start(bf16[3,64,384]{2,1,0:T(8,128)(2,1)S(1)} %get-tuple-element.62), channel_id=1, source_target_pairs={{0,2},{1,3},{2,0},{3,1},{4,6},{5,7},{6,4},{7,5},{8,10},{9,11},{10,... | collective-permute-start | bytes 442376 | tf_op jit(solution)/shard_map/ppermute | solution.py:213
  10.4 11.9 %collective-permute-start = (bf16[3,64,384]{2,1,0:T(8,128)(2,1)}, bf16[3,64,384]{2,1,0:T(8,128)(2,1)S(1)}, u32[]{:S(2)}, u32[]{:S(2)}) collective-permute-start(bf16[3,64,384]{2,1,0:T(8,128)(2,1)} %get-tuple-element.42), channel_id=1, source_target_pairs={{0,1},{1,0},{2,3},{3,2},{4,5},{5,4},{6,7},{7,6},{8,9},{9,8},{10,11... | collective-permute-start | bytes 442376 | tf_op jit(solution)/shard_map/ppermute | solution.py:213
  11.2 17.7 %collective-permute-start.1 = (bf16[3,64,384]{2,1,0:T(8,128)(2,1)}, bf16[3,64,384]{2,1,0:T(8,128)(2,1)S(1)}, u32[]{:S(2)}, u32[]{:S(2)}) collective-permute-start(bf16[3,64,384]{2,1,0:T(8,128)(2,1)} %get-tuple-element.43), channel_id=1, source_target_pairs={{0,2},{1,3},{2,0},{3,1},{4,6},{5,7},{6,4},{7,5},{8,10},{9,11},{10,... | collective-permute-start | bytes 442376 | tf_op jit(solution)/shard_map/ppermute | solution.py:213
  14.7 17.0 %collective-permute-start.2 = (bf16[3,64,384]{2,1,0:T(8,128)(2,1)}, bf16[3,64,384]{2,1,0:T(8,128)(2,1)S(1)}, u32[]{:S(2)}, u32[]{:S(2)}) collective-permute-start(bf16[3,64,384]{2,1,0:T(8,128)(2,1)} %get-tuple-element.44), channel_id=1, source_target_pairs={{0,3},{1,2},{2,1},{3,0},{4,7},{5,6},{6,5},{7,4},{8,11},{9,10},{10,... | collective-permute-start | bytes 442376 | tf_op jit(solution)/shard_map/ppermute | solution.py:213
  19.3 15.4 %collective-permute-start.11 = (bf16[2,2,64,384]{3,2,1,0:T(8,128)(2,1)S(1)}, bf16[2,2,64,384]{3,2,1,0:T(8,128)(2,1)S(1)}, u32[]{:S(2)}, u32[]{:S(2)}) collective-permute-start(bf16[2,2,64,384]{3,2,1,0:T(8,128)(2,1)S(1)} %pad_maximum_fusion.1), channel_id=1, source_target_pairs={{0,4},{4,8},{8,12},{12,16},{16,20},{20,24},{24,28},{1,5},{5,9},{9,... | collective-permute-start | bytes 589832 | tf_op jit(solution)/shard_map/ppermute | solution.py:471
  31.8 10.1 %collective-permute-start.3 = (bf16[2,2,64,384]{3,2,1,0:T(8,128)(2,1)S(1)}, bf16[2,2,64,384]{3,2,1,0:T(8,128)(2,1)S(1)}, u32[]{:S(2)}, u32[]{:S(2)}) collective-permute-start(bf16[2,2,64,384]{3,2,1,0:T(8,128)(2,1)S(1)} %pad_maximum_fusion), channel_id=1, source_target_pairs={{0,4},{4,8},{8,12},{12,16},{16,20},{20,24},{24,28},{1,5},{5,9},{9,... | collective-permute-start | bytes 589832 | tf_op jit(solution)/shard_map/ppermute | solution.py:471
  36.3 10.5 %collective-permute-start.12 = (bf16[2,2,64,384]{3,2,1,0:T(8,128)(2,1)S(1)}, bf16[2,2,64,384]{3,2,1,0:T(8,128)(2,1)S(1)}, u32[]{:S(2)}, u32[]{:S(2)}) collective-permute-start(bf16[2,2,64,384]{3,2,1,0:T(8,128)(2,1)S(1)} %get-tuple-element.74), channel_id=1, source_target_pairs={{4,0},{8,4},{12,8},{16,12},{20,16},{24,20},{28,24},{5,1},{9,5},{13... | collective-permute-start | bytes 589832 | tf_op jit(solution)/shard_map/ppermute | solution.py:474
  43.4 8.7 %collective-permute-start.4 = (bf16[2,2,64,384]{3,2,1,0:T(8,128)(2,1)S(1)}, bf16[2,2,64,384]{3,2,1,0:T(8,128)(2,1)S(1)}, u32[]{:S(2)}, u32[]{:S(2)}) collective-permute-start(bf16[2,2,64,384]{3,2,1,0:T(8,128)(2,1)S(1)} %get-tuple-element.55), channel_id=1, source_target_pairs={{4,0},{8,4},{12,8},{16,12},{20,16},{24,20},{28,24},{5,1},{9,5},{13... | collective-permute-start | bytes 589832 | tf_op jit(solution)/shard_map/ppermute | solution.py:474
  47.0 8.4 %collective-permute-start.13 = (bf16[3,64,384]{2,1,0:T(8,128)(2,1)S(1)}, bf16[3,64,384]{2,1,0:T(8,128)(2,1)S(1)}, u32[]{:S(2)}, u32[]{:S(2)}) collective-permute-start(bf16[3,64,384]{2,1,0:T(8,128)(2,1)S(1)} %get-tuple-element.76), channel_id=1, source_target_pairs={{0,1},{1,0},{2,3},{3,2},{4,5},{5,4},{6,7},{7,6},{8,9},{9,8},{10,11... | collective-permute-start | bytes 442376 | tf_op jit(solution)/shard_map/ppermute | solution.py:213
  48.5 13.1 %collective-permute-start.14 = (bf16[3,64,384]{2,1,0:T(8,128)(2,1)S(1)}, bf16[3,64,384]{2,1,0:T(8,128)(2,1)S(1)}, u32[]{:S(2)}, u32[]{:S(2)}) collective-permute-start(bf16[3,64,384]{2,1,0:T(8,128)(2,1)S(1)} %get-tuple-element.77), channel_id=1, source_target_pairs={{0,2},{1,3},{2,0},{3,1},{4,6},{5,7},{6,4},{7,5},{8,10},{9,11},{10,... | collective-permute-start | bytes 442376 | tf_op jit(solution)/shard_map/ppermute | solution.py:213
  51.6 21.0 %collective-permute-start.15 = (bf16[3,64,384]{2,1,0:T(8,128)(2,1)S(1)}, bf16[3,64,384]{2,1,0:T(8,128)(2,1)S(1)}, u32[]{:S(2)}, u32[]{:S(2)}) collective-permute-start(bf16[3,64,384]{2,1,0:T(8,128)(2,1)S(1)} %get-tuple-element.78), channel_id=1, source_target_pairs={{0,3},{1,2},{2,1},{3,0},{4,7},{5,6},{6,5},{7,4},{8,11},{9,10},{10,... | collective-permute-start | bytes 442376 | tf_op jit(solution)/shard_map/ppermute | solution.py:213
  52.3 20.3 %collective-permute-start.5 = (bf16[3,64,384]{2,1,0:T(8,128)(2,1)S(1)}, bf16[3,64,384]{2,1,0:T(8,128)(2,1)S(1)}, u32[]{:S(2)}, u32[]{:S(2)}) collective-permute-start(bf16[3,64,384]{2,1,0:T(8,128)(2,1)S(1)} %get-tuple-element.57), channel_id=1, source_target_pairs={{0,1},{1,0},{2,3},{3,2},{4,5},{5,4},{6,7},{7,6},{8,9},{9,8},{10,11... | collective-permute-start | bytes 442376 | tf_op jit(solution)/shard_map/ppermute | solution.py:213
  53.5 21.0 %collective-permute-start.6 = (bf16[3,64,384]{2,1,0:T(8,128)(2,1)S(1)}, bf16[3,64,384]{2,1,0:T(8,128)(2,1)S(1)}, u32[]{:S(2)}, u32[]{:S(2)}) collective-permute-start(bf16[3,64,384]{2,1,0:T(8,128)(2,1)S(1)} %get-tuple-element.58), channel_id=1, source_target_pairs={{0,2},{1,3},{2,0},{3,1},{4,6},{5,7},{6,4},{7,5},{8,10},{9,11},{10,... | collective-permute-start | bytes 442376 | tf_op jit(solution)/shard_map/ppermute | solution.py:213
  55.4 22.8 %collective-permute-start.7 = (bf16[3,64,384]{2,1,0:T(8,128)(2,1)S(1)}, bf16[3,64,384]{2,1,0:T(8,128)(2,1)S(1)}, u32[]{:S(2)}, u32[]{:S(2)}) collective-permute-start(bf16[3,64,384]{2,1,0:T(8,128)(2,1)S(1)} %get-tuple-element.59), channel_id=1, source_target_pairs={{0,3},{1,2},{2,1},{3,0},{4,7},{5,6},{6,5},{7,4},{8,11},{9,10},{10,... | collective-permute-start | bytes 442376 | tf_op jit(solution)/shard_map/ppermute | solution.py:213

commit v5 on v4

--- a/solution.py
+++ b/solution.py
@@ -12,7 +12,6 @@
 HEADS = 16
 WINDOW = 256
 CHUNKS = 2
-PACK_MIB = 58
 NEGATIVE = -1e30
 LOG2E = math.log2(math.e)
 BF16 = jnp.bfloat16
@@ -23,7 +22,7 @@
 HBM_SPEC = pl.BlockSpec(memory_space=pltpu.HBM)
 
 
-def call(kernel, arrays, outs, scratch=(), flops=0, spec=VMEM_SPEC, out_spec=VMEM_SPEC, vmem=48):
+def call(kernel, arrays, outs, scratch=(), flops=0, spec=VMEM_SPEC, out_spec=VMEM_SPEC):
     moved = sum(a.size * a.dtype.itemsize for a in arrays)
     moved += sum(math.prod(o.shape) * o.dtype.itemsize for o in outs)
     return pl.pallas_call(
@@ -33,7 +32,7 @@
         out_specs=tuple([out_spec] * len(outs)),
         scratch_shapes=list(scratch),
         cost_estimate=pl.CostEstimate(flops=flops, bytes_accessed=moved, transcendentals=0),
-        compiler_params=pltpu.CompilerParams(vmem_limit_bytes=vmem * 1024 * 1024),
+        compiler_params=pltpu.CompilerParams(vmem_limit_bytes=48 * 1024 * 1024),
     )(*arrays)
 
 
@@ -90,31 +89,21 @@
     return folded(x[:, chunk * plan.chunk_width : (chunk + 1) * plan.chunk_width], plan)
 
 
-def pack_first_kernel(plan, *refs):
-    me = lax.axis_index("dev")
-    in_refs, out_refs, (held, made, in_sems, out_sems) = refs[:3], refs[3:-4], refs[-4:]
-    steps = range(plan.devs - 1, 0, -1)
-
-    def taken(step, at):
-        start = pl.multiple_of((me ^ step) * plan.local_width, 128)
+def pack_first_kernel(plan, steps, *refs):
+    me = lax.axis_index("dev")
+    in_refs, out_refs, (held, sems) = refs[:3], refs[3:-2], refs[-2:]
+
+    def taken(i, at):
+        start = pl.multiple_of((me ^ steps[i]) * plan.local_width, 128)
         block = in_refs[at].at[:, pl.ds(start, plan.local_width)]
-        return pltpu.make_async_copy(block, held.at[step - 1, at], in_sems.at[step - 1, at])
-
-    def given(step):
-        return pltpu.make_async_copy(
-            made.at[step - 1], out_refs[step - 1], out_sems.at[step - 1]
-        )
-
-    for step in steps:
-        for at in range(3):
-            taken(step, at).start()
-    for step in steps:
-        for at in range(3):
-            taken(step, at).wait()
-            made[step - 1, at] = columns_of(held[step - 1, at], 0, plan)
-        given(step).start()
-    for step in steps:
-        given(step).wait()
+        return pltpu.make_async_copy(block, held.at[i, at], sems.at[i, at])
+
+    each = [(i, at) for i in range(len(steps)) for at in range(3)]
+    for i, at in each:
+        taken(i, at).start()
+    for i, at in each:
+        taken(i, at).wait()
+        out_refs[i][at] = columns_of(held[i, at], 0, plan)
 
 
 def pack_rest_kernel(plan, chunk, *refs):
@@ -133,18 +122,19 @@
     piece = shape((3,) + plan.piece)
     chunks = []
     if plan.local_width % 128 == 0 and plan.chunks > 1:
-        others = plan.devs - 1
-        scratch = [
-            pltpu.VMEM((others, 3, plan.rows, plan.local_width), BF16),
-            pltpu.VMEM((others, 3) + plan.piece, BF16),
-            pltpu.SemaphoreType.DMA((others, 3)),
-            pltpu.SemaphoreType.DMA((others,)),
-        ]
-        kernel = functools.partial(pack_first_kernel, plan)
-        sent = call(
-            kernel, arrays, [piece] * others, scratch, spec=HBM_SPEC, out_spec=HBM_SPEC, vmem=PACK_MIB
-        )
-        chunks.append([None] + list(sent))
+        sent = [None] * plan.devs
+        far_away = plan.devs - 1
+        held = [pltpu.with_memory_space_constraint(a, pltpu.HBM) for a in arrays]
+        for steps in ([far_away], list(range(far_away - 1, 0, -1))):
+            scratch = [
+                pltpu.VMEM((len(steps), 3, plan.rows, plan.local_width), BF16),
+                pltpu.SemaphoreType.DMA((len(steps), 3)),
+            ]
+            kernel = functools.partial(pack_first_kernel, plan, steps)
+            got = call(kernel, held, [piece] * len(steps), scratch, spec=HBM_SPEC)
+            for step, x in zip(steps, got):
+                sent[step] = x
+        chunks.append(sent)
         for chunk in range(1, plan.chunks):
             kernel = functools.partial(pack_rest_kernel, plan, chunk)
             got = list(call(kernel, arrays, [piece] * (plan.devs + (chunk == 1))))

time: 80 us -> 80 us (level)
    pallas_call x11 -> x12, Pallas kernels: 12.5 us -> 12.7 us  [call(): pl.pallas_call(kernel, out_shape=tuple(outs), in_specs=[spec] * len(array...]
where the time goes in v5:
time: 80 us; the launch traced here: 79.6 us
  waiting for transfers between devices  37.4 us (47%)
  starting transfers between devices  25.6 us (32%)
  Pallas kernels  12.7 us (16%)
  local copies, waits for them, and re-layouts  2.98 us (4%)
  between operations  0.8 us (1%)
    ppermute x12, waiting for transfers between devices, exchange(): got[step] = lax.ppermute(pieces[step], 'dev', pairs)  37.4 us
    ppermute x12, starting transfers between devices, exchange(): got[step] = lax.ppermute(pieces[step], 'dev', pairs)  15.3 us
    pallas_call x12, Pallas kernels, call(): pl.pallas_call(kernel, out_shape=tuple(outs), in_specs=[spec] * len(array...  12.7 us
    ppermute x2, starting transfers between devices, local(): far = lax.ppermute(far, 'seg', backward)  6.46 us
    ppermute x2, starting transfers between devices, local(): halo = lax.ppermute(halo, 'seg', onward)  3.84 us
    unnamed x6, local copies, waits for them, and re-layouts  2.98 us
  transfers between devices with their start and end apart: 16, of which 10 were waited for; matrix products, arithmetic and copies ran while one was open for 0% of the time, Pallas kernels for 14%

profile of v5, /device:TPU:12, one launch (start us, length us, event | category | flops | bytes accessed | tf_op | source)
XLA Modules:
  0.0 79.6 jit_solution(3667251383499681861)
XLA Ops:
  0.6 1.0 %copy-done = bf16[128,1536]{1,0:T(8,128)(2,1)S(1)} copy-done((bf16[128,1536]{1,0:T(8,128)(2,1)S(1)}, bf16[128,1536]{1,0:T(8,128)(2,1)}, u32[]{:S(2)}) %copy-start) | copy-done | bytes 393240
  1.6 1.0 %copy-done.1 = bf16[128,1536]{1,0:T(8,128)(2,1)S(1)} copy-done((bf16[128,1536]{1,0:T(8,128)(2,1)S(1)}, bf16[128,1536]{1,0:T(8,128)(2,1)}, u32[]{:S(2)}) %copy-start.1) | copy-done | bytes 393240
  2.6 1.0 %copy-done.2 = bf16[128,1536]{1,0:T(8,128)(2,1)S(1)} copy-done((bf16[128,1536]{1,0:T(8,128)(2,1)S(1)}, bf16[128,1536]{1,0:T(8,128)(2,1)}, u32[]{:S(2)}) %copy-start.2) | copy-done | bytes 393240
  3.9 1.6 %collective-permute-start.10 = (bf16[3,64,384]{2,1,0:T(8,128)(2,1)S(1)}, bf16[3,64,384]{2,1,0:T(8,128)(2,1)S(1)}, u32[]{:S(2)}, u32[]{:S(2)}) collective-permute-start(bf16[3,64,384]{2,1,0:T(8,128)(2,1)S(1)} %get-tuple-element.61), channel_id=1, source_target_pairs={{0,3},{1,2},{2,1},{3,0},{4,7},{5,6},{6,5},{7,4},{8,11},{9,10},{10,... | collective-permute-start | bytes 442376 | tf_op jit(solution)/shard_map/ppermute | solution.py:203
  5.5 2.5 %collective-permute-start.8 = (bf16[3,64,384]{2,1,0:T(8,128)(2,1)S(1)}, bf16[3,64,384]{2,1,0:T(8,128)(2,1)S(1)}, u32[]{:S(2)}, u32[]{:S(2)}) collective-permute-start(bf16[3,64,384]{2,1,0:T(8,128)(2,1)S(1)} %get-tuple-element.59), channel_id=1, source_target_pairs={{0,1},{1,0},{2,3},{3,2},{4,5},{5,4},{6,7},{7,6},{8,9},{9,8},{10,11... | collective-permute-start | bytes 442376 | tf_op jit(solution)/shard_map/ppermute | solution.py:203
  8.0 1.4 %shard_map.59 = (bf16[3,64,384]{2,1,0:T(8,128)(2,1)S(1)}, bf16[3,64,384]{2,1,0:T(8,128)(2,1)S(1)}) custom-call(bf16[128,1536]{1,0:T(8,128)(2,1)} %refs_0_.5, bf16[128,1536]{1,0:T(8,128)(2,1)} %refs_1_.5, bf16[128,1536]{1,0:T(8,128)(2,1)} %refs_2_.5), custom_call_target="tpu_custom_call" | custom-call | bytes 1474560 | tf_op jit(solution)/shard_map/pallas_call | solution.py:28
  10.3 2.2 %collective-permute-start.1 = (bf16[3,64,384]{2,1,0:T(8,128)(2,1)S(1)}, bf16[3,64,384]{2,1,0:T(8,128)(2,1)S(1)}, u32[]{:S(2)}, u32[]{:S(2)}) collective-permute-start(bf16[3,64,384]{2,1,0:T(8,128)(2,1)S(1)} %get-tuple-element.42), channel_id=1, source_target_pairs={{0,2},{1,3},{2,0},{3,1},{4,6},{5,7},{6,4},{7,5},{8,10},{9,11},{10,... | collective-permute-start | bytes 442376 | tf_op jit(solution)/shard_map/ppermute | solution.py:203
  12.5 1.1 %shard_map.60 = bf16[3,64,384]{2,1,0:T(8,128)(2,1)S(1)} custom-call(bf16[128,1536]{1,0:T(8,128)(2,1)} %refs_0_.5, bf16[128,1536]{1,0:T(8,128)(2,1)} %refs_1_.5, bf16[128,1536]{1,0:T(8,128)(2,1)} %refs_2_.5), custom_call_target="tpu_custom_call" | custom-call | bytes 1327104 | tf_op jit(solution)/shard_map/pallas_call | solution.py:28
  13.6 1.1 %collective-permute-done.10.refs_3_ = bf16[3,64,384]{2,1,0:T(8,128)(2,1)S(1)} collective-permute-done((bf16[3,64,384]{2,1,0:T(8,128)(2,1)S(1)}, bf16[3,64,384]{2,1,0:T(8,128)(2,1)S(1)}, u32[]{:S(2)}, u32[]{:S(2)}) %collective-permute-start.10) | collective-permute-done | bytes 147488 | tf_op jit(solution)/shard_map/ppermute | solution.py:203
  14.7 1.0 %collective-permute-start.2 = (bf16[3,64,384]{2,1,0:T(8,128)(2,1)S(1)}, bf16[3,64,384]{2,1,0:T(8,128)(2,1)S(1)}, u32[]{:S(2)}, u32[]{:S(2)}) collective-permute-start(bf16[3,64,384]{2,1,0:T(8,128)(2,1)S(1)} %shard_map.60), channel_id=1, source_target_pairs={{0,3},{1,2},{2,1},{3,0},{4,7},{5,6},{6,5},{7,4},{8,11},{9,10},{10,... | collective-permute-start | bytes 442376 | tf_op jit(solution)/shard_map/ppermute | solution.py:203
  15.9 3.4 %collective-permute-done.9.refs_2_ = bf16[3,64,384]{2,1,0:T(8,128)(2,1)S(1)} collective-permute-done((bf16[3,64,384]{2,1,0:T(8,128)(2,1)S(1)}, bf16[3,64,384]{2,1,0:T(8,128)(2,1)S(1)}, u32[]{:S(2)}, u32[]{:S(2)}) %collective-permute-start.9) | collective-permute-done | bytes 147488 | tf_op jit(solution)/shard_map/ppermute | solution.py:203
  19.3 1.9 %collective-permute-start.11 = (bf16[2,2,64,384]{3,2,1,0:T(8,128)(2,1)S(1)}, bf16[2,2,64,384]{3,2,1,0:T(8,128)(2,1)S(1)}, u32[]{:S(2)}, u32[]{:S(2)}) collective-permute-start(bf16[2,2,64,384]{3,2,1,0:T(8,128)(2,1)S(1)} %pad_maximum_fusion.1), channel_id=1, source_target_pairs={{0,4},{4,8},{8,12},{12,16},{16,20},{20,24},{24,28},{1,5},{5,9},{9,... | collective-permute-start | bytes 589832 | tf_op jit(solution)/shard_map/ppermute | solution.py:461
  21.3 1.0 %collective-permute-done.refs_1_ = bf16[3,64,384]{2,1,0:T(8,128)(2,1)S(1)} collective-permute-done((bf16[3,64,384]{2,1,0:T(8,128)(2,1)S(1)}, bf16[3,64,384]{2,1,0:T(8,128)(2,1)S(1)}, u32[]{:S(2)}, u32[]{:S(2)}) %collective-permute-start) | collective-permute-done | bytes 147488 | tf_op jit(solution)/shard_map/ppermute | solution.py:203
  22.2 6.5 %collective-permute-done.1.refs_2_ = bf16[3,64,384]{2,1,0:T(8,128)(2,1)S(1)} collective-permute-done((bf16[3,64,384]{2,1,0:T(8,128)(2,1)S(1)}, bf16[3,64,384]{2,1,0:T(8,128)(2,1)S(1)}, u32[]{:S(2)}, u32[]{:S(2)}) %collective-permute-start.1) | collective-permute-done | bytes 147488 | tf_op jit(solution)/shard_map/ppermute | solution.py:203
  28.8 2.9 %collective-permute-done.2.refs_3_ = bf16[3,64,384]{2,1,0:T(8,128)(2,1)S(1)} collective-permute-done((bf16[3,64,384]{2,1,0:T(8,128)(2,1)S(1)}, bf16[3,64,384]{2,1,0:T(8,128)(2,1)S(1)}, u32[]{:S(2)}, u32[]{:S(2)}) %collective-permute-start.2) | collective-permute-done | bytes 147488 | tf_op jit(solution)/shard_map/ppermute | solution.py:203
  31.8 1.9 %collective-permute-start.3 = (bf16[2,2,64,384]{3,2,1,0:T(8,128)(2,1)S(1)}, bf16[2,2,64,384]{3,2,1,0:T(8,128)(2,1)S(1)}, u32[]{:S(2)}, u32[]{:S(2)}) collective-permute-start(bf16[2,2,64,384]{3,2,1,0:T(8,128)(2,1)S(1)} %pad_maximum_fusion), channel_id=1, source_target_pairs={{0,4},{4,8},{8,12},{12,16},{16,20},{20,24},{24,28},{1,5},{5,9},{9,... | collective-permute-start | bytes 589832 | tf_op jit(solution)/shard_map/ppermute | solution.py:461
  33.7 1.0 %shard_map.65 = (bf16[512,192]{1,0:T(8,128)(2,1)S(1)}, bf16[512,192]{1,0:T(8,128)(2,1)S(1)}, bf16[512,192]{1,0:T(8,128)(2,1)S(1)}, bf16[512,192]{1,0:T(8,128)(2,1)S(1)}) custom-call(bf16[3,64,384]{2,1,0:T(8,128)(2,1)S(1)} %get-tuple-element.58.refs_0_, bf16[3,64,384]{2,1,0:T(8,128)(2,1)S(1)} %collective-permute-done.8.refs_1_, ...), custom_call_target="tpu_custom_call" | custom-call | flops 201326592 | bytes 1376256 | tf_op jit(solution)/shard_map/pallas_call | solution.py:28
  34.8 1.5 %shard_map.66 = (bf16[256,192]{1,0:T(8,128)(2,1)S(1)}, f32[256,192]{1,0:T(8,128)S(1)}, f32[256,192]{1,0:T(8,128)S(1)}, bf16[2,2,64,384]{3,2,1,0:T(8,128)(2,1)S(1)}) custom-call(bf16[512,192]{1,0:T(8,128)(2,1)S(1)} %get-tuple-element.62.q_ref, bf16[512,192]{1,0:T(8,128)(2,1)S(1)} %get-tuple-element.63.k_ref, bf16[512,192]{1,0:T(8,128)(2,1)S(1)} %get-tuple-element.64.v_ref, ...), custom_call_target="tpu_custom_call" | custom-call | flops 301989888 | bytes 1671168 | tf_op jit(solution)/shard_map/pallas_call | solution.py:28
  36.3 4.5 %collective-permute-start.12 = (bf16[2,2,64,384]{3,2,1,0:T(8,128)(2,1)S(1)}, bf16[2,2,64,384]{3,2,1,0:T(8,128)(2,1)S(1)}, u32[]{:S(2)}, u32[]{:S(2)}) collective-permute-start(bf16[2,2,64,384]{3,2,1,0:T(8,128)(2,1)S(1)} %get-tuple-element.72), channel_id=1, source_target_pairs={{4,0},{8,4},{12,8},{16,12},{20,16},{24,20},{28,24},{5,1},{9,5},{13... | collective-permute-start | bytes 589832 | tf_op jit(solution)/shard_map/ppermute | solution.py:464
  40.8 1.0 %shard_map.61 = (bf16[512,192]{1,0:T(8,128)(2,1)S(1)}, bf16[512,192]{1,0:T(8,128)(2,1)S(1)}, bf16[512,192]{1,0:T(8,128)(2,1)S(1)}, bf16[512,192]{1,0:T(8,128)(2,1)S(1)}) custom-call(bf16[3,64,384]{2,1,0:T(8,128)(2,1)S(1)} %get-tuple-element.40.refs_0_, bf16[3,64,384]{2,1,0:T(8,128)(2,1)S(1)} %collective-permute-done.refs_1_, ...), custom_call_target="tpu_custom_call" | custom-call | flops 201326592 | bytes 1376256 | tf_op jit(solution)/shard_map/pallas_call | solution.py:28
  41.9 1.5 %shard_map.62 = (bf16[256,192]{1,0:T(8,128)(2,1)S(1)}, f32[256,192]{1,0:T(8,128)S(1)}, f32[256,192]{1,0:T(8,128)S(1)}, bf16[2,2,64,384]{3,2,1,0:T(8,128)(2,1)S(1)}) custom-call(bf16[512,192]{1,0:T(8,128)(2,1)S(1)} %get-tuple-element.43.q_ref, bf16[512,192]{1,0:T(8,128)(2,1)S(1)} %get-tuple-element.44.k_ref, bf16[512,192]{1,0:T(8,128)(2,1)S(1)} %get-tuple-element.45.v_ref, ...), custom_call_target="tpu_custom_call" | custom-call | flops 301989888 | bytes 1671168 | tf_op jit(solution)/shard_map/pallas_call | solution.py:28
  43.4 1.9 %collective-permute-start.4 = (bf16[2,2,64,384]{3,2,1,0:T(8,128)(2,1)S(1)}, bf16[2,2,64,384]{3,2,1,0:T(8,128)(2,1)S(1)}, u32[]{:S(2)}, u32[]{:S(2)}) collective-permute-start(bf16[2,2,64,384]{3,2,1,0:T(8,128)(2,1)S(1)} %get-tuple-element.53), channel_id=1, source_target_pairs={{4,0},{8,4},{12,8},{16,12},{20,16},{24,20},{28,24},{5,1},{9,5},{13... | collective-permute-start | bytes 589832 | tf_op jit(solution)/shard_map/ppermute | solution.py:464
  45.3 1.4 %shard_map.67 = (bf16[256,192]{1,0:T(8,128)(2,1)S(1)}, f32[512,192]{1,0:T(8,128)S(1)}, f32[512,192]{1,0:T(8,128)S(1)}) custom-call(bf16[512,192]{1,0:T(8,128)(2,1)S(1)} %get-tuple-element.62.q_ref, bf16[512,192]{1,0:T(8,128)(2,1)S(1)} %get-tuple-element.63.k_ref, bf16[512,192]{1,0:T(8,128)(2,1)S(1)} %get-tuple-element.64.v_ref, ...), custom_call_target="tpu_custom_call" | custom-call | flops 301989888 | bytes 2064384 | tf_op jit(solution)/shard_map/pallas_call | solution.py:28
  47.1 1.4 %shard_map.63 = (bf16[256,192]{1,0:T(8,128)(2,1)S(1)}, f32[512,192]{1,0:T(8,128)S(1)}, f32[512,192]{1,0:T(8,128)S(1)}) custom-call(bf16[512,192]{1,0:T(8,128)(2,1)S(1)} %get-tuple-element.43.q_ref, bf16[512,192]{1,0:T(8,128)(2,1)S(1)} %get-tuple-element.44.k_ref, bf16[512,192]{1,0:T(8,128)(2,1)S(1)} %get-tuple-element.45.v_ref, ...), custom_call_target="tpu_custom_call" | custom-call | flops 301989888 | bytes 2064384 | tf_op jit(solution)/shard_map/pallas_call | solution.py:28
  48.5 3.1 %collective-permute-start.14 = (bf16[3,64,384]{2,1,0:T(8,128)(2,1)S(1)}, bf16[3,64,384]{2,1,0:T(8,128)(2,1)S(1)}, u32[]{:S(2)}, u32[]{:S(2)}) collective-permute-start(bf16[3,64,384]{2,1,0:T(8,128)(2,1)S(1)} %get-tuple-element.75), channel_id=1, source_target_pairs={{0,2},{1,3},{2,0},{3,1},{4,6},{5,7},{6,4},{7,5},{8,10},{9,11},{10,... | collective-permute-start | bytes 442376 | tf_op jit(solution)/shard_map/ppermute | solution.py:203
  52.3 1.1 %collective-permute-start.5 = (bf16[3,64,384]{2,1,0:T(8,128)(2,1)S(1)}, bf16[3,64,384]{2,1,0:T(8,128)(2,1)S(1)}, u32[]{:S(2)}, u32[]{:S(2)}) collective-permute-start(bf16[3,64,384]{2,1,0:T(8,128)(2,1)S(1)} %get-tuple-element.55), channel_id=1, source_target_pairs={{0,1},{1,0},{2,3},{3,2},{4,5},{5,4},{6,7},{7,6},{8,9},{9,8},{10,11... | collective-permute-start | bytes 442376 | tf_op jit(solution)/shard_map/ppermute | solution.py:203
  53.5 1.9 %collective-permute-start.6 = (bf16[3,64,384]{2,1,0:T(8,128)(2,1)S(1)}, bf16[3,64,384]{2,1,0:T(8,128)(2,1)S(1)}, u32[]{:S(2)}, u32[]{:S(2)}) collective-permute-start(bf16[3,64,384]{2,1,0:T(8,128)(2,1)S(1)} %get-tuple-element.56), channel_id=1, source_target_pairs={{0,2},{1,3},{2,0},{3,1},{4,6},{5,7},{6,4},{7,5},{8,10},{9,11},{10,... | collective-permute-start | bytes 442376 | tf_op jit(solution)/shard_map/ppermute | solution.py:203
  55.9 5.8 %collective-permute-done.14.refs_6_ = bf16[3,64,384]{2,1,0:T(8,128)(2,1)S(1)} collective-permute-done((bf16[3,64,384]{2,1,0:T(8,128)(2,1)S(1)}, bf16[3,64,384]{2,1,0:T(8,128)(2,1)S(1)}, u32[]{:S(2)}, u32[]{:S(2)}) %collective-permute-start.14) | collective-permute-done | bytes 147488 | tf_op jit(solution)/shard_map/ppermute | solution.py:203
  61.7 10.9 %collective-permute-done.15.refs_7_ = bf16[3,64,384]{2,1,0:T(8,128)(2,1)S(1)} collective-permute-done((bf16[3,64,384]{2,1,0:T(8,128)(2,1)S(1)}, bf16[3,64,384]{2,1,0:T(8,128)(2,1)S(1)}, u32[]{:S(2)}, u32[]{:S(2)}) %collective-permute-start.15) | collective-permute-done | bytes 147488 | tf_op jit(solution)/shard_map/ppermute | solution.py:203
  72.6 1.8 %collective-permute-done.6.refs_2_ = bf16[3,64,384]{2,1,0:T(8,128)(2,1)S(1)} collective-permute-done((bf16[3,64,384]{2,1,0:T(8,128)(2,1)S(1)}, bf16[3,64,384]{2,1,0:T(8,128)(2,1)S(1)}, u32[]{:S(2)}, u32[]{:S(2)}) %collective-permute-start.6) | collective-permute-done | bytes 147488 | tf_op jit(solution)/shard_map/ppermute | solution.py:203
  74.4 3.7 %collective-permute-done.7.refs_3_ = bf16[3,64,384]{2,1,0:T(8,128)(2,1)S(1)} collective-permute-done((bf16[3,64,384]{2,1,0:T(8,128)(2,1)S(1)}, bf16[3,64,384]{2,1,0:T(8,128)(2,1)S(1)}, u32[]{:S(2)}, u32[]{:S(2)}) %collective-permute-start.7) | collective-permute-done | bytes 147488 | tf_op jit(solution)/shard_map/ppermute | solution.py:203
  78.2 1.4 %shard_map.69 = (bf16[128,1536]{1,0:T(8,128)(2,1)}, bf16[128,1536]{1,0:T(8,128)(2,1)}, bf16[128,1536]{1,0:T(8,128)(2,1)}) custom-call(bf16[3,64,384]{2,1,0:T(8,128)(2,1)S(1)} %get-tuple-element.54.refs_0_, bf16[3,64,384]{2,1,0:T(8,128)(2,1)S(1)} %collective-permute-done.5.refs_1_, bf16[3,64,384]{2,1,0:T(8,128)(2,1)S(1)} %collective-permute-done.6.refs_2_, ...), custom_call_target="tpu_custom_call" | custom-call | bytes 2359296 | tf_op jit(solution)/shard_map/pallas_call | solution.py:28
  (22 shorter events, 2.9 us)
Async XLA Ops:
  0.6 1.0 %copy-start = (bf16[128,1536]{1,0:T(8,128)(2,1)S(1)}, bf16[128,1536]{1,0:T(8,128)(2,1)}, u32[]{:S(2)}) copy-start(bf16[128,1536]{1,0:T(8,128)(2,1)} %refs_0_.5) | copy-start | bytes 1179652
  1.6 1.0 %copy-start.1 = (bf16[128,1536]{1,0:T(8,128)(2,1)S(1)}, bf16[128,1536]{1,0:T(8,128)(2,1)}, u32[]{:S(2)}) copy-start(bf16[128,1536]{1,0:T(8,128)(2,1)} %refs_1_.5) | copy-start | bytes 1179652
  2.6 1.0 %copy-start.2 = (bf16[128,1536]{1,0:T(8,128)(2,1)S(1)}, bf16[128,1536]{1,0:T(8,128)(2,1)}, u32[]{:S(2)}) copy-start(bf16[128,1536]{1,0:T(8,128)(2,1)} %refs_2_.5) | copy-start | bytes 1179652
  3.9 10.8 %collective-permute-start.10 = (bf16[3,64,384]{2,1,0:T(8,128)(2,1)S(1)}, bf16[3,64,384]{2,1,0:T(8,128)(2,1)S(1)}, u32[]{:S(2)}, u32[]{:S(2)}) collective-permute-start(bf16[3,64,384]{2,1,0:T(8,128)(2,1)S(1)} %get-tuple-element.61), channel_id=1, source_target_pairs={{0,3},{1,2},{2,1},{3,0},{4,7},{5,6},{6,5},{7,4},{8,11},{9,10},{10,... | collective-permute-start | bytes 442376 | tf_op jit(solution)/shard_map/ppermute | solution.py:203
  5.5 10.3 %collective-permute-start.8 = (bf16[3,64,384]{2,1,0:T(8,128)(2,1)S(1)}, bf16[3,64,384]{2,1,0:T(8,128)(2,1)S(1)}, u32[]{:S(2)}, u32[]{:S(2)}) collective-permute-start(bf16[3,64,384]{2,1,0:T(8,128)(2,1)S(1)} %get-tuple-element.59), channel_id=1, source_target_pairs={{0,1},{1,0},{2,3},{3,2},{4,5},{5,4},{6,7},{7,6},{8,9},{9,8},{10,11... | collective-permute-start | bytes 442376 | tf_op jit(solution)/shard_map/ppermute | solution.py:203
  8.0 11.2 %collective-permute-start.9 = (bf16[3,64,384]{2,1,0:T(8,128)(2,1)S(1)}, bf16[3,64,384]{2,1,0:T(8,128)(2,1)S(1)}, u32[]{:S(2)}, u32[]{:S(2)}) collective-permute-start(bf16[3,64,384]{2,1,0:T(8,128)(2,1)S(1)} %get-tuple-element.60), channel_id=1, source_target_pairs={{0,2},{1,3},{2,0},{3,1},{4,6},{5,7},{6,4},{7,5},{8,10},{9,11},{10,... | collective-permute-start | bytes 442376 | tf_op jit(solution)/shard_map/ppermute | solution.py:203
  9.4 12.8 %collective-permute-start = (bf16[3,64,384]{2,1,0:T(8,128)(2,1)S(1)}, bf16[3,64,384]{2,1,0:T(8,128)(2,1)S(1)}, u32[]{:S(2)}, u32[]{:S(2)}) collective-permute-start(bf16[3,64,384]{2,1,0:T(8,128)(2,1)S(1)} %get-tuple-element.41), channel_id=1, source_target_pairs={{0,1},{1,0},{2,3},{3,2},{4,5},{5,4},{6,7},{7,6},{8,9},{9,8},{10,11... | collective-permute-start | bytes 442376 | tf_op jit(solution)/shard_map/ppermute | solution.py:203
  10.3 18.5 %collective-permute-start.1 = (bf16[3,64,384]{2,1,0:T(8,128)(2,1)S(1)}, bf16[3,64,384]{2,1,0:T(8,128)(2,1)S(1)}, u32[]{:S(2)}, u32[]{:S(2)}) collective-permute-start(bf16[3,64,384]{2,1,0:T(8,128)(2,1)S(1)} %get-tuple-element.42), channel_id=1, source_target_pairs={{0,2},{1,3},{2,0},{3,1},{4,6},{5,7},{6,4},{7,5},{8,10},{9,11},{10,... | collective-permute-start | bytes 442376 | tf_op jit(solution)/shard_map/ppermute | solution.py:203
  14.7 17.0 %collective-permute-start.2 = (bf16[3,64,384]{2,1,0:T(8,128)(2,1)S(1)}, bf16[3,64,384]{2,1,0:T(8,128)(2,1)S(1)}, u32[]{:S(2)}, u32[]{:S(2)}) collective-permute-start(bf16[3,64,384]{2,1,0:T(8,128)(2,1)S(1)} %shard_map.60), channel_id=1, source_target_pairs={{0,3},{1,2},{2,1},{3,0},{4,7},{5,6},{6,5},{7,4},{8,11},{9,10},{10,... | collective-permute-start | bytes 442376 | tf_op jit(solution)/shard_map/ppermute | solution.py:203
  19.3 15.4 %collective-permute-start.11 = (bf16[2,2,64,384]{3,2,1,0:T(8,128)(2,1)S(1)}, bf16[2,2,64,384]{3,2,1,0:T(8,128)(2,1)S(1)}, u32[]{:S(2)}, u32[]{:S(2)}) collective-permute-start(bf16[2,2,64,384]{3,2,1,0:T(8,128)(2,1)S(1)} %pad_maximum_fusion.1), channel_id=1, source_target_pairs={{0,4},{4,8},{8,12},{12,16},{16,20},{20,24},{24,28},{1,5},{5,9},{9,... | collective-permute-start | bytes 589832 | tf_op jit(solution)/shard_map/ppermute | solution.py:461
  31.8 10.1 %collective-permute-start.3 = (bf16[2,2,64,384]{3,2,1,0:T(8,128)(2,1)S(1)}, bf16[2,2,64,384]{3,2,1,0:T(8,128)(2,1)S(1)}, u32[]{:S(2)}, u32[]{:S(2)}) collective-permute-start(bf16[2,2,64,384]{3,2,1,0:T(8,128)(2,1)S(1)} %pad_maximum_fusion), channel_id=1, source_target_pairs={{0,4},{4,8},{8,12},{12,16},{16,20},{20,24},{24,28},{1,5},{5,9},{9,... | collective-permute-start | bytes 589832 | tf_op jit(solution)/shard_map/ppermute | solution.py:461
  36.3 10.5 %collective-permute-start.12 = (bf16[2,2,64,384]{3,2,1,0:T(8,128)(2,1)S(1)}, bf16[2,2,64,384]{3,2,1,0:T(8,128)(2,1)S(1)}, u32[]{:S(2)}, u32[]{:S(2)}) collective-permute-start(bf16[2,2,64,384]{3,2,1,0:T(8,128)(2,1)S(1)} %get-tuple-element.72), channel_id=1, source_target_pairs={{4,0},{8,4},{12,8},{16,12},{20,16},{24,20},{28,24},{5,1},{9,5},{13... | collective-permute-start | bytes 589832 | tf_op jit(solution)/shard_map/ppermute | solution.py:464
  43.4 8.7 %collective-permute-start.4 = (bf16[2,2,64,384]{3,2,1,0:T(8,128)(2,1)S(1)}, bf16[2,2,64,384]{3,2,1,0:T(8,128)(2,1)S(1)}, u32[]{:S(2)}, u32[]{:S(2)}) collective-permute-start(bf16[2,2,64,384]{3,2,1,0:T(8,128)(2,1)S(1)} %get-tuple-element.53), channel_id=1, source_target_pairs={{4,0},{8,4},{12,8},{16,12},{20,16},{24,20},{28,24},{5,1},{9,5},{13... | collective-permute-start | bytes 589832 | tf_op jit(solution)/shard_map/ppermute | solution.py:464
  47.0 8.4 %collective-permute-start.13 = (bf16[3,64,384]{2,1,0:T(8,128)(2,1)S(1)}, bf16[3,64,384]{2,1,0:T(8,128)(2,1)S(1)}, u32[]{:S(2)}, u32[]{:S(2)}) collective-permute-start(bf16[3,64,384]{2,1,0:T(8,128)(2,1)S(1)} %get-tuple-element.74), channel_id=1, source_target_pairs={{0,1},{1,0},{2,3},{3,2},{4,5},{5,4},{6,7},{7,6},{8,9},{9,8},{10,11... | collective-permute-start | bytes 442376 | tf_op jit(solution)/shard_map/ppermute | solution.py:203
  48.5 13.1 %collective-permute-start.14 = (bf16[3,64,384]{2,1,0:T(8,128)(2,1)S(1)}, bf16[3,64,384]{2,1,0:T(8,128)(2,1)S(1)}, u32[]{:S(2)}, u32[]{:S(2)}) collective-permute-start(bf16[3,64,384]{2,1,0:T(8,128)(2,1)S(1)} %get-tuple-element.75), channel_id=1, source_target_pairs={{0,2},{1,3},{2,0},{3,1},{4,6},{5,7},{6,4},{7,5},{8,10},{9,11},{10,... | collective-permute-start | bytes 442376 | tf_op jit(solution)/shard_map/ppermute | solution.py:203
  51.6 21.0 %collective-permute-start.15 = (bf16[3,64,384]{2,1,0:T(8,128)(2,1)S(1)}, bf16[3,64,384]{2,1,0:T(8,128)(2,1)S(1)}, u32[]{:S(2)}, u32[]{:S(2)}) collective-permute-start(bf16[3,64,384]{2,1,0:T(8,128)(2,1)S(1)} %get-tuple-element.76), channel_id=1, source_target_pairs={{0,3},{1,2},{2,1},{3,0},{4,7},{5,6},{6,5},{7,4},{8,11},{9,10},{10,... | collective-permute-start | bytes 442376 | tf_op jit(solution)/shard_map/ppermute | solution.py:203
  52.3 20.3 %collective-permute-start.5 = (bf16[3,64,384]{2,1,0:T(8,128)(2,1)S(1)}, bf16[3,64,384]{2,1,0:T(8,128)(2,1)S(1)}, u32[]{:S(2)}, u32[]{:S(2)}) collective-permute-start(bf16[3,64,384]{2,1,0:T(8,128)(2,1)S(1)} %get-tuple-element.55), channel_id=1, source_target_pairs={{0,1},{1,0},{2,3},{3,2},{4,5},{5,4},{6,7},{7,6},{8,9},{9,8},{10,11... | collective-permute-start | bytes 442376 | tf_op jit(solution)/shard_map/ppermute | solution.py:203
  53.5 21.0 %collective-permute-start.6 = (bf16[3,64,384]{2,1,0:T(8,128)(2,1)S(1)}, bf16[3,64,384]{2,1,0:T(8,128)(2,1)S(1)}, u32[]{:S(2)}, u32[]{:S(2)}) collective-permute-start(bf16[3,64,384]{2,1,0:T(8,128)(2,1)S(1)} %get-tuple-element.56), channel_id=1, source_target_pairs={{0,2},{1,3},{2,0},{3,1},{4,6},{5,7},{6,4},{7,5},{8,10},{9,11},{10,... | collective-permute-start | bytes 442376 | tf_op jit(solution)/shard_map/ppermute | solution.py:203
  55.4 22.8 %collective-permute-start.7 = (bf16[3,64,384]{2,1,0:T(8,128)(2,1)S(1)}, bf16[3,64,384]{2,1,0:T(8,128)(2,1)S(1)}, u32[]{:S(2)}, u32[]{:S(2)}) collective-permute-start(bf16[3,64,384]{2,1,0:T(8,128)(2,1)S(1)} %get-tuple-element.57), channel_id=1, source_target_pairs={{0,3},{1,2},{2,1},{3,0},{4,7},{5,6},{6,5},{7,4},{8,11},{9,10},{10,... | collective-permute-start | bytes 442376 | tf_op jit(solution)/shard_map/ppermute | solution.py:203

commit v6 on v5

--- a/solution.py
+++ b/solution.py
@@ -56,7 +56,6 @@
         self.seg_rows = rows * devs
         self.near = self.reach * rows
         self.groups = self.seg_rows // self.near
-        self.teacher_rows = self.seg_rows if self.seg_rows <= 512 else rows
         self.scale = self.dim ** (-0.5)
 
 
@@ -125,7 +124,7 @@
         sent = [None] * plan.devs
         far_away = plan.devs - 1
         held = [pltpu.with_memory_space_constraint(a, pltpu.HBM) for a in arrays]
-        for steps in ([far_away], list(range(far_away - 1, 0, -1))):
+        for steps in [[step] for step in range(far_away, 0, -1)]:
             scratch = [
                 pltpu.VMEM((len(steps), 3, plan.rows, plan.local_width), BF16),
                 pltpu.SemaphoreType.DMA((len(steps), 3)),
@@ -321,22 +320,12 @@
             groups = unfolded(ref[at], plan)
             for part, rows in block_parts((me ^ step) * plan.rows, plan):
                 to[rows, :] = groups[part]
-    count = plan.teacher_rows
-    if count == plan.seg_rows:
-        target_ref[...] = teacher_rows(plan, q_ref[...], k_ref[...], v_ref[...])
-        return
-
-    def body(i, _):
-        rows = pl.ds(pl.multiple_of(i * count, count), count)
-        target_ref[rows, :] = teacher_rows(plan, q_ref[rows, :], k_ref[...], v_ref[...])
-        return 0
-
-    lax.fori_loop(0, plan.seg_rows // count, body, 0)
+    target_ref[...] = teacher_rows(plan, q_ref[: plan.near, :], k_ref[...], v_ref[...])
 
 
 def teacher(plan, pieces):
-    outs = [shape((plan.seg_rows, plan.chunk_width))] * 4
-    flops = 4 * plan.heads * plan.seg_rows * plan.seg_rows * plan.dim
+    outs = [shape((plan.seg_rows, plan.chunk_width))] * 3 + [shape((plan.near, plan.chunk_width))]
+    flops = 4 * plan.heads * plan.near * plan.seg_rows * plan.dim
     return call(functools.partial(teacher_kernel, plan), list(pieces), outs, (), flops)
 
 
@@ -349,7 +338,7 @@
                 ext[at, rows, :] = groups[part]
         ext[at, near:, :] = ref[:near, :]
     open_far = lax.axis_index("seg") > 0
-    gq, gk, gv = student_group(plan, q_ref[:near, :], ext[0], ext[1], target_ref[:near, :], open_far)
+    gq, gk, gv = student_group(plan, q_ref[:near, :], ext[0], ext[1], target_ref[...], open_far)
     gq_ref[...] = gq.astype(BF16)
     for at, (grad, ref) in enumerate(((gk, gk_ref), (gv, gv_ref))):
         ref[...] = grad[near:]
@@ -371,13 +360,13 @@
     return call(functools.partial(first_kernel, plan), list(held) + [halo], outs, scratch, flops)
 
 
-def rest_kernel(plan, q_ref, k_ref, v_ref, target_ref, k_start, v_start, gq_ref, gk_ref, gv_ref):
+def rest_kernel(plan, q_ref, k_ref, v_ref, k_start, v_start, gq_ref, gk_ref, gv_ref):
     near = plan.near
 
     def group(start):
         rows, keys = pl.ds(start + near, near), pl.ds(start, 2 * near)
-        args = (q_ref[rows, :], k_ref[keys, :], v_ref[keys, :], target_ref[rows, :])
-        return student_group(plan, *args, None)
+        target = teacher_rows(plan, q_ref[rows, :], k_ref[...], v_ref[...])
+        return student_group(plan, q_ref[rows, :], k_ref[keys, :], v_ref[keys, :], target, None)
 
     if plan.groups == 2:
         gq, gk, gv = group(0)
@@ -409,7 +398,7 @@
         shape((plan.seg_rows, width), F32),
         shape((plan.seg_rows, width), F32),
     ]
-    flops = 24 * plan.heads * count * near * plan.dim
+    flops = plan.heads * count * plan.dim * (24 * near + 4 * plan.seg_rows)
     return call(functools.partial(rest_kernel, plan), list(held) + list(starts), outs, (), flops)
 
 
@@ -462,7 +451,7 @@
         held = teacher(plan, pieces)
         gq_first, gk, gv, far = first_group(plan, held, halo)
         far = lax.ppermute(far, "seg", backward)
-        gq_rest, gk, gv = rest_groups(plan, held, (gk, gv))
+        gq_rest, gk, gv = rest_groups(plan, held[:3], (gk, gv))
         pieces = finish(plan, gq_first, gq_rest, gk, gv, far)
         returned.append(exchange(plan, pieces))
     return tuple(unpack(plan, returned))

time: 80 us -> 79.9 us (level)
  waiting for transfers between devices: 37.4 us -> 36.5 us
    ppermute x12, waiting for transfers between devices: 37.4 us -> 36.5 us  [exchange(): got[step] = lax.ppermute(pieces[step], 'dev', pairs)]
    pallas_call x12 -> x13, Pallas kernels: 12.7 us -> 13.4 us  [call(): pl.pallas_call(kernel, out_shape=tuple(outs), in_specs=[spec] * len(array...]
  transfers between devices with their start and end apart: 16 -> 16, of which waited for: 10 -> 10; matrix products, arithmetic and copies ran while one was open for 0% -> 0% of each run, Pallas kernels for 14% -> 15%
where the time goes in v6:
time: 79.9 us; the launch traced here: 79.5 us
  waiting for transfers between devices  36.5 us (46%)
  starting transfers between devices  25.6 us (32%)
  Pallas kernels  13.4 us (17%)
  local copies, waits for them, and re-layouts  2.98 us (4%)
  between operations  0.82 us (1%)
    ppermute x12, waiting for transfers between devices, exchange(): got[step] = lax.ppermute(pieces[step], 'dev', pairs)  36.5 us
    ppermute x12, starting transfers between devices, exchange(): got[step] = lax.ppermute(pieces[step], 'dev', pairs)  15.3 us
    pallas_call x13, Pallas kernels, call(): pl.pallas_call(kernel, out_shape=tuple(outs), in_specs=[spec] * len(array...  13.4 us
    ppermute x2, starting transfers between devices, local(): far = lax.ppermute(far, 'seg', backward)  6.46 us
    ppermute x2, starting transfers between devices, local(): halo = lax.ppermute(halo, 'seg', onward)  3.84 us
    unnamed x6, local copies, waits for them, and re-layouts  2.98 us
  transfers between devices with their start and end apart: 16, of which 10 were waited for; matrix products, arithmetic and copies ran while one was open for 0% of the time, Pallas kernels for 15%

profile of v6, /device:TPU:12, one launch (start us, length us, event | category | flops | bytes accessed | tf_op | source)
XLA Modules:
  0.0 79.5 jit_solution(10468148687650103691)
XLA Ops:
  0.6 1.0 %copy-done = bf16[128,1536]{1,0:T(8,128)(2,1)S(1)} copy-done((bf16[128,1536]{1,0:T(8,128)(2,1)S(1)}, bf16[128,1536]{1,0:T(8,128)(2,1)}, u32[]{:S(2)}) %copy-start) | copy-done | bytes 393240
  1.6 1.0 %copy-done.1 = bf16[128,1536]{1,0:T(8,128)(2,1)S(1)} copy-done((bf16[128,1536]{1,0:T(8,128)(2,1)S(1)}, bf16[128,1536]{1,0:T(8,128)(2,1)}, u32[]{:S(2)}) %copy-start.1) | copy-done | bytes 393240
  2.6 1.0 %copy-done.2 = bf16[128,1536]{1,0:T(8,128)(2,1)S(1)} copy-done((bf16[128,1536]{1,0:T(8,128)(2,1)S(1)}, bf16[128,1536]{1,0:T(8,128)(2,1)}, u32[]{:S(2)}) %copy-start.2) | copy-done | bytes 393240
  3.9 1.6 %collective-permute-start.10 = (bf16[3,64,384]{2,1,0:T(8,128)(2,1)S(1)}, bf16[3,64,384]{2,1,0:T(8,128)(2,1)S(1)}, u32[]{:S(2)}, u32[]{:S(2)}) collective-permute-start(bf16[3,64,384]{2,1,0:T(8,128)(2,1)S(1)} %get-tuple-element.57), channel_id=1, source_target_pairs={{0,3},{1,2},{2,1},{3,0},{4,7},{5,6},{6,5},{7,4},{8,11},{9,10},{10,... | collective-permute-start | bytes 442376 | tf_op jit(solution)/shard_map/ppermute | solution.py:202
  5.5 2.5 %collective-permute-start.8 = (bf16[3,64,384]{2,1,0:T(8,128)(2,1)S(1)}, bf16[3,64,384]{2,1,0:T(8,128)(2,1)S(1)}, u32[]{:S(2)}, u32[]{:S(2)}) collective-permute-start(bf16[3,64,384]{2,1,0:T(8,128)(2,1)S(1)} %get-tuple-element.55), channel_id=1, source_target_pairs={{0,1},{1,0},{2,3},{3,2},{4,5},{5,4},{6,7},{7,6},{8,9},{9,8},{10,11... | collective-permute-start | bytes 442376 | tf_op jit(solution)/shard_map/ppermute | solution.py:202
  8.0 1.1 %shard_map.59 = bf16[3,64,384]{2,1,0:T(8,128)(2,1)S(1)} custom-call(bf16[128,1536]{1,0:T(8,128)(2,1)} %refs_0_.7, bf16[128,1536]{1,0:T(8,128)(2,1)} %refs_1_.7, bf16[128,1536]{1,0:T(8,128)(2,1)} %refs_2_.7), custom_call_target="tpu_custom_call" | custom-call | bytes 1327104 | tf_op jit(solution)/shard_map/pallas_call | solution.py:28
  9.2 0.8 %collective-permute-start = (bf16[3,64,384]{2,1,0:T(8,128)(2,1)S(1)}, bf16[3,64,384]{2,1,0:T(8,128)(2,1)S(1)}, u32[]{:S(2)}, u32[]{:S(2)}) collective-permute-start(bf16[3,64,384]{2,1,0:T(8,128)(2,1)S(1)} %shard_map.59), channel_id=1, source_target_pairs={{0,1},{1,0},{2,3},{3,2},{4,5},{5,4},{6,7},{7,6},{8,9},{9,8},{10,11... | collective-permute-start | bytes 442376 | tf_op jit(solution)/shard_map/ppermute | solution.py:202
  10.0 1.1 %shard_map.60 = bf16[3,64,384]{2,1,0:T(8,128)(2,1)S(1)} custom-call(bf16[128,1536]{1,0:T(8,128)(2,1)} %refs_0_.7, bf16[128,1536]{1,0:T(8,128)(2,1)} %refs_1_.7, bf16[128,1536]{1,0:T(8,128)(2,1)} %refs_2_.7), custom_call_target="tpu_custom_call" | custom-call | bytes 1327104 | tf_op jit(solution)/shard_map/pallas_call | solution.py:28
  11.2 2.2 %collective-permute-start.1 = (bf16[3,64,384]{2,1,0:T(8,128)(2,1)S(1)}, bf16[3,64,384]{2,1,0:T(8,128)(2,1)S(1)}, u32[]{:S(2)}, u32[]{:S(2)}) collective-permute-start(bf16[3,64,384]{2,1,0:T(8,128)(2,1)S(1)} %shard_map.60), channel_id=1, source_target_pairs={{0,2},{1,3},{2,0},{3,1},{4,6},{5,7},{6,4},{7,5},{8,10},{9,11},{10,... | collective-permute-start | bytes 442376 | tf_op jit(solution)/shard_map/ppermute | solution.py:202
  13.4 1.1 %shard_map.61 = bf16[3,64,384]{2,1,0:T(8,128)(2,1)S(1)} custom-call(bf16[128,1536]{1,0:T(8,128)(2,1)} %refs_0_.7, bf16[128,1536]{1,0:T(8,128)(2,1)} %refs_1_.7, bf16[128,1536]{1,0:T(8,128)(2,1)} %refs_2_.7), custom_call_target="tpu_custom_call" | custom-call | bytes 1327104 | tf_op jit(solution)/shard_map/pallas_call | solution.py:28
  14.7 1.0 %collective-permute-start.2 = (bf16[3,64,384]{2,1,0:T(8,128)(2,1)S(1)}, bf16[3,64,384]{2,1,0:T(8,128)(2,1)S(1)}, u32[]{:S(2)}, u32[]{:S(2)}) collective-permute-start(bf16[3,64,384]{2,1,0:T(8,128)(2,1)S(1)} %shard_map.61), channel_id=1, source_target_pairs={{0,3},{1,2},{2,1},{3,0},{4,7},{5,6},{6,5},{7,4},{8,11},{9,10},{10,... | collective-permute-start | bytes 442376 | tf_op jit(solution)/shard_map/ppermute | solution.py:202
  15.9 3.4 %collective-permute-done.9.refs_2_ = bf16[3,64,384]{2,1,0:T(8,128)(2,1)S(1)} collective-permute-done((bf16[3,64,384]{2,1,0:T(8,128)(2,1)S(1)}, bf16[3,64,384]{2,1,0:T(8,128)(2,1)S(1)}, u32[]{:S(2)}, u32[]{:S(2)}) %collective-permute-start.9) | collective-permute-done | bytes 147488 | tf_op jit(solution)/shard_map/ppermute | solution.py:202
  19.3 1.9 %collective-permute-start.11 = (bf16[2,2,64,384]{3,2,1,0:T(8,128)(2,1)S(1)}, bf16[2,2,64,384]{3,2,1,0:T(8,128)(2,1)S(1)}, u32[]{:S(2)}, u32[]{:S(2)}) collective-permute-start(bf16[2,2,64,384]{3,2,1,0:T(8,128)(2,1)S(1)} %pad_maximum_fusion.1), channel_id=1, source_target_pairs={{0,4},{4,8},{8,12},{12,16},{16,20},{20,24},{24,28},{1,5},{5,9},{9,... | collective-permute-start | bytes 589832 | tf_op jit(solution)/shard_map/ppermute | solution.py:450
  21.3 1.0 %collective-permute-done.refs_1_ = bf16[3,64,384]{2,1,0:T(8,128)(2,1)S(1)} collective-permute-done((bf16[3,64,384]{2,1,0:T(8,128)(2,1)S(1)}, bf16[3,64,384]{2,1,0:T(8,128)(2,1)S(1)}, u32[]{:S(2)}, u32[]{:S(2)}) %collective-permute-start) | collective-permute-done | bytes 147488 | tf_op jit(solution)/shard_map/ppermute | solution.py:202
  22.2 6.5 %collective-permute-done.1.refs_2_ = bf16[3,64,384]{2,1,0:T(8,128)(2,1)S(1)} collective-permute-done((bf16[3,64,384]{2,1,0:T(8,128)(2,1)S(1)}, bf16[3,64,384]{2,1,0:T(8,128)(2,1)S(1)}, u32[]{:S(2)}, u32[]{:S(2)}) %collective-permute-start.1) | collective-permute-done | bytes 147488 | tf_op jit(solution)/shard_map/ppermute | solution.py:202
  28.8 2.9 %collective-permute-done.2.refs_3_ = bf16[3,64,384]{2,1,0:T(8,128)(2,1)S(1)} collective-permute-done((bf16[3,64,384]{2,1,0:T(8,128)(2,1)S(1)}, bf16[3,64,384]{2,1,0:T(8,128)(2,1)S(1)}, u32[]{:S(2)}, u32[]{:S(2)}) %collective-permute-start.2) | collective-permute-done | bytes 147488 | tf_op jit(solution)/shard_map/ppermute | solution.py:202
  31.8 1.9 %collective-permute-start.3 = (bf16[2,2,64,384]{3,2,1,0:T(8,128)(2,1)S(1)}, bf16[2,2,64,384]{3,2,1,0:T(8,128)(2,1)S(1)}, u32[]{:S(2)}, u32[]{:S(2)}) collective-permute-start(bf16[2,2,64,384]{3,2,1,0:T(8,128)(2,1)S(1)} %pad_maximum_fusion), channel_id=1, source_target_pairs={{0,4},{4,8},{8,12},{12,16},{16,20},{20,24},{24,28},{1,5},{5,9},{9,... | collective-permute-start | bytes 589832 | tf_op jit(solution)/shard_map/ppermute | solution.py:450
  34.5 1.5 %shard_map.67 = (bf16[256,192]{1,0:T(8,128)(2,1)S(1)}, f32[256,192]{1,0:T(8,128)S(1)}, f32[256,192]{1,0:T(8,128)S(1)}, bf16[2,2,64,384]{3,2,1,0:T(8,128)(2,1)S(1)}) custom-call(bf16[512,192]{1,0:T(8,128)(2,1)S(1)} %get-tuple-element.58.q_ref, bf16[512,192]{1,0:T(8,128)(2,1)S(1)} %get-tuple-element.59.k_ref, bf16[512,192]{1,0:T(8,128)(2,1)S(1)} %get-tuple-element.60.v_ref, ...), custom_call_target="tpu_custom_call" | custom-call | flops 301989888 | bytes 1572864 | tf_op jit(solution)/shard_map/pallas_call | solution.py:28
  36.0 4.5 %collective-permute-start.12 = (bf16[2,2,64,384]{3,2,1,0:T(8,128)(2,1)S(1)}, bf16[2,2,64,384]{3,2,1,0:T(8,128)(2,1)S(1)}, u32[]{:S(2)}, u32[]{:S(2)}) collective-permute-start(bf16[2,2,64,384]{3,2,1,0:T(8,128)(2,1)S(1)} %get-tuple-element.68), channel_id=1, source_target_pairs={{4,0},{8,4},{12,8},{16,12},{20,16},{24,20},{28,24},{5,1},{9,5},{13... | collective-permute-start | bytes 589832 | tf_op jit(solution)/shard_map/ppermute | solution.py:453
  40.6 0.8 shard_map.62
  41.4 1.5 %shard_map.63 = (bf16[256,192]{1,0:T(8,128)(2,1)S(1)}, f32[256,192]{1,0:T(8,128)S(1)}, f32[256,192]{1,0:T(8,128)S(1)}, bf16[2,2,64,384]{3,2,1,0:T(8,128)(2,1)S(1)}) custom-call(bf16[512,192]{1,0:T(8,128)(2,1)S(1)} %get-tuple-element.39.q_ref, bf16[512,192]{1,0:T(8,128)(2,1)S(1)} %get-tuple-element.40.k_ref, bf16[512,192]{1,0:T(8,128)(2,1)S(1)} %get-tuple-element.41.v_ref, ...), custom_call_target="tpu_custom_call" | custom-call | flops 301989888 | bytes 1572864 | tf_op jit(solution)/shard_map/pallas_call | solution.py:28
  42.9 1.9 %collective-permute-start.4 = (bf16[2,2,64,384]{3,2,1,0:T(8,128)(2,1)S(1)}, bf16[2,2,64,384]{3,2,1,0:T(8,128)(2,1)S(1)}, u32[]{:S(2)}, u32[]{:S(2)}) collective-permute-start(bf16[2,2,64,384]{3,2,1,0:T(8,128)(2,1)S(1)} %get-tuple-element.49), channel_id=1, source_target_pairs={{4,0},{8,4},{12,8},{16,12},{20,16},{24,20},{28,24},{5,1},{9,5},{13... | collective-permute-start | bytes 589832 | tf_op jit(solution)/shard_map/ppermute | solution.py:453
  44.8 1.6 %shard_map.68 = (bf16[256,192]{1,0:T(8,128)(2,1)S(1)}, f32[512,192]{1,0:T(8,128)S(1)}, f32[512,192]{1,0:T(8,128)S(1)}) custom-call(bf16[512,192]{1,0:T(8,128)(2,1)S(1)} %get-tuple-element.58.q_ref, bf16[512,192]{1,0:T(8,128)(2,1)S(1)} %get-tuple-element.59.k_ref, bf16[512,192]{1,0:T(8,128)(2,1)S(1)} %get-tuple-element.60.v_ref, ...), custom_call_target="tpu_custom_call" | custom-call | flops 402653184 | bytes 1867776 | tf_op jit(solution)/shard_map/pallas_call | solution.py:28
  46.8 1.6 %shard_map.64 = (bf16[256,192]{1,0:T(8,128)(2,1)S(1)}, f32[512,192]{1,0:T(8,128)S(1)}, f32[512,192]{1,0:T(8,128)S(1)}) custom-call(bf16[512,192]{1,0:T(8,128)(2,1)S(1)} %get-tuple-element.39.q_ref, bf16[512,192]{1,0:T(8,128)(2,1)S(1)} %get-tuple-element.40.k_ref, bf16[512,192]{1,0:T(8,128)(2,1)S(1)} %get-tuple-element.41.v_ref, ...), custom_call_target="tpu_custom_call" | custom-call | flops 402653184 | bytes 1867776 | tf_op jit(solution)/shard_map/pallas_call | solution.py:28
  48.4 3.1 %collective-permute-start.14 = (bf16[3,64,384]{2,1,0:T(8,128)(2,1)S(1)}, bf16[3,64,384]{2,1,0:T(8,128)(2,1)S(1)}, u32[]{:S(2)}, u32[]{:S(2)}) collective-permute-start(bf16[3,64,384]{2,1,0:T(8,128)(2,1)S(1)} %get-tuple-element.71), channel_id=1, source_target_pairs={{0,2},{1,3},{2,0},{3,1},{4,6},{5,7},{6,4},{7,5},{8,10},{9,11},{10,... | collective-permute-start | bytes 442376 | tf_op jit(solution)/shard_map/ppermute | solution.py:202
  52.2 1.1 %collective-permute-start.5 = (bf16[3,64,384]{2,1,0:T(8,128)(2,1)S(1)}, bf16[3,64,384]{2,1,0:T(8,128)(2,1)S(1)}, u32[]{:S(2)}, u32[]{:S(2)}) collective-permute-start(bf16[3,64,384]{2,1,0:T(8,128)(2,1)S(1)} %get-tuple-element.51), channel_id=1, source_target_pairs={{0,1},{1,0},{2,3},{3,2},{4,5},{5,4},{6,7},{7,6},{8,9},{9,8},{10,11... | collective-permute-start | bytes 442376 | tf_op jit(solution)/shard_map/ppermute | solution.py:202
  53.3 1.9 %collective-permute-start.6 = (bf16[3,64,384]{2,1,0:T(8,128)(2,1)S(1)}, bf16[3,64,384]{2,1,0:T(8,128)(2,1)S(1)}, u32[]{:S(2)}, u32[]{:S(2)}) collective-permute-start(bf16[3,64,384]{2,1,0:T(8,128)(2,1)S(1)} %get-tuple-element.52), channel_id=1, source_target_pairs={{0,2},{1,3},{2,0},{3,1},{4,6},{5,7},{6,4},{7,5},{8,10},{9,11},{10,... | collective-permute-start | bytes 442376 | tf_op jit(solution)/shard_map/ppermute | solution.py:202
  55.8 5.9 %collective-permute-done.14.refs_6_ = bf16[3,64,384]{2,1,0:T(8,128)(2,1)S(1)} collective-permute-done((bf16[3,64,384]{2,1,0:T(8,128)(2,1)S(1)}, bf16[3,64,384]{2,1,0:T(8,128)(2,1)S(1)}, u32[]{:S(2)}, u32[]{:S(2)}) %collective-permute-start.14) | collective-permute-done | bytes 147488 | tf_op jit(solution)/shard_map/ppermute | solution.py:202
  61.6 10.9 %collective-permute-done.15.refs_7_ = bf16[3,64,384]{2,1,0:T(8,128)(2,1)S(1)} collective-permute-done((bf16[3,64,384]{2,1,0:T(8,128)(2,1)S(1)}, bf16[3,64,384]{2,1,0:T(8,128)(2,1)S(1)}, u32[]{:S(2)}, u32[]{:S(2)}) %collective-permute-start.15) | collective-permute-done | bytes 147488 | tf_op jit(solution)/shard_map/ppermute | solution.py:202
  72.5 1.8 %collective-permute-done.6.refs_2_ = bf16[3,64,384]{2,1,0:T(8,128)(2,1)S(1)} collective-permute-done((bf16[3,64,384]{2,1,0:T(8,128)(2,1)S(1)}, bf16[3,64,384]{2,1,0:T(8,128)(2,1)S(1)}, u32[]{:S(2)}, u32[]{:S(2)}) %collective-permute-start.6) | collective-permute-done | bytes 147488 | tf_op jit(solution)/shard_map/ppermute | solution.py:202
  74.3 3.8 %collective-permute-done.7.refs_3_ = bf16[3,64,384]{2,1,0:T(8,128)(2,1)S(1)} collective-permute-done((bf16[3,64,384]{2,1,0:T(8,128)(2,1)S(1)}, bf16[3,64,384]{2,1,0:T(8,128)(2,1)S(1)}, u32[]{:S(2)}, u32[]{:S(2)}) %collective-permute-start.7) | collective-permute-done | bytes 147488 | tf_op jit(solution)/shard_map/ppermute | solution.py:202
  78.0 1.4 %shard_map.70 = (bf16[128,1536]{1,0:T(8,128)(2,1)}, bf16[128,1536]{1,0:T(8,128)(2,1)}, bf16[128,1536]{1,0:T(8,128)(2,1)}) custom-call(bf16[3,64,384]{2,1,0:T(8,128)(2,1)S(1)} %get-tuple-element.50.refs_0_, bf16[3,64,384]{2,1,0:T(8,128)(2,1)S(1)} %collective-permute-done.5.refs_1_, bf16[3,64,384]{2,1,0:T(8,128)(2,1)S(1)} %collective-permute-done.6.refs_2_, ...), custom_call_target="tpu_custom_call" | custom-call | bytes 2359296 | tf_op jit(solution)/shard_map/pallas_call | solution.py:28
  (23 shorter events, 3.0 us)
Async XLA Ops:
  0.6 1.0 %copy-start = (bf16[128,1536]{1,0:T(8,128)(2,1)S(1)}, bf16[128,1536]{1,0:T(8,128)(2,1)}, u32[]{:S(2)}) copy-start(bf16[128,1536]{1,0:T(8,128)(2,1)} %refs_0_.7) | copy-start | bytes 1179652
  1.6 1.0 %copy-start.1 = (bf16[128,1536]{1,0:T(8,128)(2,1)S(1)}, bf16[128,1536]{1,0:T(8,128)(2,1)}, u32[]{:S(2)}) copy-start(bf16[128,1536]{1,0:T(8,128)(2,1)} %refs_1_.7) | copy-start | bytes 1179652
  2.6 1.0 %copy-start.2 = (bf16[128,1536]{1,0:T(8,128)(2,1)S(1)}, bf16[128,1536]{1,0:T(8,128)(2,1)}, u32[]{:S(2)}) copy-start(bf16[128,1536]{1,0:T(8,128)(2,1)} %refs_2_.7) | copy-start | bytes 1179652
  3.9 10.8 %collective-permute-start.10 = (bf16[3,64,384]{2,1,0:T(8,128)(2,1)S(1)}, bf16[3,64,384]{2,1,0:T(8,128)(2,1)S(1)}, u32[]{:S(2)}, u32[]{:S(2)}) collective-permute-start(bf16[3,64,384]{2,1,0:T(8,128)(2,1)S(1)} %get-tuple-element.57), channel_id=1, source_target_pairs={{0,3},{1,2},{2,1},{3,0},{4,7},{5,6},{6,5},{7,4},{8,11},{9,10},{10,... | collective-permute-start | bytes 442376 | tf_op jit(solution)/shard_map/ppermute | solution.py:202
  5.5 10.3 %collective-permute-start.8 = (bf16[3,64,384]{2,1,0:T(8,128)(2,1)S(1)}, bf16[3,64,384]{2,1,0:T(8,128)(2,1)S(1)}, u32[]{:S(2)}, u32[]{:S(2)}) collective-permute-start(bf16[3,64,384]{2,1,0:T(8,128)(2,1)S(1)} %get-tuple-element.55), channel_id=1, source_target_pairs={{0,1},{1,0},{2,3},{3,2},{4,5},{5,4},{6,7},{7,6},{8,9},{9,8},{10,11... | collective-permute-start | bytes 442376 | tf_op jit(solution)/shard_map/ppermute | solution.py:202
  8.0 11.2 %collective-permute-start.9 = (bf16[3,64,384]{2,1,0:T(8,128)(2,1)S(1)}, bf16[3,64,384]{2,1,0:T(8,128)(2,1)S(1)}, u32[]{:S(2)}, u32[]{:S(2)}) collective-permute-start(bf16[3,64,384]{2,1,0:T(8,128)(2,1)S(1)} %get-tuple-element.56), channel_id=1, source_target_pairs={{0,2},{1,3},{2,0},{3,1},{4,6},{5,7},{6,4},{7,5},{8,10},{9,11},{10,... | collective-permute-start | bytes 442376 | tf_op jit(solution)/shard_map/ppermute | solution.py:202
  9.2 13.1 %collective-permute-start = (bf16[3,64,384]{2,1,0:T(8,128)(2,1)S(1)}, bf16[3,64,384]{2,1,0:T(8,128)(2,1)S(1)}, u32[]{:S(2)}, u32[]{:S(2)}) collective-permute-start(bf16[3,64,384]{2,1,0:T(8,128)(2,1)S(1)} %shard_map.59), channel_id=1, source_target_pairs={{0,1},{1,0},{2,3},{3,2},{4,5},{5,4},{6,7},{7,6},{8,9},{9,8},{10,11... | collective-permute-start | bytes 442376 | tf_op jit(solution)/shard_map/ppermute | solution.py:202
  11.2 17.6 %collective-permute-start.1 = (bf16[3,64,384]{2,1,0:T(8,128)(2,1)S(1)}, bf16[3,64,384]{2,1,0:T(8,128)(2,1)S(1)}, u32[]{:S(2)}, u32[]{:S(2)}) collective-permute-start(bf16[3,64,384]{2,1,0:T(8,128)(2,1)S(1)} %shard_map.60), channel_id=1, source_target_pairs={{0,2},{1,3},{2,0},{3,1},{4,6},{5,7},{6,4},{7,5},{8,10},{9,11},{10,... | collective-permute-start | bytes 442376 | tf_op jit(solution)/shard_map/ppermute | solution.py:202
  14.7 17.0 %collective-permute-start.2 = (bf16[3,64,384]{2,1,0:T(8,128)(2,1)S(1)}, bf16[3,64,384]{2,1,0:T(8,128)(2,1)S(1)}, u32[]{:S(2)}, u32[]{:S(2)}) collective-permute-start(bf16[3,64,384]{2,1,0:T(8,128)(2,1)S(1)} %shard_map.61), channel_id=1, source_target_pairs={{0,3},{1,2},{2,1},{3,0},{4,7},{5,6},{6,5},{7,4},{8,11},{9,10},{10,... | collective-permute-start | bytes 442376 | tf_op jit(solution)/shard_map/ppermute | solution.py:202
  19.3 15.2 %collective-permute-start.11 = (bf16[2,2,64,384]{3,2,1,0:T(8,128)(2,1)S(1)}, bf16[2,2,64,384]{3,2,1,0:T(8,128)(2,1)S(1)}, u32[]{:S(2)}, u32[]{:S(2)}) collective-permute-start(bf16[2,2,64,384]{3,2,1,0:T(8,128)(2,1)S(1)} %pad_maximum_fusion.1), channel_id=1, source_target_pairs={{0,4},{4,8},{8,12},{12,16},{16,20},{20,24},{24,28},{1,5},{5,9},{9,... | collective-permute-start | bytes 589832 | tf_op jit(solution)/shard_map/ppermute | solution.py:450
  31.8 9.6 %collective-permute-start.3 = (bf16[2,2,64,384]{3,2,1,0:T(8,128)(2,1)S(1)}, bf16[2,2,64,384]{3,2,1,0:T(8,128)(2,1)S(1)}, u32[]{:S(2)}, u32[]{:S(2)}) collective-permute-start(bf16[2,2,64,384]{3,2,1,0:T(8,128)(2,1)S(1)} %pad_maximum_fusion), channel_id=1, source_target_pairs={{0,4},{4,8},{8,12},{12,16},{16,20},{20,24},{24,28},{1,5},{5,9},{9,... | collective-permute-start | bytes 589832 | tf_op jit(solution)/shard_map/ppermute | solution.py:450
  36.0 10.4 %collective-permute-start.12 = (bf16[2,2,64,384]{3,2,1,0:T(8,128)(2,1)S(1)}, bf16[2,2,64,384]{3,2,1,0:T(8,128)(2,1)S(1)}, u32[]{:S(2)}, u32[]{:S(2)}) collective-permute-start(bf16[2,2,64,384]{3,2,1,0:T(8,128)(2,1)S(1)} %get-tuple-element.68), channel_id=1, source_target_pairs={{4,0},{8,4},{12,8},{16,12},{20,16},{24,20},{28,24},{5,1},{9,5},{13... | collective-permute-start | bytes 589832 | tf_op jit(solution)/shard_map/ppermute | solution.py:453
  42.9 9.1 %collective-permute-start.4 = (bf16[2,2,64,384]{3,2,1,0:T(8,128)(2,1)S(1)}, bf16[2,2,64,384]{3,2,1,0:T(8,128)(2,1)S(1)}, u32[]{:S(2)}, u32[]{:S(2)}) collective-permute-start(bf16[2,2,64,384]{3,2,1,0:T(8,128)(2,1)S(1)} %get-tuple-element.49), channel_id=1, source_target_pairs={{4,0},{8,4},{12,8},{16,12},{20,16},{24,20},{28,24},{5,1},{9,5},{13... | collective-permute-start | bytes 589832 | tf_op jit(solution)/shard_map/ppermute | solution.py:453
  46.7 8.6 %collective-permute-start.13 = (bf16[3,64,384]{2,1,0:T(8,128)(2,1)S(1)}, bf16[3,64,384]{2,1,0:T(8,128)(2,1)S(1)}, u32[]{:S(2)}, u32[]{:S(2)}) collective-permute-start(bf16[3,64,384]{2,1,0:T(8,128)(2,1)S(1)} %get-tuple-element.70), channel_id=1, source_target_pairs={{0,1},{1,0},{2,3},{3,2},{4,5},{5,4},{6,7},{7,6},{8,9},{9,8},{10,11... | collective-permute-start | bytes 442376 | tf_op jit(solution)/shard_map/ppermute | solution.py:202
  48.4 13.2 %collective-permute-start.14 = (bf16[3,64,384]{2,1,0:T(8,128)(2,1)S(1)}, bf16[3,64,384]{2,1,0:T(8,128)(2,1)S(1)}, u32[]{:S(2)}, u32[]{:S(2)}) collective-permute-start(bf16[3,64,384]{2,1,0:T(8,128)(2,1)S(1)} %get-tuple-element.71), channel_id=1, source_target_pairs={{0,2},{1,3},{2,0},{3,1},{4,6},{5,7},{6,4},{7,5},{8,10},{9,11},{10,... | collective-permute-start | bytes 442376 | tf_op jit(solution)/shard_map/ppermute | solution.py:202
  51.5 21.0 %collective-permute-start.15 = (bf16[3,64,384]{2,1,0:T(8,128)(2,1)S(1)}, bf16[3,64,384]{2,1,0:T(8,128)(2,1)S(1)}, u32[]{:S(2)}, u32[]{:S(2)}) collective-permute-start(bf16[3,64,384]{2,1,0:T(8,128)(2,1)S(1)} %get-tuple-element.72), channel_id=1, source_target_pairs={{0,3},{1,2},{2,1},{3,0},{4,7},{5,6},{6,5},{7,4},{8,11},{9,10},{10,... | collective-permute-start | bytes 442376 | tf_op jit(solution)/shard_map/ppermute | solution.py:202
  52.2 20.3 %collective-permute-start.5 = (bf16[3,64,384]{2,1,0:T(8,128)(2,1)S(1)}, bf16[3,64,384]{2,1,0:T(8,128)(2,1)S(1)}, u32[]{:S(2)}, u32[]{:S(2)}) collective-permute-start(bf16[3,64,384]{2,1,0:T(8,128)(2,1)S(1)} %get-tuple-element.51), channel_id=1, source_target_pairs={{0,1},{1,0},{2,3},{3,2},{4,5},{5,4},{6,7},{7,6},{8,9},{9,8},{10,11... | collective-permute-start | bytes 442376 | tf_op jit(solution)/shard_map/ppermute | solution.py:202
  53.3 20.9 %collective-permute-start.6 = (bf16[3,64,384]{2,1,0:T(8,128)(2,1)S(1)}, bf16[3,64,384]{2,1,0:T(8,128)(2,1)S(1)}, u32[]{:S(2)}, u32[]{:S(2)}) collective-permute-start(bf16[3,64,384]{2,1,0:T(8,128)(2,1)S(1)} %get-tuple-element.52), channel_id=1, source_target_pairs={{0,2},{1,3},{2,0},{3,1},{4,6},{5,7},{6,4},{7,5},{8,10},{9,11},{10,... | collective-permute-start | bytes 442376 | tf_op jit(solution)/shard_map/ppermute | solution.py:202
  55.3 22.7 %collective-permute-start.7 = (bf16[3,64,384]{2,1,0:T(8,128)(2,1)S(1)}, bf16[3,64,384]{2,1,0:T(8,128)(2,1)S(1)}, u32[]{:S(2)}, u32[]{:S(2)}) collective-permute-start(bf16[3,64,384]{2,1,0:T(8,128)(2,1)S(1)} %get-tuple-element.53), channel_id=1, source_target_pairs={{0,3},{1,2},{2,1},{3,0},{4,7},{5,6},{6,5},{7,4},{8,11},{9,10},{10,... | collective-permute-start | bytes 442376 | tf_op jit(solution)/shard_map/ppermute | solution.py:202
